TPU v7x, 128 devices: a whole 4x4x4 slice. The times are simulated.
128 devices in a mesh: dev: 128 (over y, x, z, core).
Axes of the slice: x: 4, y: 4, z: 4, core: 2. Of those that a mesh axis runs over, the one named last changes fastest.
Arguments:
- field_in: float32 [32, 8, 512, 128], P(None, None, 'dev'), may hold values from -6 to 6
- source: float32 [32, 8, 512, 128], P(None, None, 'dev'), may hold values from -12 to 12
- cell_factor: float32 [8, 512, 128], P(None, 'dev'), may hold values from 0.5 to 2
- layer_material: int32 [8], replicated, may hold values from 0 to 3
- material_scale: float32 [4], replicated, may hold values from 0.25 to 4
- panel_cell: int32 [131072], P('dev'), may hold values from 0 to 65535
- panel_pos: float32 [3, 131072], replicated, may hold values from 0 to 1
- panel_area: float32 [131072], replicated, may hold values from 0.5 to 2
- flux_in: float32 [32, 131072], P(None, 'dev'), may hold values from -6 to 6
- pair_list: int32 [2048, 2], P('dev'), may hold values from -1 to 63, as said below
Outputs:
- field_out: float32 [32, 8, 512, 128], P(None, None, 'dev')
- flux_out: float32 [32, 131072], P(None, 'dev')
Inputs may be any that keep to these rules, and one draw needn't show every extreme that they name: `pair_list`: each row is a tile pair (i, j) with i >= j, or (-1, -1) for an empty slot. No pair is listed twice. In each device's 16 rows the pairs come first, then the empty slots; at least a quarter of every device's slots are filled, and some device has all 16 filled.
All inputs are finite; a program needn't handle non-finite values.
Results may differ from a plain program's by a relative error of at most 0.0038.
Values may be sent and summed in bfloat16 or wider, within the bound.
A program may use at most 192 MiB of HBM per device.

v0:
```python
import math

import jax
import jax.numpy as jnp
from jax import lax
from jax.sharding import PartitionSpec as P

TILE = 2048


softening = 0.0004
relax_rate = 0.8
update_rate = 0.5
kernel_gain = 0.25


def padded_2(array, sides, width):
    for axis, dim in sides:
        size, length = (lax.axis_size(axis), array.shape[dim])
        up = [(i, (i + 1) % size) for i in range(size - 1)]
        down = [(j, i) for i, j in up]
        last = lax.slice_in_dim(array, length - width, length, axis=dim)
        first = lax.slice_in_dim(array, 0, width, axis=dim)
        before = lax.ppermute(last, axis, up)
        after = lax.ppermute(first, axis, down)
        array = jnp.concatenate([before, array, after], axis=dim)
    return array


def coefficient(cell_factor, layer_material, material_scale):
    matched = (
        layer_material[:, None] == jnp.arange(material_scale.shape[0], dtype=jnp.int32)[None, :]
    )
    layer_scale = jnp.sum(jnp.where(matched, material_scale[None, :], 0.0), axis=1)
    return layer_scale[:, None, None] * cell_factor


def relax_rows(widened, source, conduct):
    centre = widened[:, :, 1:-1, :]
    padded = jnp.pad(centre, ((0, 0), (1, 1), (0, 0), (1, 1)))
    beside = (
        padded[:, 2:, :, 1:-1]
        + padded[:, :-2, :, 1:-1]
        + (widened[:, :, 2:, :] + widened[:, :, :-2, :])
        + (padded[:, 1:-1, :, 2:] + padded[:, 1:-1, :, :-2])
    )
    applied = conduct * (6.0 * centre - beside) + centre
    return centre + relax_rate * (source - applied) / (6.0 * conduct + 1.0)


def kernel_tile(row_pos, row_area, col_pos, col_area):
    delta_x = row_pos[0][:, None] - col_pos[0][None, :]
    delta_y = row_pos[1][:, None] - col_pos[1][None, :]
    delta_z = row_pos[2][:, None] - col_pos[2][None, :]
    distance = delta_x * delta_x + delta_y * delta_y + delta_z * delta_z
    weight = row_area[:, None] * col_area[None, :]
    return (weight * lax.rsqrt(distance + softening) * (kernel_gain / math.sqrt(TILE))).astype(
        jnp.bfloat16
    )


def apply_pairs(pair_rows, flux_half, panel_pos, panel_area, totals):
    load_count = flux_half.shape[0]

    def visit(totals, pair_row):
        upper = pair_row[0]
        lower = pair_row[1]

        def work(totals):
            anchor = jnp.int32(0)
            row_start = upper * TILE
            col_start = lower * TILE
            tile_block = kernel_tile(
                lax.dynamic_slice(panel_pos, (anchor, row_start), (3, TILE)),
                lax.dynamic_slice(panel_area, (row_start,), (TILE,)),
                lax.dynamic_slice(panel_pos, (anchor, col_start), (3, TILE)),
                lax.dynamic_slice(panel_area, (col_start,), (TILE,)),
            )
            row_flux = lax.dynamic_slice(flux_half, (anchor, row_start), (load_count, TILE))
            col_flux = lax.dynamic_slice(flux_half, (anchor, col_start), (load_count, TILE))
            onward = jnp.dot(row_flux, tile_block, preferred_element_type=jnp.float32)
            current = lax.dynamic_slice(totals, (anchor, col_start), (load_count, TILE))
            totals = lax.dynamic_update_slice(totals, current + onward, (anchor, col_start))

            def transposed(totals):
                backward = lax.dot_general(
                    col_flux,
                    tile_block,
                    (((1,), (1,)), ((), ())),
                    preferred_element_type=jnp.float32,
                )
                present = lax.dynamic_slice(totals, (anchor, row_start), (load_count, TILE))
                return lax.dynamic_update_slice(totals, present + backward, (anchor, row_start))

            return lax.cond(upper != lower, transposed, lambda kept: kept, totals)

        return (lax.cond(upper >= 0, work, lambda kept: kept, totals), None)

    totals, unused = lax.scan(visit, totals, pair_rows)
    return totals


def body(
    field_in,
    source,
    cell_factor,
    layer_material,
    material_scale,
    panel_cell,
    panel_pos,
    panel_area,
    flux_in,
    pair_list,
):
    conduct = coefficient(cell_factor, layer_material, material_scale)
    load_count = field_in.shape[0]
    field_now = field_in
    for repeat in range(2):
        widened = padded_2(field_now, (("dev", 2),), 1)
        field_now = relax_rows(widened, source, conduct)
    surface_top = field_now[:, -1].astype(jnp.bfloat16)
    gathered = lax.all_gather(surface_top, "dev", axis=1, tiled=True)
    flattened = gathered.reshape(gathered.shape[0], -1)
    traces = jnp.take(flattened, panel_cell, axis=1)
    flux_half = lax.all_gather(flux_in.astype(jnp.bfloat16), "dev", axis=1, tiled=True)
    totals = jnp.zeros((load_count, flux_half.shape[1]), jnp.float32)
    totals = apply_pairs(pair_list, flux_half, panel_pos, panel_area, totals)
    potential = lax.psum_scatter(totals, "dev", scatter_dimension=1, tiled=True)
    flux_out = flux_in + update_rate * (traces.astype(jnp.float32) - potential)
    return (field_now, flux_out)


def solution(mesh):
    in_specs = (
        P(None, None, "dev", None),
        P(None, None, "dev", None),
        P(None, "dev", None),
        P(),
        P(),
        P("dev"),
        P(),
        P(),
        P(None, "dev"),
        P("dev", None),
    )
    out_specs = (P(None, None, "dev", None), P(None, "dev"))
    return jax.shard_map(body, mesh=mesh, in_specs=in_specs, out_specs=out_specs, check_vma=False)
```

profile of v0, /device:TPU:1, one launch (start us, length us, event | category | flops | bytes accessed | tf_op | source)
XLA Modules:
  0.0 1385.9 jit_solution(1619266360225122936)
XLA Ops:
  32.0 53.7 %all-gather.4.cloned.1.call-done = bf16[32,131072]{1,0:T(8,128)(2,1)} async-done(((bf16[32,1024]{1,0:T(8,128)(2,1)}), bf16[32,131072]{1,0:T(8,128)(2,1)}) %all-gather.4.cloned.1.call-update) | async-done | bytes 8388624 | tf_op jit(solution)/shard_map/all_gather | solution.py:125
  85.7 6.9 broadcast_in_dim.42
  92.6 375.2 %while.13 = (s32[]{:T(128)}, f32[32,131072]{1,0:T(8,128)}, s32[16,2]{1,0:T(8,128)S(1)}, bf16[32,131072]{1,0:T(8,128)(2,1)}, f32[131072]{0:T(1024)}, /*index=5*/f32[3,131072]{1,0:T(4,128)}, s32[]{:T(128)}, s32[]{:T(128)}) while((s32[]{:T(128)}, f32[32,131072]{1,0:T(8,128)}, s32[16,2]{1,0:T(8,128)S(1)}, bf16[32,131072]{1,0:T(8,128)(2,1)}, ...), condition=%wide.region_6.7_spmd, body=%wide.region_1.6_spmd.sunk | while | flops 646053888 | bytes 18875816 | solution.py:99
  92.6 31.9 %conditional.3 = (f32[32,131072]{1,0:T(8,128)}) conditional(s32[]{:T(128)} %convert_element_type.30, f32[32,131072]{1,0:T(8,128)} %get-tuple-element.186, (s32[1,2]{1,0:T(1,128)S(1)}, s32[]{:T(128)S(1)}, f32[32,131072]{1,0:T(8,128)}, bf16[32,131072]{1,0:T(8,128)(2,1)}, f32[131072]{0:T(1024)}, /*index=5*/f32[3,131072]{1,0:T(4,128)}) %tuple.66), branch_computations={%region_2.2_spmd, %region_3.5_spmd} | conditional | flops 646053888 | bytes 18875648 | solution.py:97
  95.6 9.5 fusion.2
  105.1 10.8 multiply_convert_fusion
  116.5 7.9 conditional
  116.6 6.1 convolution_add_fusion
  124.5 32.0 %conditional.3 = (f32[32,131072]{1,0:T(8,128)}) conditional(s32[]{:T(128)} %convert_element_type.30, f32[32,131072]{1,0:T(8,128)} %get-tuple-element.186, (s32[1,2]{1,0:T(1,128)S(1)}, s32[]{:T(128)S(1)}, f32[32,131072]{1,0:T(8,128)}, bf16[32,131072]{1,0:T(8,128)(2,1)}, f32[131072]{0:T(1024)}, /*index=5*/f32[3,131072]{1,0:T(4,128)}) %tuple.66), branch_computations={%region_2.2_spmd, %region_3.5_spmd} | conditional | flops 646053888 | bytes 18875648 | solution.py:97
  127.5 9.5 fusion.2
  137.0 10.8 multiply_convert_fusion
  148.5 8.0 conditional
  148.5 6.2 convolution_add_fusion
  156.5 31.8 %conditional.3 = (f32[32,131072]{1,0:T(8,128)}) conditional(s32[]{:T(128)} %convert_element_type.30, f32[32,131072]{1,0:T(8,128)} %get-tuple-element.186, (s32[1,2]{1,0:T(1,128)S(1)}, s32[]{:T(128)S(1)}, f32[32,131072]{1,0:T(8,128)}, bf16[32,131072]{1,0:T(8,128)(2,1)}, f32[131072]{0:T(1024)}, /*index=5*/f32[3,131072]{1,0:T(4,128)}) %tuple.66), branch_computations={%region_2.2_spmd, %region_3.5_spmd} | conditional | flops 646053888 | bytes 18875648 | solution.py:97
  159.6 9.5 fusion.2
  169.0 10.8 multiply_convert_fusion
  180.5 7.9 conditional
  180.5 6.0 convolution_add_fusion
  188.4 31.8 %conditional.3 = (f32[32,131072]{1,0:T(8,128)}) conditional(s32[]{:T(128)} %convert_element_type.30, f32[32,131072]{1,0:T(8,128)} %get-tuple-element.186, (s32[1,2]{1,0:T(1,128)S(1)}, s32[]{:T(128)S(1)}, f32[32,131072]{1,0:T(8,128)}, bf16[32,131072]{1,0:T(8,128)(2,1)}, f32[131072]{0:T(1024)}, /*index=5*/f32[3,131072]{1,0:T(4,128)}) %tuple.66), branch_computations={%region_2.2_spmd, %region_3.5_spmd} | conditional | flops 646053888 | bytes 18875648 | solution.py:97
  191.4 9.5 fusion.2
  200.9 10.8 multiply_convert_fusion
  212.3 7.9 conditional
  212.3 6.0 convolution_add_fusion
  220.2 31.8 %conditional.3 = (f32[32,131072]{1,0:T(8,128)}) conditional(s32[]{:T(128)} %convert_element_type.30, f32[32,131072]{1,0:T(8,128)} %get-tuple-element.186, (s32[1,2]{1,0:T(1,128)S(1)}, s32[]{:T(128)S(1)}, f32[32,131072]{1,0:T(8,128)}, bf16[32,131072]{1,0:T(8,128)(2,1)}, f32[131072]{0:T(1024)}, /*index=5*/f32[3,131072]{1,0:T(4,128)}) %tuple.66), branch_computations={%region_2.2_spmd, %region_3.5_spmd} | conditional | flops 646053888 | bytes 18875648 | solution.py:97
  223.3 9.4 fusion.2
  232.7 10.8 multiply_convert_fusion
  244.2 7.9 conditional
  244.2 6.0 convolution_add_fusion
  252.1 31.8 %conditional.3 = (f32[32,131072]{1,0:T(8,128)}) conditional(s32[]{:T(128)} %convert_element_type.30, f32[32,131072]{1,0:T(8,128)} %get-tuple-element.186, (s32[1,2]{1,0:T(1,128)S(1)}, s32[]{:T(128)S(1)}, f32[32,131072]{1,0:T(8,128)}, bf16[32,131072]{1,0:T(8,128)(2,1)}, f32[131072]{0:T(1024)}, /*index=5*/f32[3,131072]{1,0:T(4,128)}) %tuple.66), branch_computations={%region_2.2_spmd, %region_3.5_spmd} | conditional | flops 646053888 | bytes 18875648 | solution.py:97
  255.1 9.5 fusion.2
  264.6 10.8 multiply_convert_fusion
  276.0 7.9 conditional
  276.1 6.0 convolution_add_fusion
  284.0 31.8 %conditional.3 = (f32[32,131072]{1,0:T(8,128)}) conditional(s32[]{:T(128)} %convert_element_type.30, f32[32,131072]{1,0:T(8,128)} %get-tuple-element.186, (s32[1,2]{1,0:T(1,128)S(1)}, s32[]{:T(128)S(1)}, f32[32,131072]{1,0:T(8,128)}, bf16[32,131072]{1,0:T(8,128)(2,1)}, f32[131072]{0:T(1024)}, /*index=5*/f32[3,131072]{1,0:T(4,128)}) %tuple.66), branch_computations={%region_2.2_spmd, %region_3.5_spmd} | conditional | flops 646053888 | bytes 18875648 | solution.py:97
  287.0 9.5 fusion.2
  296.5 10.8 multiply_convert_fusion
  307.9 7.9 conditional
  315.8 31.8 %conditional.3 = (f32[32,131072]{1,0:T(8,128)}) conditional(s32[]{:T(128)} %convert_element_type.30, f32[32,131072]{1,0:T(8,128)} %get-tuple-element.186, (s32[1,2]{1,0:T(1,128)S(1)}, s32[]{:T(128)S(1)}, f32[32,131072]{1,0:T(8,128)}, bf16[32,131072]{1,0:T(8,128)(2,1)}, f32[131072]{0:T(1024)}, /*index=5*/f32[3,131072]{1,0:T(4,128)}) %tuple.66), branch_computations={%region_2.2_spmd, %region_3.5_spmd} | conditional | flops 646053888 | bytes 18875648 | solution.py:97
  318.9 9.5 fusion.2
  328.3 10.8 multiply_convert_fusion
  339.8 7.9 conditional
  339.8 6.0 convolution_add_fusion
  347.7 24.1 %conditional.3 = (f32[32,131072]{1,0:T(8,128)}) conditional(s32[]{:T(128)} %convert_element_type.30, f32[32,131072]{1,0:T(8,128)} %get-tuple-element.186, (s32[1,2]{1,0:T(1,128)S(1)}, s32[]{:T(128)S(1)}, f32[32,131072]{1,0:T(8,128)}, bf16[32,131072]{1,0:T(8,128)(2,1)}, f32[131072]{0:T(1024)}, /*index=5*/f32[3,131072]{1,0:T(4,128)}) %tuple.66), branch_computations={%region_2.2_spmd, %region_3.5_spmd} | conditional | flops 646053888 | bytes 18875648 | solution.py:97
  350.9 9.4 fusion.2
  360.3 10.8 multiply_convert_fusion
  371.9 31.8 %conditional.3 = (f32[32,131072]{1,0:T(8,128)}) conditional(s32[]{:T(128)} %convert_element_type.30, f32[32,131072]{1,0:T(8,128)} %get-tuple-element.186, (s32[1,2]{1,0:T(1,128)S(1)}, s32[]{:T(128)S(1)}, f32[32,131072]{1,0:T(8,128)}, bf16[32,131072]{1,0:T(8,128)(2,1)}, f32[131072]{0:T(1024)}, /*index=5*/f32[3,131072]{1,0:T(4,128)}) %tuple.66), branch_computations={%region_2.2_spmd, %region_3.5_spmd} | conditional | flops 646053888 | bytes 18875648 | solution.py:97
  374.9 9.5 fusion.2
  384.4 10.8 multiply_convert_fusion
  395.8 7.9 conditional
  395.8 6.0 convolution_add_fusion
  403.8 31.8 %conditional.3 = (f32[32,131072]{1,0:T(8,128)}) conditional(s32[]{:T(128)} %convert_element_type.30, f32[32,131072]{1,0:T(8,128)} %get-tuple-element.186, (s32[1,2]{1,0:T(1,128)S(1)}, s32[]{:T(128)S(1)}, f32[32,131072]{1,0:T(8,128)}, bf16[32,131072]{1,0:T(8,128)(2,1)}, f32[131072]{0:T(1024)}, /*index=5*/f32[3,131072]{1,0:T(4,128)}) %tuple.66), branch_computations={%region_2.2_spmd, %region_3.5_spmd} | conditional | flops 646053888 | bytes 18875648 | solution.py:97
  406.8 9.5 fusion.2
  416.2 10.8 multiply_convert_fusion
  427.7 7.9 conditional
  427.7 6.0 convolution_add_fusion
  435.6 31.8 %conditional.3 = (f32[32,131072]{1,0:T(8,128)}) conditional(s32[]{:T(128)} %convert_element_type.30, f32[32,131072]{1,0:T(8,128)} %get-tuple-element.186, (s32[1,2]{1,0:T(1,128)S(1)}, s32[]{:T(128)S(1)}, f32[32,131072]{1,0:T(8,128)}, bf16[32,131072]{1,0:T(8,128)(2,1)}, f32[131072]{0:T(1024)}, /*index=5*/f32[3,131072]{1,0:T(4,128)}) %tuple.66), branch_computations={%region_2.2_spmd, %region_3.5_spmd} | conditional | flops 646053888 | bytes 18875648 | solution.py:97
  438.6 9.5 fusion.2
  448.1 10.8 multiply_convert_fusion
  459.5 7.9 conditional
  459.6 6.0 convolution_add_fusion
  467.8 35.4 %copy.49 = f32[32,131072]{0,1:T(8,128)} copy(f32[32,131072]{1,0:T(8,128)} %get-tuple-element.89) | data formatting | bytes 33554432 | tf_op jit(solution)/shard_map/while | solution.py:99
  505.4 13.6 copy.47
  519.0 10.8 gather_fusion
  529.8 847.5 %reduce-scatter.2.cloned.1.call-done = f32[32,1024]{0,1:T(8,128)} async-done(((f32[32,131072]{0,1:T(8,128)}), f32[32,1024]{0,1:T(8,128)}) %reduce-scatter.2.cloned.1.call-update) | async-done | bytes 131088 | tf_op jit(solution)/shard_map/reduce_scatter | solution.py:128
  (106 shorter events, 83.3 us)
Async XLA Ops:
  7.2 78.5 %all-gather.4.cloned.1.call-start = ((), (), s32[]{:S(2)}) async-start(), calls=%async_computation.1 | async-start | bytes 8454144 | tf_op jit(solution)/shard_map/all_gather | solution.py:125
  8.8 496.6 %all-gather.6.cloned.1.call-start = ((), (), s32[]{:S(2)}) async-start(), calls=%async_computation.3 | async-start | bytes 4227072 | tf_op jit(solution)/shard_map/all_gather | solution.py:122
  10.2 8.4 collective-permute-start
  13.5 5.5 collective-permute-start.1
  20.7 7.0 collective-permute-start.2
  22.6 6.3 collective-permute-start.3
  31.2 1346.2 %reduce-scatter.2.cloned.1.call-start = ((), (), s32[]{:S(2)}) async-start(), calls=%async_computation.2 | async-start | bytes 67633152 | tf_op jit(solution)/shard_map/reduce_scatter | solution.py:128
  503.1 0.9 copy-start
  503.2 1.1 copy-start.1
Sparse Core Ops, SparseCore 0:
  11.6 74.0 all-gather.3
  88.8 65.1 all-gather.5
  503.3 873.9 reduce-scatter.1
where the time goes:
time: 1390 us
  waiting for transfers between devices  904 us (65%)
  matrix products  180 us (13%)
  other arithmetic  137 us (10%)
  local copies, waits for them, and re-layouts  121 us (9%)
  loops' own time  17.3 us (1%)
  between operations  13.9 us (1%)
    reduce_scatter x1, waiting for transfers between devices, body(): potential = lax.psum_scatter(totals, 'dev', scatter_dimension=1, tiled=True)  848 us
    convert_element_type x12, other arithmetic, kernel_tile(): (weight * lax.rsqrt(distance + softening) * (kernel_gain / math.sqrt(TILE...  130 us
    dot_general x12, matrix products, work(): onward = jnp.dot(row_flux, tile_block, preferred_element_type=jnp.float32)  113 us
    dot_general x11, matrix products, transposed(): lax.dot_general(col_flux, tile_block, (((1,), (1,)), ((), ())), preferred...  66.7 us
    all_gather x1, waiting for transfers between devices, body(): lax.all_gather(flux_in.astype(jnp.bfloat16), 'dev', axis=1, tiled=True)  53.7 us
    while x2, local copies, waits for them, and re-layouts, apply_pairs(): totals, unused = lax.scan(visit, totals, pair_rows)  36.1 us
  transfers between devices with their start and end apart: 7, of which 5 were waited for; matrix products, arithmetic and copies ran while one was open for 31% of the time, Pallas kernels for 0%

commit v1 on v0

v1 whole, which is shorter than its diff:
```python
import functools
import math

import jax
import jax.numpy as jnp
from jax import lax
from jax.experimental import pallas as pl
from jax.experimental.pallas import tpu as pltpu
from jax.sharding import PartitionSpec as P

TILE = 2048
TILES = 64
LINE = 8
PLANE = 16
COLS = 4 * TILE

softening = 0.0004
relax_rate = 0.8
update_rate = 0.5
kernel_gain = 0.25


def padded_2(array, sides, width):
    for axis, dim in sides:
        size, length = (lax.axis_size(axis), array.shape[dim])
        up = [(i, (i + 1) % size) for i in range(size - 1)]
        down = [(j, i) for i, j in up]
        last = lax.slice_in_dim(array, length - width, length, axis=dim)
        first = lax.slice_in_dim(array, 0, width, axis=dim)
        before = lax.ppermute(last, axis, up)
        after = lax.ppermute(first, axis, down)
        array = jnp.concatenate([before, array, after], axis=dim)
    return array


def coefficient(cell_factor, layer_material, material_scale):
    matched = (
        layer_material[:, None] == jnp.arange(material_scale.shape[0], dtype=jnp.int32)[None, :]
    )
    layer_scale = jnp.sum(jnp.where(matched, material_scale[None, :], 0.0), axis=1)
    return layer_scale[:, None, None] * cell_factor


def relax_rows(widened, source, conduct):
    centre = widened[:, :, 1:-1, :]
    padded = jnp.pad(centre, ((0, 0), (1, 1), (0, 0), (1, 1)))
    beside = (
        padded[:, 2:, :, 1:-1]
        + padded[:, :-2, :, 1:-1]
        + (widened[:, :, 2:, :] + widened[:, :, :-2, :])
        + (padded[:, 1:-1, :, 2:] + padded[:, 1:-1, :, :-2])
    )
    applied = conduct * (6.0 * centre - beside) + centre
    return centre + relax_rate * (source - applied) / (6.0 * conduct + 1.0)


def split3(value):
    high = lax.reduce_precision(value, 8, 7)
    rest = value - high
    middle = lax.reduce_precision(rest, 8, 7)
    low = lax.reduce_precision(rest - middle, 8, 7)
    return high, middle, low


def features(pos, area, row_side):
    pos = pos - 0.5
    scale = math.sqrt(TILE) / kernel_gain / (area * area)
    norm = jnp.sum(pos * pos, axis=0)
    if row_side:
        parts = jnp.stack(
            [scale * (norm + softening), scale] + [-2.0 * scale * pos[a] for a in range(3)]
        )
    else:
        parts = jnp.stack([scale, scale * norm] + [scale * pos[a] for a in range(3)])
    high, middle, low = split3(parts)
    if row_side:
        stack = [high, high, middle, middle, high, low]
    else:
        stack = [high, middle, high, middle, low, high]
    stack.append(jnp.zeros((2,) + parts.shape[1:], jnp.float32))
    return jnp.concatenate(stack, axis=0).astype(jnp.bfloat16)


def pair_kernel(mask_ref, f_ref, pt_ref, q_ref, o_ref, order_ref):
    for j in range(4):

        def note(i, count):
            order_ref[count] = i
            return count + mask_ref[j * TILES + i]

        count = lax.fori_loop(0, TILES, note, jnp.int32(0))
        order_ref[count] = TILES
        o_ref[:, j * TILE : (j + 1) * TILE] = jnp.zeros((32, TILE), jnp.float32)

        def step(b, carry):
            first = order_ref[2 * b]
            second = order_ref[2 * b + 1]
            flux = jnp.concatenate([f_ref[first], f_ref[second]], axis=1)
            for c in range(2):
                columns = pl.ds(j * TILE + c * 1024, 1024)
                block = []
                for which in (first, second):
                    distance = jnp.dot(
                        pt_ref[which], q_ref[:, columns], preferred_element_type=jnp.float32
                    )
                    block.append(lax.rsqrt(distance).astype(jnp.bfloat16))
                o_ref[:, columns] += jnp.dot(
                    flux, jnp.concatenate(block, axis=0), preferred_element_type=jnp.float32
                )
            return carry

        lax.fori_loop(0, (count + 1) // 2, step, 0)


def apply_pairs(mask, flux_rows, row_features, col_features):
    vmem = pl.BlockSpec(memory_space=pltpu.VMEM)
    return pl.pallas_call(
        pair_kernel,
        out_shape=jax.ShapeDtypeStruct((32, COLS), jnp.float32),
        in_specs=[pl.BlockSpec(memory_space=pltpu.SMEM), vmem, vmem, vmem],
        out_specs=vmem,
        scratch_shapes=[pltpu.SMEM((TILES + 2,), jnp.int32)],
        compiler_params=pltpu.CompilerParams(vmem_limit_bytes=40 << 20),
        cost_estimate=pl.CostEstimate(
            flops=100_000_000_000, bytes_accessed=8 << 20, transcendentals=0
        ),
    )(mask, flux_rows, row_features, col_features)


def body(
    field_in,
    source,
    cell_factor,
    layer_material,
    material_scale,
    panel_cell,
    panel_pos,
    panel_area,
    flux_in,
    pair_list,
):
    lines = [[LINE * m + r for r in range(LINE)] for m in range(PLANE)]
    planes = [[LINE * m + r for m in range(PLANE)] for r in range(LINE)]
    me = lax.axis_index("dev")
    m, r = me // LINE, me % LINE

    pairs = lax.all_gather(pair_list, "dev", axis=0, tiled=True)
    tile_ids = jnp.arange(TILES, dtype=jnp.int32)
    upper = (pairs[:, 0:1] == tile_ids[None, :]).astype(jnp.bfloat16)
    lower = (pairs[:, 1:2] == tile_ids[None, :]).astype(jnp.bfloat16)
    listed = lax.dot_general(
        upper, lower, (((0,), (0,)), ((), ())), preferred_element_type=jnp.float32
    )
    listed = (listed + listed.T > 0.0).astype(jnp.int32)
    mask = lax.dynamic_slice(listed, (4 * m, 0), (4, TILES)).reshape(-1)

    flux_half = flux_in.astype(jnp.bfloat16).reshape(32, LINE, 128).transpose(1, 0, 2)
    shared = lax.all_to_all(flux_half, "dev", 0, 0, axis_index_groups=lines)
    rows = lax.all_gather(shared, "dev", axis=0, tiled=True, axis_index_groups=planes)
    rows = rows.reshape(TILES, 2, 32, 128).transpose(0, 2, 1, 3).reshape(TILES, 32, 256)
    rows = jnp.concatenate([rows, jnp.zeros((1, 32, 256), jnp.bfloat16)], axis=0)

    row_pos = lax.dynamic_index_in_dim(panel_pos.reshape(3, 128, LINE, 128), r, 2, False)
    row_area = lax.dynamic_index_in_dim(panel_area.reshape(128, LINE, 128), r, 1, False)
    row_features = features(row_pos.reshape(3, -1), row_area.reshape(-1), True)
    row_features = row_features.reshape(32, TILES, 256).transpose(1, 2, 0)
    row_features = jnp.concatenate([row_features, row_features[:1]], axis=0)
    col_features = features(
        lax.dynamic_slice(panel_pos, (0, m * COLS), (3, COLS)),
        lax.dynamic_slice(panel_area, (m * COLS,), (COLS,)),
        False,
    )

    conduct = coefficient(cell_factor, layer_material, material_scale)
    field_now = field_in
    for repeat in range(2):
        widened = padded_2(field_now, (("dev", 2),), 1)
        field_now = relax_rows(widened, source, conduct)
    surface_top = field_now[:, -1].astype(jnp.bfloat16)
    gathered = lax.all_gather(surface_top, "dev", axis=1, tiled=True)
    flattened = gathered.reshape(gathered.shape[0], -1)

    partial = apply_pairs(mask, rows, row_features, col_features)
    potential = lax.psum_scatter(
        partial, "dev", scatter_dimension=1, axis_index_groups=lines, tiled=True
    )
    traces = jnp.take(flattened, panel_cell, axis=1)
    flux_out = flux_in + update_rate * (traces.astype(jnp.float32) - potential)
    return (field_now, flux_out)


def solution(mesh):
    in_specs = (
        P(None, None, "dev", None),
        P(None, None, "dev", None),
        P(None, "dev", None),
        P(),
        P(),
        P("dev"),
        P(),
        P(),
        P(None, "dev"),
        P("dev", None),
    )
    out_specs = (P(None, None, "dev", None), P(None, "dev"))
    return jax.shard_map(body, mesh=mesh, in_specs=in_specs, out_specs=out_specs, check_vma=False)
```

time: 1390 us -> 243 us (0.17)
  waiting for transfers between devices: 904 us -> 34.4 us
  matrix products: 180 us -> 1.01 us
  other arithmetic: 137 us -> 13.8 us
  local copies, waits for them, and re-layouts: 121 us -> 41.2 us
  Pallas kernels: 0 us -> 78.5 us
  blocking collectives: 0 us -> 38.4 us
  loops' own time: 17.3 us -> 0 us
    reduce_scatter x1, waiting for transfers between devices: 848 us -> 11.6 us  [body(): lax.psum_scatter(partial, 'dev', scatter_dimension=1, axis_index_groups=l...]
    dot_general x23 -> x1, matrix products: 180 us -> 1.01 us  [body(): lax.dot_general(upper, lower, (((0,), (0,)), ((), ())), preferred_element...]
    convert_element_type x13 -> x1, other arithmetic: 131 us -> 0.01 us  [body(): listed = (listed + listed.T > 0.0).astype(jnp.int32)]
    pallas_call x0 -> x1, Pallas kernels: none -> 78.5 us  [apply_pairs(): pl.pallas_call(pair_kernel, out_shape=jax.ShapeDtypeStruct((32, COLS), jn...]
    all_gather x0 -> x1, blocking collectives: none -> 38.4 us  [body(): pairs = lax.all_gather(pair_list, 'dev', axis=0, tiled=True)]
    while x2 -> x0, local copies, waits for them, and re-layouts: 36.1 us -> none  [apply_pairs(): totals, unused = lax.scan(visit, totals, pair_rows)]
    all_gather x1, waiting for transfers between devices: 53.7 us -> 22.8 us  [body(): lax.all_gather(shared, 'dev', axis=0, tiled=True, axis_index_groups=planes)]
    dynamic_update_slice x11 -> x0, local copies, waits for them, and re-layouts: 19.7 us -> none  [transposed(): lax.dynamic_update_slice(totals, present + backward, (anchor, row_start))]
  transfers between devices with their start and end apart: 7 -> 8, of which waited for: 5 -> 2; matrix products, arithmetic and copies ran while one was open for 31% -> 21% of each run, Pallas kernels for 0% -> 33%
where the time goes in v1:
time: 243 us; the launch traced here: 240 us
  Pallas kernels  78.5 us (32%)
  local copies, waits for them, and re-layouts  41.2 us (17%)
  blocking collectives  38.4 us (16%)
  waiting for transfers between devices  34.4 us (14%)
  starting transfers between devices  18 us (7%)
  between operations  14.2 us (6%)
  other arithmetic  13.8 us (6%)
    pallas_call x1, Pallas kernels, apply_pairs(): pl.pallas_call(pair_kernel, out_shape=jax.ShapeDtypeStruct((32, COLS), jn...  78.5 us
    all_gather x1, blocking collectives, body(): pairs = lax.all_gather(pair_list, 'dev', axis=0, tiled=True)  38.4 us
    all_gather x1, waiting for transfers between devices, body(): lax.all_gather(shared, 'dev', axis=0, tiled=True, axis_index_groups=planes)  22.8 us
    all_gather x1, local copies, waits for them, and re-layouts, body(): gathered = lax.all_gather(surface_top, 'dev', axis=1, tiled=True)  13.6 us
    reduce_scatter x1, waiting for transfers between devices, body(): lax.psum_scatter(partial, 'dev', scatter_dimension=1, axis_index_groups=l...  11.6 us
    gather x2, local copies, waits for them, and re-layouts, body(): traces = jnp.take(flattened, panel_cell, axis=1)  11 us
    unnamed x26, local copies, waits for them, and re-layouts  7.19 us
    ppermute x2, starting transfers between devices, padded_2(): before = lax.ppermute(last, axis, up)  7.1 us
  transfers between devices with their start and end apart: 8, of which 2 were waited for; matrix products, arithmetic and copies ran while one was open for 21% of the time, Pallas kernels for 33%

profile of v1, /device:TPU:1, one launch (start us, length us, event | category | flops | bytes accessed | tf_op | source)
XLA Modules:
  0.0 239.7 jit_solution(5467381244410627908)
XLA Ops:
  7.2 0.9 convert_bitcast_fusion
  8.1 0.6 copy.98
  8.7 6.8 %all-to-all-start = ((bf16[8,32,128]{2,1,0:T(8,128)(2,1)}), bf16[8,32,128]{2,1,0:T(8,128)(2,1)S(1)}, u32[]{:S(2)}, u32[]{:S(2)}) async-start(bf16[8,32,128]{2,1,0:T(8,128)(2,1)} %copy.98), calls=%async_computation | async-start | bytes 131072 | tf_op jit(solution)/shard_map/all_to_all | solution.py:158
  15.6 0.0 all-gather.5.cloned.1.call-start
  15.6 1.3 copy.92
  16.9 2.0 collective-permute-start
  18.9 3.6 %collective-permute-start.1 = (f32[32,8,1,128]{3,0,1,2:T(8,128)S(1)}, f32[32,8,1,128]{3,0,1,2:T(8,128)S(1)}, u32[]{:S(2)}, u32[]{:S(2)}) collective-permute-start(f32[32,8,1,128]{3,0,1,2:T(8,128)S(1)} %get-tuple-element.23), channel_id=1, source_target_pairs={{0,1},{1,2},{2,3},{3,4},{4,5},{5,6},{6,7},{7,8},{8,9},{9,10},{10,1... | collective-permute-start | bytes 393224 | tf_op jit(solution)/shard_map/ppermute | solution.py:30
  22.5 1.7 copy.109
  24.2 0.4 multiply_reduce_fusion
  24.7 1.7 fusion.35
  26.3 0.5 broadcast.133
  26.9 0.8 reduce.17
  28.0 0.0 copy-start.6
  28.1 0.1 fusion.31
  28.2 1.0 multiply_reduce_fusion.1
  29.2 0.1 fusion.46
  29.3 0.0 copy-start.7
  29.3 0.0 copy-start.8
  29.3 0.0 copy-start.4
  29.3 0.8 fusion.43
  30.1 0.2 stack.41
  30.4 0.1 fusion.30
  30.4 0.0 copy-start.1
  30.4 3.3 %copy.100 = bf16[32,64,256]{0,2,1:T(8,128)(2,1)} copy(bf16[32,64,256]{2,1,0:T(8,128)(2,1)S(1)} %broadcast_dynamic-update-slice_fusion) | data formatting | bytes 2097152 | tf_op jit(solution)/shard_map/concatenate | solution.py:81
  33.8 0.8 slice.133
  34.6 0.0 copy-done.6
  34.6 38.4 %all-gather.1 = s32[128,16,2]{1,2,0:T(2,128)S(1)} all-gather(s32[1,16,2]{1,2,0:T(2,128)S(1)} %bitcast.82), channel_id=1, replica_groups=mesh['dev'=128] {'dev'}, dimensions={0}, use_global_device_ids=true | all-gather | bytes 16512 | tf_op jit(solution)/shard_map/all_gather | solution.py:147
  73.1 0.1 reshape.146
  73.2 0.0 all-to-all-done
  73.2 0.0 copy-start.3
  73.2 0.6 copy-done.3
  73.8 0.0 all-gather.5.cloned.1.call-update
  73.8 0.0 all-gather.7.cloned.1.call-start
  73.9 1.0 fusion
  74.9 0.1 copy.97
  75.0 0.1 reshape.128.mask_ref
  75.1 0.0 copy-done.7
  75.1 0.1 select_reduce_fusion
  75.2 0.1 multiply_add_fusion
  75.3 1.3 concatenate.39.q_ref
  76.6 0.0 collective-permute-done
  76.6 0.0 collective-permute-done.1
  76.7 0.5 fusion.10
  77.2 2.1 collective-permute-start.2
  79.3 3.5 %collective-permute-start.3 = (f32[32,8,1,128]{3,0,1,2:T(8,128)S(1)}, f32[32,8,1,128]{3,0,1,2:T(8,128)S(1)}, u32[]{:S(2)}, u32[]{:S(2)}) collective-permute-start(f32[32,8,1,128]{3,0,1,2:T(8,128)S(1)} %get-tuple-element.21), channel_id=1, source_target_pairs={{0,1},{1,2},{2,3},{3,4},{4,5},{5,6},{6,7},{7,8},{8,9},{9,10},{10,1... | collective-permute-start | bytes 393224 | tf_op jit(solution)/shard_map/ppermute | solution.py:30
  82.8 5.0 %pad_maximum_fusion.pt_ref = bf16[65,256,32]{2,1,0:T(8,128)(2,1)} fusion(bf16[1,256,32]{2,1,0:T(8,128)(2,1)S(1)} %slice.133, bf16[64,256,32]{2,1,0:T(8,128)(2,1)} %bitcast.64), kind=kLoop, calls=%fused_computation.1 | loop fusion | flops 532480 | bytes 2129920 | tf_op jit(solution)/shard_map/concatenate | solution.py:167
  87.8 0.0 collective-permute-done.2
  87.8 0.0 collective-permute-done.3
  87.8 0.6 fusion.21
  88.4 0.6 slice.217
  89.0 0.0 all-gather.7.cloned.1.call-update
  89.1 0.0 reduce-scatter.2.cloned.1.call-start
  89.1 22.8 %all-gather.5.cloned.1.call-done = bf16[128,32,128]{2,1,0:T(8,128)(2,1)} async-done(((bf16[8,32,128]{2,1,0:T(8,128)(2,1)}), bf16[128,32,128]{2,1,0:T(8,128)(2,1)}) %all-gather.5.cloned.1.call-update) | async-done | bytes 1048592 | tf_op jit(solution)/shard_map/all_gather | solution.py:159
  111.9 1.4 copy.110
  113.3 0.1 concatenate.36.f_ref
  113.4 2.2 copy-done
  115.6 78.5 %shard_map.113 = f32[32,8192]{1,0:T(8,128)} custom-call(s32[256]{0:T(256)S(1)} %reshape.128.mask_ref, bf16[65,32,256]{2,1,0:T(8,128)(2,1)S(1)} %concatenate.36.f_ref, bf16[65,256,32]{2,1,0:T(8,128)(2,1)S(1)} %copy-done, bf16[32,8192]{1,0:T(8,128)(2,1)S(1)} %concatenate.39.q_ref), custom_call_target="tpu_custom_call" | custom-call | flops 99999997952 | bytes 8388608 | tf_op jit(solution)/shard_map/pallas_call | solution.py:117
  194.1 0.0 reduce-scatter.2.cloned.1.call-update
  194.2 1.1 copy.101
  195.3 13.6 %copy.94 = bf16[32,1,512,128]{0,3,2,1:T(8,128)(2,1)} copy(bf16[32,1,512,128]{3,0,1,2:T(8,128)(2,1)} %all-gather.7.cloned.1.call-done) | data formatting | bytes 8388608 | tf_op jit(solution)/shard_map/all_gather | solution.py:180
  208.9 10.9 %gather_fusion = bf16[1024,32]{1,0:T(8,128)(2,1)S(1)} fusion(bf16[32,65536]{0,1:T(8,128)(2,1)} %bitcast.62, s32[1024]{0:T(1024)S(1)} %fusion.40), kind=kCustom, calls=%fused_computation | custom fusion | bytes 135168 | tf_op jit(solution)/shard_map/jit(_take)/gather | solution.py:187
  219.8 0.1 copy.95
  220.0 11.6 %reduce-scatter.2.cloned.1.call-done = f32[32,1024]{1,0:T(8,128)} async-done(((f32[32,8192]{1,0:T(8,128)}), f32[32,1024]{1,0:T(8,128)}) %reduce-scatter.2.cloned.1.call-update) | async-done | bytes 131088 | tf_op jit(solution)/shard_map/reduce_scatter | solution.py:184
  231.6 1.6 fusion.33
  (38 shorter events, 0.4 us)
Async XLA Ops:
  8.7 64.4 %all-to-all-start = ((bf16[8,32,128]{2,1,0:T(8,128)(2,1)}), bf16[8,32,128]{2,1,0:T(8,128)(2,1)S(1)}, u32[]{:S(2)}, u32[]{:S(2)}) async-start(bf16[8,32,128]{2,1,0:T(8,128)(2,1)} %copy.98), calls=%async_computation | async-start | bytes 131072 | tf_op jit(solution)/shard_map/all_to_all | solution.py:158
  15.6 96.3 %all-gather.5.cloned.1.call-start = ((), (), s32[]{:S(2)}) async-start(), calls=%async_computation.2 | async-start | bytes 1114112 | tf_op jit(solution)/shard_map/all_gather | solution.py:159
  16.9 59.7 %collective-permute-start = (f32[32,8,1,128]{3,0,1,2:T(8,128)S(1)}, f32[32,8,1,128]{3,0,1,2:T(8,128)S(1)}, u32[]{:S(2)}, u32[]{:S(2)}) collective-permute-start(f32[32,8,1,128]{3,0,1,2:T(8,128)S(1)} %get-tuple-element.22), channel_id=1, source_target_pairs={{1,0},{2,1},{3,2},{4,3},{5,4},{6,5},{7,6},{8,7},{9,8},{10,9},{11,1... | collective-permute-start | bytes 393224 | tf_op jit(solution)/shard_map/ppermute | solution.py:31
  18.9 57.7 %collective-permute-start.1 = (f32[32,8,1,128]{3,0,1,2:T(8,128)S(1)}, f32[32,8,1,128]{3,0,1,2:T(8,128)S(1)}, u32[]{:S(2)}, u32[]{:S(2)}) collective-permute-start(f32[32,8,1,128]{3,0,1,2:T(8,128)S(1)} %get-tuple-element.23), channel_id=1, source_target_pairs={{0,1},{1,2},{2,3},{3,4},{4,5},{5,6},{6,7},{7,8},{8,9},{9,10},{10,1... | collective-permute-start | bytes 393224 | tf_op jit(solution)/shard_map/ppermute | solution.py:30
  28.0 6.6 %copy-start.6 = (s32[16,2]{0,1:T(2,128)S(1)}, s32[16,2]{0,1:T(2,128)}, u32[]{:S(2)}) copy-start(s32[16,2]{0,1:T(2,128)} %param.19) | copy-start | bytes 388
  29.3 45.8 %copy-start.7 = (f32[4]{0:T(128)S(1)}, f32[4]{0:T(128)}, u32[]{:S(2)}) copy-start(f32[4]{0:T(128)} %param.14) | copy-start | bytes 52
  29.3 45.8 %copy-start.8 = (s32[8]{0:T(128)S(1)}, s32[8]{0:T(128)}, u32[]{:S(2)}) copy-start(s32[8]{0:T(128)} %param.13) | copy-start | bytes 100
  29.3 45.9 %copy-start.4 = (f32[8,4,128]{2,1,0:T(4,128)S(1)}, f32[8,4,128]{2,1,0:T(4,128)}, u32[]{:S(2)}) copy-start(f32[8,4,128]{2,1,0:T(4,128)} %param.12) | copy-start | bytes 49156
  30.4 46.2 %copy-start.1 = (f32[32,8,4,128]{3,2,1,0:T(4,128)S(1)}, f32[32,8,4,128]{3,2,1,0:T(4,128)}, u32[]{:S(2)}) copy-start(f32[32,8,4,128]{3,2,1,0:T(4,128)} %param.11) | copy-start | bytes 1572868
  73.2 0.6 copy-start.3
  73.8 121.5 %all-gather.7.cloned.1.call-start = ((), (), s32[]{:S(2)}) async-start(), calls=%async_computation.4 | async-start | bytes 4227072 | tf_op jit(solution)/shard_map/all_gather | solution.py:180
  77.2 10.6 %collective-permute-start.2 = (f32[32,8,1,128]{3,0,1,2:T(8,128)S(1)}, f32[32,8,1,128]{3,0,1,2:T(8,128)S(1)}, u32[]{:S(2)}, u32[]{:S(2)}) collective-permute-start(f32[32,8,1,128]{3,0,1,2:T(8,128)S(1)} %get-tuple-element.20), channel_id=1, source_target_pairs={{1,0},{2,1},{3,2},{4,3},{5,4},{6,5},{7,6},{8,7},{9,8},{10,9},{11,1... | collective-permute-start | bytes 393224 | tf_op jit(solution)/shard_map/ppermute | solution.py:31
  79.3 8.5 %collective-permute-start.3 = (f32[32,8,1,128]{3,0,1,2:T(8,128)S(1)}, f32[32,8,1,128]{3,0,1,2:T(8,128)S(1)}, u32[]{:S(2)}, u32[]{:S(2)}) collective-permute-start(f32[32,8,1,128]{3,0,1,2:T(8,128)S(1)} %get-tuple-element.21), channel_id=1, source_target_pairs={{0,1},{1,2},{2,3},{3,4},{4,5},{5,6},{6,7},{7,8},{8,9},{9,10},{10,1... | collective-permute-start | bytes 393224 | tf_op jit(solution)/shard_map/ppermute | solution.py:30
  89.1 142.5 %reduce-scatter.2.cloned.1.call-start = ((), (), s32[]{:S(2)}) async-start(), calls=%async_computation.3 | async-start | bytes 1179648 | tf_op jit(solution)/shard_map/reduce_scatter | solution.py:184
  113.4 2.2 copy-start
  115.6 78.5 %copy-start.5 = (s32[1024]{0:T(1024)S(1)}, s32[1024]{0:T(1024)}, u32[]{:S(2)}) copy-start(s32[1024]{0:T(1024)} %param.15) | copy-start | bytes 12292
  195.3 36.3 %copy-start.2 = (f32[32,1024]{1,0:T(8,128)S(1)}, f32[32,1024]{1,0:T(8,128)}, u32[]{:S(2)}) copy-start(f32[32,1024]{1,0:T(8,128)} %param.18) | copy-start | bytes 393220
Sparse Core Ops, SparseCore 0:
  74.0 37.8 all-gather.4
  115.1 68.2 all-gather.6
  194.2 37.2 reduce-scatter.1

commit v2 on v1

v2 whole, which is shorter than its diff:
```python
import math

import jax
import jax.numpy as jnp
from jax import lax
from jax.experimental import pallas as pl
from jax.experimental.pallas import tpu as pltpu
from jax.sharding import PartitionSpec as P

TILE = 2048
TILES = 64
LAYERS = 8
LINE = 8
PLANE = 16
COLS = 4 * TILE

softening = 0.0004
relax_rate = 0.8
update_rate = 0.5
kernel_gain = 0.25


def coefficient(cell_factor, layer_material, material_scale):
    matched = (
        layer_material[:, None] == jnp.arange(material_scale.shape[0], dtype=jnp.int32)[None, :]
    )
    layer_scale = jnp.sum(jnp.where(matched, material_scale[None, :], 0.0), axis=1)
    return layer_scale[:, None, None] * cell_factor


def relax_rows(widened, source, conduct):
    centre = widened[:, :, 1:-1, :]
    padded = jnp.pad(centre, ((0, 0), (1, 1), (0, 0), (1, 1)))
    beside = (
        padded[:, 2:, :, 1:-1]
        + padded[:, :-2, :, 1:-1]
        + (widened[:, :, 2:, :] + widened[:, :, :-2, :])
        + (padded[:, 1:-1, :, 2:] + padded[:, 1:-1, :, :-2])
    )
    applied = conduct * (6.0 * centre - beside) + centre
    return centre + relax_rate * (source - applied) / (6.0 * conduct + 1.0)


def split3(value):
    high = lax.reduce_precision(value, 8, 7)
    rest = value - high
    middle = lax.reduce_precision(rest, 8, 7)
    low = lax.reduce_precision(rest - middle, 8, 7)
    return high, middle, low


def features(pos, area, row_side):
    pos = pos - 0.5
    scale = math.sqrt(TILE) / kernel_gain / (area * area)
    norm = jnp.sum(pos * pos, axis=0)
    if row_side:
        parts = jnp.stack(
            [scale * (norm + softening), scale] + [-2.0 * scale * pos[a] for a in range(3)]
        )
    else:
        parts = jnp.stack([scale, scale * norm] + [scale * pos[a] for a in range(3)])
    high, middle, low = split3(parts)
    if row_side:
        stack = [high, high, middle, middle, high, low]
    else:
        stack = [high, middle, high, middle, low, high]
    stack.append(jnp.zeros((2,) + parts.shape[1:], jnp.float32))
    return jnp.concatenate(stack, axis=0).astype(jnp.bfloat16)


def pair_kernel(mask_ref, f_ref, pt_ref, q_ref, o_ref, total_ref, order_ref):
    for j in range(4):

        def note(i, count):
            order_ref[count] = i
            return count + mask_ref[j * TILES + i]

        count = lax.fori_loop(0, TILES, note, jnp.int32(0))
        order_ref[count] = 0
        total_ref[...] = jnp.zeros((32, TILE), jnp.float32)

        def flux_of(i):
            at = pl.multiple_of((i % 4) * 64, 64)
            return [f_ref[i // 4, pl.ds(at, 32), :], f_ref[i // 4, pl.ds(at + 32, 32), :]]

        def step(b, carry):
            first = order_ref[2 * b]
            second = order_ref[2 * b + 1]
            there = 2 * b + 1 < count
            later = [jnp.where(there, part, jnp.zeros_like(part)) for part in flux_of(second)]
            flux = jnp.concatenate(flux_of(first) + later, axis=1)
            for c in range(2):
                columns = pl.ds(j * TILE + c * 1024, 1024)
                block = []
                for which in (first, second):
                    distance = jnp.dot(
                        pt_ref[which], q_ref[:, columns], preferred_element_type=jnp.float32
                    )
                    block.append(lax.rsqrt(distance).astype(jnp.bfloat16))
                total_ref[:, c * 1024 : (c + 1) * 1024] += jnp.dot(
                    flux, jnp.concatenate(block, axis=0), preferred_element_type=jnp.float32
                )
            return carry

        lax.fori_loop(0, (count + 1) // 2, step, 0)
        for c in range(2):
            o_ref[2 * j + c] = total_ref[:, c * 1024 : (c + 1) * 1024].astype(jnp.bfloat16)


def apply_pairs(mask, flux_rows, row_features, col_features):
    vmem = pl.BlockSpec(memory_space=pltpu.VMEM)
    return pl.pallas_call(
        pair_kernel,
        out_shape=jax.ShapeDtypeStruct((LINE, 32, 1024), jnp.bfloat16),
        in_specs=[pl.BlockSpec(memory_space=pltpu.SMEM), vmem, vmem, vmem],
        out_specs=vmem,
        scratch_shapes=[
            pltpu.VMEM((32, TILE), jnp.float32),
            pltpu.SMEM((TILES + 2,), jnp.int32),
        ],
        compiler_params=pltpu.CompilerParams(vmem_limit_bytes=40 << 20),
        cost_estimate=pl.CostEstimate(
            flops=100_000_000_000, bytes_accessed=8 << 20, transcendentals=0
        ),
    )(mask, flux_rows, row_features, col_features)


def remote(src, dst, sends, recvs, at, device):
    return pltpu.make_async_remote_copy(
        src_ref=src,
        dst_ref=dst,
        send_sem=sends.at[at],
        recv_sem=recvs.at[at],
        device_id=(device,),
        device_id_type=pl.DeviceIdType.MESH,
    )


def greet(devices):
    barrier = pltpu.get_barrier_semaphore()
    for device in devices:
        pl.semaphore_signal(
            barrier, inc=1, device_id=(device,), device_id_type=pl.DeviceIdType.MESH
        )
    pl.semaphore_wait(barrier, len(devices))


def exchange_kernel(
    flux_ref,
    edge_ref,
    rows_ref,
    halo_ref,
    shared,
    line_send,
    line_recv,
    plane_send,
    plane_recv,
    edge_send,
    edge_recv,
):
    me = lax.axis_index("dev")
    m, r = me // LINE, lax.rem(me, LINE)
    line = [LINE * m + lax.rem(r + k, LINE) for k in range(1, LINE)]
    plane = [LINE * lax.rem(m + k, PLANE) + r for k in range(1, PLANE)]
    after = lax.rem(me + 1, LINE * PLANE)
    before = lax.rem(me + LINE * PLANE - 1, LINE * PLANE)
    greet(line + plane + [after, before])

    copies = []
    for k in range(1, LINE):
        there = lax.rem(r + k, LINE)
        copy = remote(
            flux_ref.at[there], shared.at[r], line_send, line_recv, k - 1, line[k - 1]
        )
        copy.start()
        copies.append(copy)
    edges = [
        remote(edge_ref.at[0], halo_ref.at[0], edge_send, edge_recv, 0, after),
        remote(edge_ref.at[1], halo_ref.at[1], edge_send, edge_recv, 1, before),
    ]
    for copy in edges:
        copy.start()
    shared[r] = flux_ref[r]
    for copy in copies:
        copy.wait()

    lists = jnp.zeros((16, 128), jnp.float32)
    for s in range(LINE):
        rows_ref[m, 32 * s : 32 * s + 32, :] = shared[s, 0:32, :]
        lists = lists + shared[s, 32:48, :].astype(jnp.float32)
    rows_ref[m, 256:272, :] = lists.astype(jnp.bfloat16)

    copies = []
    for k in range(1, PLANE):
        copy = remote(
            rows_ref.at[m], rows_ref.at[m], plane_send, plane_recv, k - 1, plane[k - 1]
        )
        copy.start()
        copies.append(copy)
    for copy in copies + edges:
        copy.wait()


def exchange(flux, edge):
    vmem = pl.BlockSpec(memory_space=pltpu.VMEM)
    return pl.pallas_call(
        exchange_kernel,
        out_shape=(
            jax.ShapeDtypeStruct((PLANE, 272, 128), jnp.bfloat16),
            jax.ShapeDtypeStruct(edge.shape, jnp.float32),
        ),
        in_specs=[vmem, vmem],
        out_specs=(vmem, vmem),
        scratch_shapes=[
            pltpu.VMEM((LINE, 48, 128), jnp.bfloat16),
            pltpu.SemaphoreType.DMA((LINE - 1,)),
            pltpu.SemaphoreType.DMA((LINE - 1,)),
            pltpu.SemaphoreType.DMA((PLANE - 1,)),
            pltpu.SemaphoreType.DMA((PLANE - 1,)),
            pltpu.SemaphoreType.DMA((2,)),
            pltpu.SemaphoreType.DMA((2,)),
        ],
        compiler_params=pltpu.CompilerParams(
            collective_id=0, has_side_effects=True, vmem_limit_bytes=16 << 20
        ),
    )(flux, edge)


def finish_kernel(
    cell_ref, part_ref, table_ref, flux_ref, out_ref, table, landed, traces, load_sem, sends, recvs
):
    me = lax.axis_index("dev")
    m, r = me // LINE, lax.rem(me, LINE)
    load = pltpu.make_async_copy(table_ref, table, load_sem)
    load.start()
    line = [LINE * m + lax.rem(r + k, LINE) for k in range(1, LINE)]
    greet(line)
    copies = []
    for k in range(1, LINE):
        there = lax.rem(r + k, LINE)
        copy = remote(part_ref.at[there], landed.at[k - 1], sends, recvs, k - 1, line[k - 1])
        copy.start()
        copies.append(copy)
    load.wait()
    lane = lax.broadcasted_iota(jnp.int32, (32, 128), 1)

    def group(g, carry):
        def pick(step, held):
            for u in range(8):
                at = step * 8 + u
                cell = cell_ref[g * 128 + at]
                block = table[cell // 128].astype(jnp.float32)
                moved = pltpu.roll(block, lax.rem(at + 128 - lax.rem(cell, 128), 128), axis=1)
                held = jnp.where(lane == at, moved, held)
            return held

        traces[g] = lax.fori_loop(0, 16, pick, jnp.zeros((32, 128), jnp.float32))
        return carry

    lax.fori_loop(0, 8, group, 0)
    for copy in copies:
        copy.wait()
    total = part_ref[r].astype(jnp.float32)
    for k in range(LINE - 1):
        total = total + landed[k].astype(jnp.float32)
    for g in range(8):
        at = slice(g * 128, (g + 1) * 128)
        out_ref[:, at] = flux_ref[:, at] + update_rate * (traces[g] - total[:, at])


def finish(cells, partial, table, flux_in):
    vmem = pl.BlockSpec(memory_space=pltpu.VMEM)
    return pl.pallas_call(
        finish_kernel,
        out_shape=jax.ShapeDtypeStruct(flux_in.shape, jnp.float32),
        in_specs=[
            pl.BlockSpec(memory_space=pltpu.SMEM),
            vmem,
            pl.BlockSpec(memory_space=pl.ANY),
            vmem,
        ],
        out_specs=vmem,
        scratch_shapes=[
            pltpu.VMEM(table.shape, jnp.bfloat16),
            pltpu.VMEM((LINE - 1, 32, 1024), jnp.bfloat16),
            pltpu.VMEM((8, 32, 128), jnp.float32),
            pltpu.SemaphoreType.DMA,
            pltpu.SemaphoreType.DMA((LINE - 1,)),
            pltpu.SemaphoreType.DMA((LINE - 1,)),
        ],
        compiler_params=pltpu.CompilerParams(
            collective_id=1, has_side_effects=True, vmem_limit_bytes=16 << 20
        ),
    )(cells, partial, table, flux_in)


def body(
    field_in,
    source,
    cell_factor,
    layer_material,
    material_scale,
    panel_cell,
    panel_pos,
    panel_area,
    flux_in,
    pair_list,
):
    me = lax.axis_index("dev")
    m, r = me // LINE, me % LINE

    flux_half = flux_in.astype(jnp.bfloat16).reshape(32, LINE, 128).transpose(1, 0, 2)
    own_list = jnp.pad(pair_list.astype(jnp.bfloat16).reshape(1, 32), ((0, 0), (0, 96)))
    in_row = jnp.arange(16, dtype=jnp.int32)[:, None] == r
    own_list = jnp.where(in_row, own_list, jnp.zeros_like(own_list))
    own_list = jnp.broadcast_to(own_list, (LINE, 16, 128))
    edge = [
        [
            field_in[:, :, at : at + 2].reshape(-1, 128),
            source[:, :, one].reshape(-1, 128),
            cell_factor[:, one].reshape(-1, 128),
        ]
        for at, one in ((2, 3), (0, 0))
    ]
    edge = jnp.stack([jnp.concatenate(side, axis=0) for side in edge], axis=0)
    rows, halo = exchange(jnp.concatenate([flux_half, own_list], axis=1), edge)

    pairs = rows[:, 256:264, 0:32].reshape(-1, 2)
    tile_ids = jnp.arange(TILES, dtype=jnp.bfloat16)
    upper = (pairs[:, 0:1] == tile_ids[None, :]).astype(jnp.bfloat16)
    lower = (pairs[:, 1:2] == tile_ids[None, :]).astype(jnp.bfloat16)
    listed = lax.dot_general(
        upper, lower, (((0,), (0,)), ((), ())), preferred_element_type=jnp.float32
    )
    listed = (listed + listed.T > 0.0).astype(jnp.int32)
    mask = lax.dynamic_slice(listed, (4 * m, 0), (4, TILES)).reshape(-1)

    row_pos = lax.dynamic_index_in_dim(panel_pos.reshape(3, 128, LINE, 128), r, 2, False)
    row_area = lax.dynamic_index_in_dim(panel_area.reshape(128, LINE, 128), r, 1, False)
    row_features = features(row_pos.reshape(3, -1), row_area.reshape(-1), True)
    row_features = row_features.reshape(32, TILES, 256).transpose(1, 2, 0)
    col_features = features(
        lax.dynamic_slice(panel_pos, (0, m * COLS), (3, COLS)),
        lax.dynamic_slice(panel_area, (m * COLS,), (COLS,)),
        False,
    )

    inner = jnp.array([me > 0, me < LINE * PLANE - 1])
    halo = jnp.where(inner[:, None, None], halo, 0.0)
    halo_field = halo[:, 0:512].reshape(2, 32, LAYERS, 2, 128)
    halo_source = halo[:, 512:768].reshape(2, 32, LAYERS, 1, 128)
    halo_factor = halo[:, 768:776].reshape(2, LAYERS, 1, 128)
    wide_field = jnp.concatenate([halo_field[0], field_in, halo_field[1]], axis=2)
    wide_source = jnp.concatenate([halo_source[0], source, halo_source[1]], axis=2)
    wide_factor = jnp.concatenate([halo_factor[0], cell_factor, halo_factor[1]], axis=1)
    conduct = coefficient(wide_factor, layer_material, material_scale)
    once = relax_rows(wide_field, wide_source, conduct)
    place = jnp.arange(6, dtype=jnp.int32)[:, None]
    kept = ((place > 0) | inner[0]) & ((place < 5) | inner[1])
    once = jnp.where(kept, once, 0.0)
    field_now = relax_rows(once, source, conduct[:, 1:-1])
    surface_top = field_now[:, -1].astype(jnp.bfloat16).transpose(1, 0, 2)
    table = lax.all_gather(surface_top, "dev", axis=0, tiled=True)

    partial = apply_pairs(mask, rows, row_features, col_features)
    flux_out = finish(panel_cell, partial, table, flux_in)
    return (field_now, flux_out)


def solution(mesh):
    in_specs = (
        P(None, None, "dev", None),
        P(None, None, "dev", None),
        P(None, "dev", None),
        P(),
        P(),
        P("dev"),
        P(),
        P(),
        P(None, "dev"),
        P("dev", None),
    )
    out_specs = (P(None, None, "dev", None), P(None, "dev"))
    return jax.shard_map(body, mesh=mesh, in_specs=in_specs, out_specs=out_specs, check_vma=False)
```

time: 243 us -> 170 us (0.70)
  the two profiles are of different devices: /device:TPU:1 before, /device:TPU:11 now
where the time goes in v2:
time: 170 us
  Pallas kernels  128 us (75%)
  local copies, waits for them, and re-layouts  19.3 us (11%)
  between operations  14.6 us (9%)
  other arithmetic  6.8 us (4%)
    pallas_call x1, Pallas kernels, apply_pairs(): pl.pallas_call(pair_kernel, out_shape=jax.ShapeDtypeStruct((LINE, 32, 102...  82.7 us
    pallas_call x1, Pallas kernels, exchange(): pl.pallas_call(exchange_kernel, out_shape=(jax.ShapeDtypeStruct((PLANE, 2...  28.6 us
    pallas_call x1, Pallas kernels, finish(): pl.pallas_call(finish_kernel, out_shape=jax.ShapeDtypeStruct(flux_in.shap...  16.5 us
    unnamed x26, local copies, waits for them, and re-layouts  9.57 us
    concatenate x3, local copies, waits for them, and re-layouts, features(): return jnp.concatenate(stack, axis=0).astype(jnp.bfloat16)  4.6 us
  transfers between devices with their start and end apart: 1, of which 0 were waited for; matrix products, arithmetic and copies ran while one was open for 9% of the time, Pallas kernels for 49%

profile of v2, /device:TPU:11, one launch (start us, length us, event | category | flops | bytes accessed | tf_op | source)
XLA Modules:
  0.0 169.6 jit_solution(6770071246824007141)
XLA Ops:
  7.2 0.0 copy-start.6
  7.2 0.0 copy-start.2
  7.2 0.0 copy-start.5
  7.2 0.0 copy-start.4
  7.2 0.0 all-gather.2.cloned.1.call-start
  7.3 1.6 fusion.47
  8.8 1.4 copy.74
  10.2 0.0 copy-done.6
  10.2 0.1 copy.70
  10.3 0.1 reshape.198
  10.4 0.0 copy-done.2
  10.5 0.0 copy-done.5
  10.5 0.0 copy-done.4
  10.5 0.2 fusion.48
  10.7 0.1 broadcast_select_fusion.1
  10.8 0.1 maximum_bitcast_fusion
  10.9 0.1 pad_maximum_fusion.edge_ref
  11.0 28.6 %shard_map.113 = (bf16[16,272,128]{2,1,0:T(8,128)(2,1)S(1)}, f32[2,776,128]{2,1,0:T(8,128)S(1)}) custom-call(bf16[8,48,128]{2,1,0:T(8,128)(2,1)S(1)} %pad_maximum_fusion.3.flux_ref, f32[2,776,128]{2,1,0:T(8,128)S(1)} %pad_maximum_fusion.edge_ref), custom_call_target="tpu_custom_call" | custom-call | tf_op jit(solution)/shard_map/pallas_call | solution.py:206
  39.6 0.1 pad_add_fusion
  39.7 0.1 broadcast_select_fusion
  39.8 0.0 copy-start.7
  39.8 0.0 copy-start.8
  39.9 0.3 copy.77
  40.2 0.1 copy.75
  40.3 0.1 copy.73
  40.5 0.0 copy-done.7
  40.5 0.0 copy-done.8
  40.5 0.1 select_reduce_fusion
  40.6 0.1 maximum_multiply_fusion
  40.7 0.1 pad_maximum_fusion.1
  40.8 0.6 fusion.14
  41.4 0.6 fusion.24
  42.0 0.6 fusion.41
  42.6 0.0 all-gather.2.cloned.1.call-update
  42.6 1.1 copy.88
  43.8 0.6 reshape.201
  44.4 0.5 slice_reduce_fusion.1
  44.9 1.0 fusion
  46.0 0.1 copy.86
  46.1 0.1 reshape.202.mask_ref
  46.1 1.7 copy.96
  47.8 0.4 multiply_reduce_fusion
  48.3 1.7 fusion.36
  50.0 0.5 broadcast.150
  50.5 0.7 reduce.21
  51.6 0.1 fusion.34
  51.7 3.3 %copy.87 = bf16[32,64,256]{0,2,1:T(8,128)(2,1)} copy(bf16[32,64,256]{2,1,0:T(8,128)(2,1)S(1)} %broadcast_dynamic-update-slice_fusion) | data formatting | bytes 2097152 | tf_op jit(solution)/shard_map/concatenate | solution.py:68
  55.0 1.0 multiply_reduce_fusion.1
  56.0 0.1 fusion.49
  56.0 0.8 fusion.44
  56.8 0.2 stack.53
  57.1 0.1 fusion.31
  57.2 1.3 concatenate.62.q_ref
  58.5 0.0 copy-start
  58.5 2.2 %copy-done = bf16[32,64,256]{0,2,1:T(8,128)(2,1)S(1)} copy-done((bf16[32,64,256]{0,2,1:T(8,128)(2,1)S(1)}, bf16[32,64,256]{0,2,1:T(8,128)(2,1)}, u32[]{:S(2)}) %copy-start) | copy-done | bytes 1048600
  60.7 0.0 copy-start.3
  60.7 82.7 %shard_map.114.part_ref = bf16[8,32,1024]{2,1,0:T(8,128)(2,1)S(1)} custom-call(s32[256]{0:T(256)S(1)} %reshape.202.mask_ref, bf16[16,272,128]{2,1,0:T(8,128)(2,1)S(1)} %get-tuple-element.5.f_ref, bf16[64,256,32]{2,1,0:T(8,128)(2,1)S(1)} %bitcast.79, bf16[32,8192]{1,0:T(8,128)(2,1)S(1)} %concatenate.62.q_ref), custom_call_target="tpu_custom_call" | custom-call | flops 99999997952 | bytes 8388608 | tf_op jit(solution)/shard_map/pallas_call | solution.py:112
  143.4 0.0 all-gather.2.cloned.1.call-done.table_ref
  143.4 0.0 copy-done.3
  143.4 0.0 copy-start.1
  143.4 2.2 %copy-done.1 = bf16[512,32,128]{2,1,0:T(8,128)(2,1)S(1)} copy-done((bf16[512,32,128]{2,1,0:T(8,128)(2,1)S(1)}, bf16[512,32,128]{2,1,0:T(8,128)(2,1)}, u32[]{:S(2)}) %copy-start.1) | copy-done | bytes 4194328
  145.6 16.5 %shard_map.115 = f32[32,1024]{1,0:T(8,128)S(1)} custom-call(s32[1024]{0:T(1024)S(1)} %copy-done.3, bf16[8,32,1024]{2,1,0:T(8,128)(2,1)S(1)} %shard_map.114.part_ref, bf16[512,32,128]{2,1,0:T(8,128)(2,1)S(1)} %copy-done.1, f32[32,1024]{1,0:T(8,128)S(1)} %copy-done.2), custom_call_target="tpu_custom_call" | custom-call | tf_op jit(solution)/shard_map/pallas_call | solution.py:273
  162.1 0.7 copy.108
  (36 shorter events, 0.6 us)
Async XLA Ops:
  7.2 3.0 %copy-start.6 = (s32[16,2]{0,1:T(2,128)S(1)}, s32[16,2]{0,1:T(2,128)}, u32[]{:S(2)}) copy-start(s32[16,2]{0,1:T(2,128)} %param.19) | copy-start | bytes 388
  7.2 3.3 %copy-start.2 = (f32[32,1024]{1,0:T(8,128)S(1)}, f32[32,1024]{1,0:T(8,128)}, u32[]{:S(2)}) copy-start(f32[32,1024]{1,0:T(8,128)} %flux_ref.1) | copy-start | bytes 393220
  7.2 3.3 %copy-start.5 = (f32[8,4,128]{2,1,0:T(4,128)S(1)}, f32[8,4,128]{2,1,0:T(4,128)}, u32[]{:S(2)}) copy-start(f32[8,4,128]{2,1,0:T(4,128)} %param.12) | copy-start | bytes 49156
  7.2 3.3 %copy-start.4 = (f32[32,8,4,128]{3,2,1,0:T(4,128)S(1)}, f32[32,8,4,128]{3,2,1,0:T(4,128)}, u32[]{:S(2)}) copy-start(f32[32,8,4,128]{3,2,1,0:T(4,128)} %param.11) | copy-start | bytes 1572868
  7.2 136.2 %all-gather.2.cloned.1.call-start = ((), (), s32[]{:S(2)}) async-start(), calls=%async_computation | async-start | bytes 4227072 | tf_op jit(solution)/shard_map/all_gather | solution.py:363
  39.8 0.7 copy-start.7
  39.8 0.7 copy-start.8
  58.5 2.2 %copy-start = (bf16[32,64,256]{0,2,1:T(8,128)(2,1)S(1)}, bf16[32,64,256]{0,2,1:T(8,128)(2,1)}, u32[]{:S(2)}) copy-start(bf16[32,64,256]{0,2,1:T(8,128)(2,1)} %copy.87) | copy-start | bytes 3145732
  60.7 82.7 %copy-start.3 = (s32[1024]{0:T(1024)S(1)}, s32[1024]{0:T(1024)}, u32[]{:S(2)}) copy-start(s32[1024]{0:T(1024)} %cell_ref.1) | copy-start | bytes 12292
  143.4 2.2 %copy-start.1 = (bf16[512,32,128]{2,1,0:T(8,128)(2,1)S(1)}, bf16[512,32,128]{2,1,0:T(8,128)(2,1)}, u32[]{:S(2)}) copy-start(bf16[512,32,128]{2,1,0:T(8,128)(2,1)} %all-gather.2.cloned.1.call-done.table_ref) | copy-start | bytes 12582916
Sparse Core Ops, SparseCore 0:
  42.8 65.6 all-gather.1

commit v3 on v2

--- a/solution.py
+++ b/solution.py
@@ -10,6 +10,7 @@
 TILE = 2048
 TILES = 64
 LAYERS = 8
+UNROLL = 4
 LINE = 8
 PLANE = 16
 COLS = 4 * TILE
@@ -41,70 +42,47 @@
     return centre + relax_rate * (source - applied) / (6.0 * conduct + 1.0)
 
 
-def split3(value):
-    high = lax.reduce_precision(value, 8, 7)
-    rest = value - high
-    middle = lax.reduce_precision(rest, 8, 7)
-    low = lax.reduce_precision(rest - middle, 8, 7)
-    return high, middle, low
-
-
-def features(pos, area, row_side):
-    pos = pos - 0.5
-    scale = math.sqrt(TILE) / kernel_gain / (area * area)
-    norm = jnp.sum(pos * pos, axis=0)
-    if row_side:
-        parts = jnp.stack(
-            [scale * (norm + softening), scale] + [-2.0 * scale * pos[a] for a in range(3)]
-        )
-    else:
-        parts = jnp.stack([scale, scale * norm] + [scale * pos[a] for a in range(3)])
-    high, middle, low = split3(parts)
-    if row_side:
-        stack = [high, high, middle, middle, high, low]
-    else:
-        stack = [high, middle, high, middle, low, high]
-    stack.append(jnp.zeros((2,) + parts.shape[1:], jnp.float32))
-    return jnp.concatenate(stack, axis=0).astype(jnp.bfloat16)
-
-
-def pair_kernel(mask_ref, f_ref, pt_ref, q_ref, o_ref, total_ref, order_ref):
+def pair_kernel(mask_ref, f_ref, pt_ref, q_ref, o_ref, total_ref, held_ref, order_ref):
+    order_ref[0] = 0
+
+    def note(at, count):
+        order_ref[count + 1] = at
+        return count + mask_ref[at]
+
+    count = lax.fori_loop(0, 4 * TILES, note, jnp.int32(0))
+    for u in range(UNROLL + 1):
+        order_ref[count + 1 + u] = 0
+    total_ref[...] = jnp.zeros(total_ref.shape, jnp.float32)
+    held_ref[1] = jnp.zeros((256, TILE), jnp.bfloat16)
+
+    def step(b, carry):
+        for u in range(UNROLL):
+            t = b * UNROLL + u
+            new, old = order_ref[t + 1], order_ref[t]
+            valid = (t >= 1) & (t <= count)
+            i = old % TILES
+            at = pl.multiple_of((i % 4) * 64, 64)
+            flux = jnp.concatenate(
+                [f_ref[i // 4, pl.ds(at, 32), :], f_ref[i // 4, pl.ds(at + 32, 32), :]], axis=1
+            )
+            flux = jnp.where(valid, flux, jnp.zeros_like(flux))
+            for c in range(4):
+                columns = slice(c * 512, (c + 1) * 512)
+                distance = jnp.dot(
+                    pt_ref[new % TILES],
+                    q_ref[new // TILES, :, columns],
+                    preferred_element_type=jnp.float32,
+                )
+                held_ref[u % 2, :, columns] = lax.rsqrt(distance).astype(jnp.bfloat16)
+                total_ref[old // TILES, :, columns] += jnp.dot(
+                    flux, held_ref[1 - u % 2, :, columns], preferred_element_type=jnp.float32
+                )
+        return carry
+
+    lax.fori_loop(0, (count + UNROLL) // UNROLL, step, 0)
     for j in range(4):
-
-        def note(i, count):
-            order_ref[count] = i
-            return count + mask_ref[j * TILES + i]
-
-        count = lax.fori_loop(0, TILES, note, jnp.int32(0))
-        order_ref[count] = 0
-        total_ref[...] = jnp.zeros((32, TILE), jnp.float32)
-
-        def flux_of(i):
-            at = pl.multiple_of((i % 4) * 64, 64)
-            return [f_ref[i // 4, pl.ds(at, 32), :], f_ref[i // 4, pl.ds(at + 32, 32), :]]
-
-        def step(b, carry):
-            first = order_ref[2 * b]
-            second = order_ref[2 * b + 1]
-            there = 2 * b + 1 < count
-            later = [jnp.where(there, part, jnp.zeros_like(part)) for part in flux_of(second)]
-            flux = jnp.concatenate(flux_of(first) + later, axis=1)
-            for c in range(2):
-                columns = pl.ds(j * TILE + c * 1024, 1024)
-                block = []
-                for which in (first, second):
-                    distance = jnp.dot(
-                        pt_ref[which], q_ref[:, columns], preferred_element_type=jnp.float32
-                    )
-                    block.append(lax.rsqrt(distance).astype(jnp.bfloat16))
-                total_ref[:, c * 1024 : (c + 1) * 1024] += jnp.dot(
-                    flux, jnp.concatenate(block, axis=0), preferred_element_type=jnp.float32
-                )
-            return carry
-
-        lax.fori_loop(0, (count + 1) // 2, step, 0)
         for c in range(2):
-            o_ref[2 * j + c] = total_ref[:, c * 1024 : (c + 1) * 1024].astype(jnp.bfloat16)
+            o_ref[2 * j + c] = total_ref[j, :, c * 1024 : (c + 1) * 1024].astype(jnp.bfloat16)
 
 
 def apply_pairs(mask, flux_rows, row_features, col_features):
@@ -115,10 +93,11 @@
         in_specs=[pl.BlockSpec(memory_space=pltpu.SMEM), vmem, vmem, vmem],
         out_specs=vmem,
         scratch_shapes=[
-            pltpu.VMEM((32, TILE), jnp.float32),
-            pltpu.SMEM((TILES + 2,), jnp.int32),
+            pltpu.VMEM((4, 32, TILE), jnp.float32),
+            pltpu.VMEM((2, 256, TILE), jnp.bfloat16),
+            pltpu.SMEM((4 * TILES + UNROLL + 2,), jnp.int32),
         ],
-        compiler_params=pltpu.CompilerParams(vmem_limit_bytes=40 << 20),
+        compiler_params=pltpu.CompilerParams(vmem_limit_bytes=20 << 20),
         cost_estimate=pl.CostEstimate(
             flops=100_000_000_000, bytes_accessed=8 << 20, transcendentals=0
         ),
@@ -145,68 +124,45 @@
     pl.semaphore_wait(barrier, len(devices))
 
 
-def exchange_kernel(
-    flux_ref,
-    edge_ref,
-    rows_ref,
-    halo_ref,
-    shared,
-    line_send,
-    line_recv,
-    plane_send,
-    plane_recv,
-    edge_send,
-    edge_recv,
+def line_kernel(
+    flux_ref, edge_ref, stage_ref, halo_ref, shared, line_send, line_recv, edge_send, edge_recv
 ):
     me = lax.axis_index("dev")
     m, r = me // LINE, lax.rem(me, LINE)
     line = [LINE * m + lax.rem(r + k, LINE) for k in range(1, LINE)]
-    plane = [LINE * lax.rem(m + k, PLANE) + r for k in range(1, PLANE)]
     after = lax.rem(me + 1, LINE * PLANE)
     before = lax.rem(me + LINE * PLANE - 1, LINE * PLANE)
-    greet(line + plane + [after, before])
-
-    copies = []
-    for k in range(1, LINE):
-        there = lax.rem(r + k, LINE)
-        copy = remote(
-            flux_ref.at[there], shared.at[r], line_send, line_recv, k - 1, line[k - 1]
-        )
-        copy.start()
-        copies.append(copy)
+    greet(line + [after, before])
     edges = [
         remote(edge_ref.at[0], halo_ref.at[0], edge_send, edge_recv, 0, after),
         remote(edge_ref.at[1], halo_ref.at[1], edge_send, edge_recv, 1, before),
     ]
-    for copy in edges:
+    copies = []
+    for k in range(1, LINE):
+        there = lax.rem(r + k, LINE)
+        copies.append(
+            remote(flux_ref.at[there], shared.at[r], line_send, line_recv, k - 1, line[k - 1])
+        )
+    for copy in edges + copies:
         copy.start()
     shared[r] = flux_ref[r]
     for copy in copies:
         copy.wait()
-
     lists = jnp.zeros((16, 128), jnp.float32)
     for s in range(LINE):
-        rows_ref[m, 32 * s : 32 * s + 32, :] = shared[s, 0:32, :]
+        stage_ref[32 * s : 32 * s + 32, :] = shared[s, 0:32, :]
         lists = lists + shared[s, 32:48, :].astype(jnp.float32)
-    rows_ref[m, 256:272, :] = lists.astype(jnp.bfloat16)
-
-    copies = []
-    for k in range(1, PLANE):
-        copy = remote(
-            rows_ref.at[m], rows_ref.at[m], plane_send, plane_recv, k - 1, plane[k - 1]
-        )
-        copy.start()
-        copies.append(copy)
-    for copy in copies + edges:
+    stage_ref[256:272, :] = lists.astype(jnp.bfloat16)
+    for copy in edges:
         copy.wait()
 
 
-def exchange(flux, edge):
+def exchange_line(flux, edge):
     vmem = pl.BlockSpec(memory_space=pltpu.VMEM)
     return pl.pallas_call(
-        exchange_kernel,
+        line_kernel,
         out_shape=(
-            jax.ShapeDtypeStruct((PLANE, 272, 128), jnp.bfloat16),
+            jax.ShapeDtypeStruct((272, 128), jnp.bfloat16),
             jax.ShapeDtypeStruct(edge.shape, jnp.float32),
         ),
         in_specs=[vmem, vmem],
@@ -215,8 +171,6 @@
             pltpu.VMEM((LINE, 48, 128), jnp.bfloat16),
             pltpu.SemaphoreType.DMA((LINE - 1,)),
             pltpu.SemaphoreType.DMA((LINE - 1,)),
-            pltpu.SemaphoreType.DMA((PLANE - 1,)),
-            pltpu.SemaphoreType.DMA((PLANE - 1,)),
             pltpu.SemaphoreType.DMA((2,)),
             pltpu.SemaphoreType.DMA((2,)),
         ],
@@ -224,6 +178,82 @@
             collective_id=0, has_side_effects=True, vmem_limit_bytes=16 << 20
         ),
     )(flux, edge)
+
+
+def split3(value):
+    high = value.astype(jnp.bfloat16).astype(jnp.float32)
+    rest = value - high
+    middle = rest.astype(jnp.bfloat16).astype(jnp.float32)
+    return high, middle, rest - middle
+
+
+def factors(pos, area, row_side):
+    pos = pos - 0.5
+    scale = (math.sqrt(TILE) / kernel_gain) / (area * area)
+    norm = pos[0:1] * pos[0:1] + pos[1:2] * pos[1:2] + pos[2:3] * pos[2:3]
+    one = jnp.ones_like(norm)
+    rest = jnp.zeros((3, norm.shape[1]), jnp.float32)
+    if row_side:
+        parts = jnp.concatenate([norm + softening, one, -2.0 * pos, rest], axis=0) * scale
+    else:
+        parts = jnp.concatenate([one, norm, pos, rest], axis=0) * scale
+    high, middle, low = split3(parts)
+    if row_side:
+        return jnp.concatenate([high, high, middle, middle, high, low], axis=0)
+    return jnp.concatenate([high, middle, high, middle, low, high], axis=0)
+
+
+def plane_kernel(
+    stage_ref, pos_ref, area_ref, rows_ref, pt_ref, q_ref, plane_send, plane_recv
+):
+    me = lax.axis_index("dev")
+    m, r = me // LINE, lax.rem(me, LINE)
+    plane = [LINE * lax.rem(m + k, PLANE) + r for k in range(1, PLANE)]
+    greet(plane)
+    copies = []
+    for k in range(1, PLANE):
+        copies.append(
+            remote(stage_ref, rows_ref.at[m], plane_send, plane_recv, k - 1, plane[k - 1])
+        )
+    for copy in copies:
+        copy.start()
+    rows_ref[m] = stage_ref[...]
+
+    def row_block(half, carry):
+        at = pl.multiple_of(half * 1024 + r * 128, 128)
+        part = factors(pos_ref[:, pl.ds(at, 128)], area_ref[:, pl.ds(at, 128)], True)
+        pt_ref[half] = part.T.astype(jnp.bfloat16)
+        return carry
+
+    lax.fori_loop(0, 2 * TILES, row_block, 0)
+    for j in range(4):
+        for c in range(4):
+            at = pl.multiple_of(m * COLS + j * TILE + c * 512, 512)
+            part = factors(pos_ref[:, pl.ds(at, 512)], area_ref[:, pl.ds(at, 512)], False)
+            q_ref[j, :, c * 512 : (c + 1) * 512] = part.astype(jnp.bfloat16)
+    for copy in copies:
+        copy.wait()
+
+
+def exchange_plane(stage, pos, area):
+    vmem = pl.BlockSpec(memory_space=pltpu.VMEM)
+    return pl.pallas_call(
+        plane_kernel,
+        out_shape=(
+            jax.ShapeDtypeStruct((PLANE, 272, 128), jnp.bfloat16),
+            jax.ShapeDtypeStruct((2 * TILES, 128, 48), jnp.bfloat16),
+            jax.ShapeDtypeStruct((4, 48, TILE), jnp.bfloat16),
+        ),
+        in_specs=[vmem, vmem, vmem],
+        out_specs=(vmem, vmem, vmem),
+        scratch_shapes=[
+            pltpu.SemaphoreType.DMA((PLANE - 1,)),
+            pltpu.SemaphoreType.DMA((PLANE - 1,)),
+        ],
+        compiler_params=pltpu.CompilerParams(
+            collective_id=2, has_side_effects=True, vmem_limit_bytes=24 << 20
+        ),
+    )(stage, pos, area)
 
 
 def finish_kernel(
@@ -323,27 +353,7 @@
         for at, one in ((2, 3), (0, 0))
     ]
     edge = jnp.stack([jnp.concatenate(side, axis=0) for side in edge], axis=0)
-    rows, halo = exchange(jnp.concatenate([flux_half, own_list], axis=1), edge)
-
-    pairs = rows[:, 256:264, 0:32].reshape(-1, 2)
-    tile_ids = jnp.arange(TILES, dtype=jnp.bfloat16)
-    upper = (pairs[:, 0:1] == tile_ids[None, :]).astype(jnp.bfloat16)
-    lower = (pairs[:, 1:2] == tile_ids[None, :]).astype(jnp.bfloat16)
-    listed = lax.dot_general(
-        upper, lower, (((0,), (0,)), ((), ())), preferred_element_type=jnp.float32
-    )
-    listed = (listed + listed.T > 0.0).astype(jnp.int32)
-    mask = lax.dynamic_slice(listed, (4 * m, 0), (4, TILES)).reshape(-1)
-
-    row_pos = lax.dynamic_index_in_dim(panel_pos.reshape(3, 128, LINE, 128), r, 2, False)
-    row_area = lax.dynamic_index_in_dim(panel_area.reshape(128, LINE, 128), r, 1, False)
-    row_features = features(row_pos.reshape(3, -1), row_area.reshape(-1), True)
-    row_features = row_features.reshape(32, TILES, 256).transpose(1, 2, 0)
-    col_features = features(
-        lax.dynamic_slice(panel_pos, (0, m * COLS), (3, COLS)),
-        lax.dynamic_slice(panel_area, (m * COLS,), (COLS,)),
-        False,
-    )
+    stage, halo = exchange_line(jnp.concatenate([flux_half, own_list], axis=1), edge)
 
     inner = jnp.array([me > 0, me < LINE * PLANE - 1])
     halo = jnp.where(inner[:, None, None], halo, 0.0)
@@ -360,9 +370,23 @@
     once = jnp.where(kept, once, 0.0)
     field_now = relax_rows(once, source, conduct[:, 1:-1])
     surface_top = field_now[:, -1].astype(jnp.bfloat16).transpose(1, 0, 2)
+
+    stage, field_now, surface_top = lax.optimization_barrier((stage, field_now, surface_top))
     table = lax.all_gather(surface_top, "dev", axis=0, tiled=True)
-
-    partial = apply_pairs(mask, rows, row_features, col_features)
+    rows, row_features, col_features = exchange_plane(
+        stage, panel_pos, panel_area.reshape(1, -1)
+    )
+    pairs = rows[:, 256:264, 0:32].reshape(-1, 2)
+    tile_ids = jnp.arange(TILES, dtype=jnp.bfloat16)
+    upper = (pairs[:, 0:1] == tile_ids[None, :]).astype(jnp.bfloat16)
+    lower = (pairs[:, 1:2] == tile_ids[None, :]).astype(jnp.bfloat16)
+    listed = lax.dot_general(
+        upper, lower, (((0,), (0,)), ((), ())), preferred_element_type=jnp.float32
+    )
+    listed = (listed + listed.T > 0.0).astype(jnp.int32)
+    mask = lax.dynamic_slice(listed, (4 * m, 0), (4, TILES)).reshape(-1)
+
+    partial = apply_pairs(mask, rows, row_features.reshape(TILES, 256, 48), col_features)
     flux_out = finish(panel_cell, partial, table, flux_in)
     return (field_now, flux_out)
 

time: 170 us -> 149 us (0.88)
  the two profiles are of different devices: /device:TPU:11 before, /device:TPU:1 now
where the time goes in v3:
time: 149 us
  Pallas kernels  112 us (75%)
  local copies, waits for them, and re-layouts  17.4 us (12%)
  between operations  14.4 us (10%)
  other arithmetic  3.49 us (2%)
    pallas_call x1, Pallas kernels, apply_pairs(): pl.pallas_call(pair_kernel, out_shape=jax.ShapeDtypeStruct((LINE, 32, 102...  58.9 us
    pallas_call x1, Pallas kernels, exchange_plane(): pl.pallas_call(plane_kernel, out_shape=(jax.ShapeDtypeStruct((PLANE, 272,...  20.5 us
    pallas_call x1, Pallas kernels, finish(): pl.pallas_call(finish_kernel, out_shape=jax.ShapeDtypeStruct(flux_in.shap...  19.8 us
    pallas_call x1, Pallas kernels, exchange_line(): pl.pallas_call(line_kernel, out_shape=(jax.ShapeDtypeStruct((272, 128), j...  13.3 us
    unnamed x36, local copies, waits for them, and re-layouts  11.2 us
  transfers between devices with their start and end apart: 1, of which 0 were waited for; matrix products, arithmetic and copies ran while one was open for 2% of the time, Pallas kernels for 53%

profile of v3, /device:TPU:1, one launch (start us, length us, event | category | flops | bytes accessed | tf_op | source)
XLA Modules:
  0.0 148.9 jit_solution(12657751241487847058)
XLA Ops:
  7.2 0.0 all-gather.2.cloned.1.call-start
  7.2 0.7 convert_element_type.22
  7.9 0.1 copy.63
  8.0 0.1 reshape.107
  8.1 0.9 bitcast_bitcast_fusion
  9.1 1.5 %fusion.35 = (f32[32,8,2,128]{3,2,1,0:T(2,128)S(1)}, f32[32,8,2,128]{3,2,1,0:T(2,128)S(1)}) fusion(f32[32,8,4,128]{3,2,1,0:T(4,128)} %param.10), kind=kLoop, calls=%fused_computation.70 | loop fusion | bytes 1048576 | tf_op jit(solution)/shard_map/slice | solution.py:349
  10.5 1.5 fusion.36
  12.0 0.8 fusion.38
  12.8 0.1 broadcast_select_fusion.1
  12.9 0.1 maximum_bitcast_fusion
  13.0 0.1 pad_maximum_fusion.edge_ref
  13.1 13.3 %shard_map.113 = (bf16[272,128]{1,0:T(8,128)(2,1)S(1)}, f32[2,776,128]{2,1,0:T(8,128)S(1)}) custom-call(bf16[8,48,128]{2,1,0:T(8,128)(2,1)S(1)} %pad_maximum_fusion.3.flux_ref, f32[2,776,128]{2,1,0:T(8,128)S(1)} %pad_maximum_fusion.edge_ref), custom_call_target="tpu_custom_call" | custom-call | tf_op jit(solution)/shard_map/pallas_call | solution.py:162
  26.4 0.1 pad_add_fusion
  26.5 0.0 copy-start.9
  26.5 0.1 broadcast_select_fusion
  26.7 0.0 copy-done.12
  26.7 0.0 copy-start.14
  26.7 0.0 copy-start.15
  26.7 0.0 copy-start.13
  26.7 0.3 copy.67
  27.1 0.5 copy-done.9
  27.5 0.3 copy.70
  27.8 0.1 copy.66
  27.9 0.1 copy.68
  28.1 0.0 copy-done.14
  28.1 0.0 copy-done.15
  28.1 0.1 select_reduce_fusion
  28.2 0.0 copy-done.13
  28.2 0.1 maximum_multiply_fusion
  28.3 0.1 pad_maximum_fusion.1
  28.4 0.6 fusion.14
  28.9 0.0 copy-start.1
  29.0 0.0 copy-start.3
  29.0 0.6 fusion.24
  29.6 0.0 copy-start.10
  29.6 0.8 copy-done.10
  30.4 0.6 fusion.30
  31.0 0.0 all-gather.2.cloned.1.call-update
  31.1 0.0 copy-done.1
  31.1 0.0 copy-done.3
  31.1 20.5 %shard_map.114 = (bf16[16,272,128]{2,1,0:T(8,128)(2,1)S(1)}, bf16[128,128,48]{2,1,0:T(8,128)(2,1)S(1)}, bf16[4,48,2048]{2,1,0:T(8,128)(2,1)S(1)}) custom-call(bf16[272,128]{1,0:T(8,128)(2,1)S(1)} %get-tuple-element.13.stage_ref, f32[3,131072]{1,0:T(4,128)S(1)} %copy-done.1, f32[1,131072]{1,0:T(1,128)S(1)} %bitcast.44), custom_call_target="tpu_custom_call" | custom-call | tf_op jit(solution)/shard_map/pallas_call | solution.py:240
  51.6 0.0 copy-start.7
  51.6 2.0 %copy-done.7 = bf16[128,128,48]{2,1,0:T(8,128)(2,1)} copy-done((bf16[128,128,48]{2,1,0:T(8,128)(2,1)}, bf16[128,128,48]{2,1,0:T(8,128)(2,1)S(1)}, u32[]{:S(2)}) %copy-start.7) | copy-done | bytes 1572888
  53.6 0.0 copy-start.11
  53.6 0.0 copy-start.5
  53.6 1.1 copy-done.5
  54.7 0.6 reshape.111
  55.3 0.0 copy-start.6
  55.3 0.5 slice_reduce_fusion.1
  55.9 1.0 fusion
  56.9 0.1 copy.79
  57.0 0.1 reshape.112.mask_ref
  57.1 0.0 copy-done.11
  57.1 1.1 copy.80
  58.2 0.0 copy-done.6
  58.2 2.2 %copy-done.8 = bf16[128,128,48]{2,1,0:T(8,128)(2,1)S(1)} copy-done((bf16[128,128,48]{2,1,0:T(8,128)(2,1)S(1)}, bf16[128,128,48]{2,1,0:T(8,128)(2,1)}, u32[]{:S(2)}) %copy-start.8) | copy-done | bytes 1572888
  60.4 58.9 %shard_map.115.part_ref = bf16[8,32,1024]{2,1,0:T(8,128)(2,1)S(1)} custom-call(s32[256]{0:T(256)S(1)} %reshape.112.mask_ref, bf16[16,272,128]{2,1,0:T(8,128)(2,1)S(1)} %copy-done.6, bf16[64,256,48]{2,1,0:T(8,128)(2,1)S(1)} %bitcast.45, bf16[4,48,2048]{2,1,0:T(8,128)(2,1)S(1)} %get-tuple-element.16.q_ref), custom_call_target="tpu_custom_call" | custom-call | flops 99999997952 | bytes 8388608 | tf_op jit(solution)/shard_map/pallas_call | solution.py:90
  119.4 0.0 all-gather.2.cloned.1.call-done.table_ref
  119.4 0.0 copy-done.2
  119.4 0.0 copy-done.4
  119.4 0.0 copy-start
  119.4 2.2 %copy-done = bf16[512,32,128]{2,1,0:T(8,128)(2,1)S(1)} copy-done((bf16[512,32,128]{2,1,0:T(8,128)(2,1)S(1)}, bf16[512,32,128]{2,1,0:T(8,128)(2,1)}, u32[]{:S(2)}) %copy-start) | copy-done | bytes 4194328
  121.6 19.8 %shard_map.116 = f32[32,1024]{1,0:T(8,128)S(1)} custom-call(s32[1024]{0:T(1024)S(1)} %copy-done.4, bf16[8,32,1024]{2,1,0:T(8,128)(2,1)S(1)} %shard_map.115.part_ref, bf16[512,32,128]{2,1,0:T(8,128)(2,1)S(1)} %copy-done, f32[32,1024]{1,0:T(8,128)S(1)} %copy-done.2), custom_call_target="tpu_custom_call" | custom-call | tf_op jit(solution)/shard_map/pallas_call | solution.py:303
  141.4 0.7 copy.87
  (18 shorter events, 0.2 us)
Async XLA Ops:
  7.2 112.2 %all-gather.2.cloned.1.call-start = ((), (), s32[]{:S(2)}) async-start(), calls=%async_computation | async-start | bytes 4227072 | tf_op jit(solution)/shard_map/all_gather | solution.py:375
  13.1 13.5 %copy-start.12 = (f32[32,8,4,128]{3,2,1,0:T(4,128)S(1)}, f32[32,8,4,128]{3,2,1,0:T(4,128)}, u32[]{:S(2)}) copy-start(f32[32,8,4,128]{3,2,1,0:T(4,128)} %param.10) | copy-start | bytes 1572868
  26.5 1.0 copy-start.9
  26.7 1.4 copy-start.14
  26.7 1.4 copy-start.15
  26.7 1.5 %copy-start.13 = (f32[8,4,128]{2,1,0:T(4,128)S(1)}, f32[8,4,128]{2,1,0:T(4,128)}, u32[]{:S(2)}) copy-start(f32[8,4,128]{2,1,0:T(4,128)} %param.12) | copy-start | bytes 49156
  28.9 2.1 %copy-start.1 = (f32[3,131072]{1,0:T(4,128)S(1)}, f32[3,131072]{1,0:T(4,128)}, u32[]{:S(2)}) copy-start(f32[3,131072]{1,0:T(4,128)} %pos_ref.1) | copy-start | bytes 4718596
  29.0 2.1 %copy-start.3 = (f32[131072]{0:T(1024)S(1)}, f32[131072]{0:T(1024)}, u32[]{:S(2)}) copy-start(f32[131072]{0:T(1024)} %param.17) | copy-start | bytes 1572868
  29.6 0.8 copy-start.10
  51.6 2.0 %copy-start.7 = (bf16[128,128,48]{2,1,0:T(8,128)(2,1)}, bf16[128,128,48]{2,1,0:T(8,128)(2,1)S(1)}, u32[]{:S(2)}) copy-start(bf16[128,128,48]{2,1,0:T(8,128)(2,1)S(1)} %get-tuple-element.15) | copy-start | bytes 4718596
  53.6 3.5 %copy-start.11 = (f32[32,8,4,128]{3,0,2,1:T(8,128)S(1)}, f32[32,8,4,128]{3,0,2,1:T(8,128)}, u32[]{:S(2)}) copy-start(f32[32,8,4,128]{3,0,2,1:T(8,128)} %copy-done.10) | copy-start | bytes 1572868
  53.6 1.1 copy-start.5
  55.3 2.9 %copy-start.6 = (bf16[16,272,128]{2,1,0:T(8,128)(2,1)S(1)}, bf16[16,272,128]{2,1,0:T(8,128)(2,1)}, u32[]{:S(2)}) copy-start(bf16[16,272,128]{2,1,0:T(8,128)(2,1)} %copy-done.5) | copy-start | bytes 3342340
  58.2 2.2 %copy-start.8 = (bf16[128,128,48]{2,1,0:T(8,128)(2,1)S(1)}, bf16[128,128,48]{2,1,0:T(8,128)(2,1)}, u32[]{:S(2)}) copy-start(bf16[128,128,48]{2,1,0:T(8,128)(2,1)} %copy-done.7) | copy-start | bytes 4718596
  60.4 59.0 %copy-start.2 = (f32[32,1024]{1,0:T(8,128)S(1)}, f32[32,1024]{1,0:T(8,128)}, u32[]{:S(2)}) copy-start(f32[32,1024]{1,0:T(8,128)} %flux_ref.1) | copy-start | bytes 393220
  60.4 59.0 %copy-start.4 = (s32[1024]{0:T(1024)S(1)}, s32[1024]{0:T(1024)}, u32[]{:S(2)}) copy-start(s32[1024]{0:T(1024)} %cell_ref.1) | copy-start | bytes 12292
  119.4 2.2 %copy-start = (bf16[512,32,128]{2,1,0:T(8,128)(2,1)S(1)}, bf16[512,32,128]{2,1,0:T(8,128)(2,1)}, u32[]{:S(2)}) copy-start(bf16[512,32,128]{2,1,0:T(8,128)(2,1)} %all-gather.2.cloned.1.call-done.table_ref) | copy-start | bytes 12582916
Sparse Core Ops, SparseCore 0:
  31.2 72.4 all-gather.1

commit v4 on v3

--- a/solution.py
+++ b/solution.py
@@ -125,27 +125,58 @@
 
 
 def line_kernel(
-    flux_ref, edge_ref, stage_ref, halo_ref, shared, line_send, line_recv, edge_send, edge_recv
+    flux_ref,
+    list_ref,
+    field_ref,
+    source_ref,
+    factor_ref,
+    stage_ref,
+    halo_field,
+    halo_source,
+    halo_factor,
+    slices,
+    shared,
+    edge_field,
+    edge_source,
+    edge_factor,
+    line_send,
+    line_recv,
+    edge_send,
+    edge_recv,
 ):
     me = lax.axis_index("dev")
     m, r = me // LINE, lax.rem(me, LINE)
     line = [LINE * m + lax.rem(r + k, LINE) for k in range(1, LINE)]
     after = lax.rem(me + 1, LINE * PLANE)
     before = lax.rem(me + LINE * PLANE - 1, LINE * PLANE)
+    for side, (at, one, device) in enumerate(((2, 3, after), (0, 0, before))):
+        edge_field[side] = field_ref[:, :, at : at + 2, :]
+        edge_source[side] = source_ref[:, :, one, :]
+        edge_factor[side] = factor_ref[:, one, :]
+    own_list = pltpu.roll(list_ref[...], 2 * r, axis=1).astype(jnp.bfloat16)
+    for s in range(LINE):
+        slices[s, 0:32, :] = flux_ref[:, s * 128 : (s + 1) * 128].astype(jnp.bfloat16)
+        slices[s, 32:48, :] = own_list
     greet(line + [after, before])
-    edges = [
-        remote(edge_ref.at[0], halo_ref.at[0], edge_send, edge_recv, 0, after),
-        remote(edge_ref.at[1], halo_ref.at[1], edge_send, edge_recv, 1, before),
-    ]
+    edges = []
+    for side, device in enumerate((after, before)):
+        for which, (src, dst) in enumerate(
+            ((edge_field, halo_field), (edge_source, halo_source), (edge_factor, halo_factor))
+        ):
+            edges.append(
+                remote(
+                    src.at[side], dst.at[side], edge_send, edge_recv, 3 * side + which, device
+                )
+            )
     copies = []
     for k in range(1, LINE):
         there = lax.rem(r + k, LINE)
         copies.append(
-            remote(flux_ref.at[there], shared.at[r], line_send, line_recv, k - 1, line[k - 1])
+            remote(slices.at[there], shared.at[r], line_send, line_recv, k - 1, line[k - 1])
         )
     for copy in edges + copies:
         copy.start()
-    shared[r] = flux_ref[r]
+    shared[r] = slices[r]
     for copy in copies:
         copy.wait()
     lists = jnp.zeros((16, 128), jnp.float32)
@@ -157,27 +188,34 @@
         copy.wait()
 
 
-def exchange_line(flux, edge):
+def exchange_line(flux, lists, field, source, factor):
     vmem = pl.BlockSpec(memory_space=pltpu.VMEM)
+    f32 = jnp.float32
     return pl.pallas_call(
         line_kernel,
         out_shape=(
             jax.ShapeDtypeStruct((272, 128), jnp.bfloat16),
-            jax.ShapeDtypeStruct(edge.shape, jnp.float32),
-        ),
-        in_specs=[vmem, vmem],
-        out_specs=(vmem, vmem),
+            jax.ShapeDtypeStruct((2, 32, LAYERS, 2, 128), f32),
+            jax.ShapeDtypeStruct((2, 32, LAYERS, 128), f32),
+            jax.ShapeDtypeStruct((2, LAYERS, 128), f32),
+        ),
+        in_specs=[vmem] * 5,
+        out_specs=(vmem,) * 4,
         scratch_shapes=[
             pltpu.VMEM((LINE, 48, 128), jnp.bfloat16),
+            pltpu.VMEM((LINE, 48, 128), jnp.bfloat16),
+            pltpu.VMEM((2, 32, LAYERS, 2, 128), f32),
+            pltpu.VMEM((2, 32, LAYERS, 128), f32),
+            pltpu.VMEM((2, LAYERS, 128), f32),
             pltpu.SemaphoreType.DMA((LINE - 1,)),
             pltpu.SemaphoreType.DMA((LINE - 1,)),
-            pltpu.SemaphoreType.DMA((2,)),
-            pltpu.SemaphoreType.DMA((2,)),
+            pltpu.SemaphoreType.DMA((6,)),
+            pltpu.SemaphoreType.DMA((6,)),
         ],
         compiler_params=pltpu.CompilerParams(
             collective_id=0, has_side_effects=True, vmem_limit_bytes=16 << 20
         ),
-    )(flux, edge)
+    )(flux, lists, field, source, factor)
 
 
 def split3(value):
@@ -204,7 +242,17 @@
 
 
 def plane_kernel(
-    stage_ref, pos_ref, area_ref, rows_ref, pt_ref, q_ref, plane_send, plane_recv
+    stage_ref,
+    pos_ref,
+    area_ref,
+    rows_ref,
+    pt_ref,
+    q_ref,
+    pt_held,
+    q_held,
+    plane_send,
+    plane_recv,
+    local,
 ):
     me = lax.axis_index("dev")
     m, r = me // LINE, lax.rem(me, LINE)
@@ -215,40 +263,51 @@
         copies.append(
             remote(stage_ref, rows_ref.at[m], plane_send, plane_recv, k - 1, plane[k - 1])
         )
+    copies.append(pltpu.make_async_copy(stage_ref, rows_ref.at[m], local.at[0]))
     for copy in copies:
         copy.start()
-    rows_ref[m] = stage_ref[...]
-
-    def row_block(half, carry):
-        at = pl.multiple_of(half * 1024 + r * 128, 128)
-        part = factors(pos_ref[:, pl.ds(at, 128)], area_ref[:, pl.ds(at, 128)], True)
-        pt_ref[half] = part.T.astype(jnp.bfloat16)
+
+    def row_block(step, carry):
+        for u in range(8):
+            half = step * 8 + u
+            at = pl.multiple_of(half * 1024 + r * 128, 128)
+            part = factors(pos_ref[:, pl.ds(at, 128)], area_ref[:, pl.ds(at, 128)], True)
+            pt_held[half] = part.T.astype(jnp.bfloat16)
         return carry
 
-    lax.fori_loop(0, 2 * TILES, row_block, 0)
+    lax.fori_loop(0, TILES // 4, row_block, 0)
+    moves = [pltpu.make_async_copy(pt_held, pt_ref, local.at[1])]
+    moves[0].start()
     for j in range(4):
         for c in range(4):
             at = pl.multiple_of(m * COLS + j * TILE + c * 512, 512)
             part = factors(pos_ref[:, pl.ds(at, 512)], area_ref[:, pl.ds(at, 512)], False)
-            q_ref[j, :, c * 512 : (c + 1) * 512] = part.astype(jnp.bfloat16)
-    for copy in copies:
+            q_held[j, :, c * 512 : (c + 1) * 512] = part.astype(jnp.bfloat16)
+    moves.append(pltpu.make_async_copy(q_held, q_ref, local.at[2]))
+    moves[1].start()
+    for copy in copies + moves:
         copy.wait()
 
 
 def exchange_plane(stage, pos, area):
     vmem = pl.BlockSpec(memory_space=pltpu.VMEM)
+    hbm = pl.BlockSpec(memory_space=pltpu.HBM)
+    row_shape, col_shape = (2 * TILES, 128, 48), (4, 48, TILE)
     return pl.pallas_call(
         plane_kernel,
         out_shape=(
             jax.ShapeDtypeStruct((PLANE, 272, 128), jnp.bfloat16),
-            jax.ShapeDtypeStruct((2 * TILES, 128, 48), jnp.bfloat16),
-            jax.ShapeDtypeStruct((4, 48, TILE), jnp.bfloat16),
+            jax.ShapeDtypeStruct(row_shape, jnp.bfloat16),
+            jax.ShapeDtypeStruct(col_shape, jnp.bfloat16),
         ),
         in_specs=[vmem, vmem, vmem],
-        out_specs=(vmem, vmem, vmem),
+        out_specs=(hbm, hbm, hbm),
         scratch_shapes=[
+            pltpu.VMEM(row_shape, jnp.bfloat16),
+            pltpu.VMEM(col_shape, jnp.bfloat16),
             pltpu.SemaphoreType.DMA((PLANE - 1,)),
             pltpu.SemaphoreType.DMA((PLANE - 1,)),
+            pltpu.SemaphoreType.DMA((3,)),
         ],
         compiler_params=pltpu.CompilerParams(
             collective_id=2, has_side_effects=True, vmem_limit_bytes=24 << 20
@@ -276,15 +335,15 @@
 
     def group(g, carry):
         def pick(step, held):
-            for u in range(8):
-                at = step * 8 + u
+            for u in range(16):
+                at = step * 16 + u
                 cell = cell_ref[g * 128 + at]
-                block = table[cell // 128].astype(jnp.float32)
-                moved = pltpu.roll(block, lax.rem(at + 128 - lax.rem(cell, 128), 128), axis=1)
+                block = table[lax.shift_right_logical(cell, 7)].astype(jnp.float32)
+                moved = pltpu.roll(block, (at - cell) & 127, axis=1)
                 held = jnp.where(lane == at, moved, held)
             return held
 
-        traces[g] = lax.fori_loop(0, 16, pick, jnp.zeros((32, 128), jnp.float32))
+        traces[g] = lax.fori_loop(0, 8, pick, jnp.zeros((32, 128), jnp.float32))
         return carry
 
     lax.fori_loop(0, 8, group, 0)
@@ -306,7 +365,7 @@
         in_specs=[
             pl.BlockSpec(memory_space=pltpu.SMEM),
             vmem,
-            pl.BlockSpec(memory_space=pl.ANY),
+            pl.BlockSpec(memory_space=pltpu.HBM),
             vmem,
         ],
         out_specs=vmem,
@@ -339,27 +398,15 @@
     me = lax.axis_index("dev")
     m, r = me // LINE, me % LINE
 
-    flux_half = flux_in.astype(jnp.bfloat16).reshape(32, LINE, 128).transpose(1, 0, 2)
-    own_list = jnp.pad(pair_list.astype(jnp.bfloat16).reshape(1, 32), ((0, 0), (0, 96)))
-    in_row = jnp.arange(16, dtype=jnp.int32)[:, None] == r
-    own_list = jnp.where(in_row, own_list, jnp.zeros_like(own_list))
-    own_list = jnp.broadcast_to(own_list, (LINE, 16, 128))
-    edge = [
-        [
-            field_in[:, :, at : at + 2].reshape(-1, 128),
-            source[:, :, one].reshape(-1, 128),
-            cell_factor[:, one].reshape(-1, 128),
-        ]
-        for at, one in ((2, 3), (0, 0))
-    ]
-    edge = jnp.stack([jnp.concatenate(side, axis=0) for side in edge], axis=0)
-    stage, halo = exchange_line(jnp.concatenate([flux_half, own_list], axis=1), edge)
+    lists = jnp.pad(pair_list.astype(jnp.float32), ((0, 0), (0, 126)))
+    stage, halo_field, halo_source, halo_factor = exchange_line(
+        flux_in, lists, field_in, source, cell_factor
+    )
 
     inner = jnp.array([me > 0, me < LINE * PLANE - 1])
-    halo = jnp.where(inner[:, None, None], halo, 0.0)
-    halo_field = halo[:, 0:512].reshape(2, 32, LAYERS, 2, 128)
-    halo_source = halo[:, 512:768].reshape(2, 32, LAYERS, 1, 128)
-    halo_factor = halo[:, 768:776].reshape(2, LAYERS, 1, 128)
+    halo_field = jnp.where(inner.reshape(2, 1, 1, 1, 1), halo_field, 0.0)
+    halo_source = halo_source[:, :, :, None]
+    halo_factor = halo_factor[:, :, None]
     wide_field = jnp.concatenate([halo_field[0], field_in, halo_field[1]], axis=2)
     wide_source = jnp.concatenate([halo_source[0], source, halo_source[1]], axis=2)
     wide_factor = jnp.concatenate([halo_factor[0], cell_factor, halo_factor[1]], axis=1)
@@ -371,12 +418,12 @@
     field_now = relax_rows(once, source, conduct[:, 1:-1])
     surface_top = field_now[:, -1].astype(jnp.bfloat16).transpose(1, 0, 2)
 
-    stage, field_now, surface_top = lax.optimization_barrier((stage, field_now, surface_top))
+    stage, surface_top = lax.optimization_barrier((stage, surface_top))
     table = lax.all_gather(surface_top, "dev", axis=0, tiled=True)
     rows, row_features, col_features = exchange_plane(
         stage, panel_pos, panel_area.reshape(1, -1)
     )
-    pairs = rows[:, 256:264, 0:32].reshape(-1, 2)
+    pairs = rows[:, 256:272, 0:16].reshape(-1, 2)
     tile_ids = jnp.arange(TILES, dtype=jnp.bfloat16)
     upper = (pairs[:, 0:1] == tile_ids[None, :]).astype(jnp.bfloat16)
     lower = (pairs[:, 1:2] == tile_ids[None, :]).astype(jnp.bfloat16)

time: 149 us -> 141 us (0.946)
  the two profiles are of different devices: /device:TPU:1 before, /device:TPU:23 now
where the time goes in v4:
time: 141 us
  Pallas kernels  106 us (75%)
  local copies, waits for them, and re-layouts  16.8 us (12%)
  between operations  14.4 us (10%)
  other arithmetic  2.57 us (2%)
    pallas_call x1, Pallas kernels, apply_pairs(): pl.pallas_call(pair_kernel, out_shape=jax.ShapeDtypeStruct((LINE, 32, 102...  62.9 us
    pallas_call x1, Pallas kernels, exchange_plane(): pl.pallas_call(plane_kernel, out_shape=(jax.ShapeDtypeStruct((PLANE, 272,...  19.2 us
    unnamed x38, local copies, waits for them, and re-layouts  14.7 us
    pallas_call x1, Pallas kernels, exchange_line(): pl.pallas_call(line_kernel, out_shape=(jax.ShapeDtypeStruct((272, 128), j...  12.6 us
    pallas_call x1, Pallas kernels, finish(): pl.pallas_call(finish_kernel, out_shape=jax.ShapeDtypeStruct(flux_in.shap...  11.5 us
  transfers between devices with their start and end apart: 1, of which 0 were waited for; matrix products, arithmetic and copies ran while one was open for 3% of the time, Pallas kernels for 58%

profile of v4, /device:TPU:23, one launch (start us, length us, event | category | flops | bytes accessed | tf_op | source)
XLA Modules:
  0.0 141.1 jit_solution(864537311546383618)
XLA Ops:
  7.2 0.0 copy-start.2
  7.2 0.0 copy-start
  7.2 0.0 copy-start.6
  7.2 0.0 copy-start.4
  7.2 0.0 all-gather.2.cloned.1.call-start
  7.3 0.8 convert_element_type.18
  8.0 0.1 copy.70
  8.1 1.3 copy.72
  9.5 1.4 copy.75
  10.8 0.1 pad_add_fusion
  10.9 0.0 copy-done.2
  10.9 0.0 copy-done
  10.9 0.0 copy-done.6
  10.9 0.0 copy-done.4
  10.9 12.6 %shard_map.113 = (bf16[272,128]{1,0:T(8,128)(2,1)S(1)}, f32[2,32,8,2,128]{4,3,2,1,0:T(2,128)S(1)}, f32[2,32,8,128]{3,2,1,0:T(8,128)S(1)}, f32[2,8,128]{2,1,0:T(8,128)S(1)}) custom-call(f32[32,1024]{1,0:T(8,128)S(1)} %copy-done.4, f32[16,128]{1,0:T(8,128)S(1)} %pad.12.list_ref, f32[32,8,4,128]{3,2,1,0:T(4,128)S(1)} %copy-done.2, ...), custom_call_target="tpu_custom_call" | custom-call | tf_op jit(solution)/shard_map/pallas_call | solution.py:194
  23.6 0.0 copy-start.15
  23.6 0.0 copy-start.16
  23.6 0.3 broadcast_select_fusion
  24.0 0.1 copy.71
  24.1 0.1 copy.73
  24.3 0.0 copy-done.15
  24.3 0.0 copy-done.16
  24.3 0.1 select_reduce_fusion
  24.4 0.1 maximum_multiply_fusion
  24.5 0.1 pad_maximum_fusion
  24.5 0.6 fusion.14
  25.2 0.0 copy-start.3
  25.2 0.0 copy-start.5
  25.2 0.6 fusion.24
  25.8 0.0 copy-start.14
  25.8 0.8 copy-done.14
  26.6 0.6 fusion.30
  27.2 0.0 all-gather.2.cloned.1.call-update
  27.2 2.2 %copy.85 = f32[32,8,4,128]{3,2,1,0:T(4,128)} copy(f32[32,8,4,128]{3,0,2,1:T(8,128)} %copy-done.14) | data formatting | bytes 1048576
  29.4 0.0 copy-done.3
  29.4 0.0 copy-done.5
  29.4 19.2 %shard_map.114 = (bf16[16,272,128]{2,1,0:T(8,128)(2,1)S(1)}, bf16[128,128,48]{2,1,0:T(8,128)(2,1)S(1)}, bf16[4,48,2048]{2,1,0:T(8,128)(2,1)S(1)}) custom-call(bf16[272,128]{1,0:T(8,128)(2,1)S(1)} %get-tuple-element.15.stage_ref, f32[3,131072]{1,0:T(4,128)S(1)} %copy-done.3, f32[1,131072]{1,0:T(1,128)S(1)} %bitcast.23), custom_call_target="tpu_custom_call" | custom-call | tf_op jit(solution)/shard_map/pallas_call | solution.py:296
  48.6 0.0 copy-start.10
  48.6 2.0 %copy-done.10 = bf16[128,128,48]{2,1,0:T(8,128)(2,1)} copy-done((bf16[128,128,48]{2,1,0:T(8,128)(2,1)}, bf16[128,128,48]{2,1,0:T(8,128)(2,1)S(1)}, u32[]{:S(2)}) %copy-start.10) | copy-done | bytes 1572888
  50.6 0.0 copy-start.12
  50.6 0.9 copy-done.12
  51.5 0.0 copy-start.13
  51.5 0.0 copy-start.8
  51.5 1.1 copy-done.8
  52.6 0.4 reshape.84
  52.9 0.0 copy-start.9
  52.9 0.5 slice_reduce_fusion.1
  53.5 1.0 fusion
  54.5 0.1 copy.84
  54.6 0.1 reshape.85.mask_ref
  54.7 0.0 copy-done.13
  54.7 0.0 copy-done.9
  54.7 0.0 copy-start.11
  54.7 2.2 %copy-done.11 = bf16[128,128,48]{2,1,0:T(8,128)(2,1)S(1)} copy-done((bf16[128,128,48]{2,1,0:T(8,128)(2,1)S(1)}, bf16[128,128,48]{2,1,0:T(8,128)(2,1)}, u32[]{:S(2)}) %copy-start.11) | copy-done | bytes 1572888
  56.9 0.0 copy-start.7
  56.9 62.9 %shard_map.115.part_ref = bf16[8,32,1024]{2,1,0:T(8,128)(2,1)S(1)} custom-call(s32[256]{0:T(256)S(1)} %reshape.85.mask_ref, bf16[16,272,128]{2,1,0:T(8,128)(2,1)S(1)} %copy-done.9, bf16[64,256,48]{2,1,0:T(8,128)(2,1)S(1)} %bitcast.24, bf16[4,48,2048]{2,1,0:T(8,128)(2,1)S(1)} %copy-done.13), custom_call_target="tpu_custom_call" | custom-call | flops 99999997952 | bytes 8388608 | tf_op jit(solution)/shard_map/pallas_call | solution.py:90
  119.8 0.0 all-gather.2.cloned.1.call-done.table_ref
  119.9 0.0 copy-done.7
  119.9 0.0 copy-start.1
  119.9 2.2 %copy-done.1 = bf16[512,32,128]{2,1,0:T(8,128)(2,1)S(1)} copy-done((bf16[512,32,128]{2,1,0:T(8,128)(2,1)S(1)}, bf16[512,32,128]{2,1,0:T(8,128)(2,1)}, u32[]{:S(2)}) %copy-start.1) | copy-done | bytes 4194328
  122.1 11.5 %shard_map.116 = f32[32,1024]{1,0:T(8,128)S(1)} custom-call(s32[1024]{0:T(1024)S(1)} %copy-done.7, bf16[8,32,1024]{2,1,0:T(8,128)(2,1)S(1)} %shard_map.115.part_ref, bf16[512,32,128]{2,1,0:T(8,128)(2,1)S(1)} %copy-done.1, f32[32,1024]{1,0:T(8,128)S(1)} %copy-done.4), custom_call_target="tpu_custom_call" | custom-call | tf_op jit(solution)/shard_map/pallas_call | solution.py:362
  133.6 0.7 copy.88
  (11 shorter events, 0.2 us)
Async XLA Ops:
  7.2 3.8 %copy-start.2 = (f32[32,8,4,128]{3,2,1,0:T(4,128)S(1)}, f32[32,8,4,128]{3,2,1,0:T(4,128)}, u32[]{:S(2)}) copy-start(f32[32,8,4,128]{3,2,1,0:T(4,128)} %field_ref.1) | copy-start | bytes 1572868
  7.2 3.7 %copy-start = (f32[32,8,4,128]{3,2,1,0:T(4,128)S(1)}, f32[32,8,4,128]{3,2,1,0:T(4,128)}, u32[]{:S(2)}) copy-start(f32[32,8,4,128]{3,2,1,0:T(4,128)} %source_ref.1) | copy-start | bytes 1572868
  7.2 3.7 %copy-start.6 = (f32[8,4,128]{2,1,0:T(4,128)S(1)}, f32[8,4,128]{2,1,0:T(4,128)}, u32[]{:S(2)}) copy-start(f32[8,4,128]{2,1,0:T(4,128)} %factor_ref.1) | copy-start | bytes 49156
  7.2 3.7 %copy-start.4 = (f32[32,1024]{1,0:T(8,128)S(1)}, f32[32,1024]{1,0:T(8,128)}, u32[]{:S(2)}) copy-start(f32[32,1024]{1,0:T(8,128)} %flux_ref.3) | copy-start | bytes 393220
  7.2 112.7 %all-gather.2.cloned.1.call-start = ((), (), s32[]{:S(2)}) async-start(), calls=%async_computation | async-start | bytes 4227072 | tf_op jit(solution)/shard_map/all_gather | solution.py:422
  23.6 0.7 copy-start.15
  23.6 0.7 copy-start.16
  25.2 4.3 %copy-start.3 = (f32[3,131072]{1,0:T(4,128)S(1)}, f32[3,131072]{1,0:T(4,128)}, u32[]{:S(2)}) copy-start(f32[3,131072]{1,0:T(4,128)} %pos_ref.1) | copy-start | bytes 4718596
  25.2 4.2 %copy-start.5 = (f32[131072]{0:T(1024)S(1)}, f32[131072]{0:T(1024)}, u32[]{:S(2)}) copy-start(f32[131072]{0:T(1024)} %param.17) | copy-start | bytes 1572868
  25.8 0.8 copy-start.14
  48.6 2.0 %copy-start.10 = (bf16[128,128,48]{2,1,0:T(8,128)(2,1)}, bf16[128,128,48]{2,1,0:T(8,128)(2,1)S(1)}, u32[]{:S(2)}) copy-start(bf16[128,128,48]{2,1,0:T(8,128)(2,1)S(1)} %get-tuple-element.17) | copy-start | bytes 4718596
  50.6 0.9 copy-start.12
  51.5 3.2 %copy-start.13 = (bf16[4,48,2048]{2,1,0:T(8,128)(2,1)S(1)}, bf16[4,48,2048]{2,1,0:T(8,128)(2,1)}, u32[]{:S(2)}) copy-start(bf16[4,48,2048]{2,1,0:T(8,128)(2,1)} %copy-done.12) | copy-start | bytes 2359300
  51.5 1.1 copy-start.8
  52.9 1.8 %copy-start.9 = (bf16[16,272,128]{2,1,0:T(8,128)(2,1)S(1)}, bf16[16,272,128]{2,1,0:T(8,128)(2,1)}, u32[]{:S(2)}) copy-start(bf16[16,272,128]{2,1,0:T(8,128)(2,1)} %copy-done.8) | copy-start | bytes 3342340
  54.7 2.2 %copy-start.11 = (bf16[128,128,48]{2,1,0:T(8,128)(2,1)S(1)}, bf16[128,128,48]{2,1,0:T(8,128)(2,1)}, u32[]{:S(2)}) copy-start(bf16[128,128,48]{2,1,0:T(8,128)(2,1)} %copy-done.10) | copy-start | bytes 4718596
  56.9 63.0 %copy-start.7 = (s32[1024]{0:T(1024)S(1)}, s32[1024]{0:T(1024)}, u32[]{:S(2)}) copy-start(s32[1024]{0:T(1024)} %cell_ref.1) | copy-start | bytes 12292
  119.9 2.2 %copy-start.1 = (bf16[512,32,128]{2,1,0:T(8,128)(2,1)S(1)}, bf16[512,32,128]{2,1,0:T(8,128)(2,1)}, u32[]{:S(2)}) copy-start(bf16[512,32,128]{2,1,0:T(8,128)(2,1)} %all-gather.2.cloned.1.call-done.table_ref) | copy-start | bytes 12582916
Sparse Core Ops, SparseCore 0:
  27.3 71.6 all-gather.1

commit v5 on v4

--- a/solution.py
+++ b/solution.py
@@ -11,6 +11,7 @@
 TILES = 64
 LAYERS = 8
 UNROLL = 4
+WIDE = (63 << 20) + (1 << 19)
 LINE = 8
 PLANE = 16
 COLS = 4 * TILE
@@ -29,20 +30,82 @@
     return layer_scale[:, None, None] * cell_factor
 
 
-def relax_rows(widened, source, conduct):
-    centre = widened[:, :, 1:-1, :]
-    padded = jnp.pad(centre, ((0, 0), (1, 1), (0, 0), (1, 1)))
-    beside = (
-        padded[:, 2:, :, 1:-1]
-        + padded[:, :-2, :, 1:-1]
-        + (widened[:, :, 2:, :] + widened[:, :, :-2, :])
-        + (padded[:, 1:-1, :, 2:] + padded[:, 1:-1, :, :-2])
+def sweep_kernel(
+    field_ref, source_ref, conduct_ref, halo_field, halo_source, halo_conduct, out_ref, top_ref, tops
+):
+    me = lax.axis_index("dev")
+    row = lax.broadcasted_iota(jnp.int32, (LAYERS, 8, 128), 1)
+    lane = lax.broadcasted_iota(jnp.int32, (LAYERS, 8, 128), 2)
+    real = ((row >= 2) | (me > 0)) & ((row < 6) | (me < LINE * PLANE - 1))
+    pad = jnp.zeros((LAYERS, 1, 128), jnp.float32)
+    conduct = jnp.concatenate(
+        [pad, halo_conduct[0][:, None], conduct_ref[...], halo_conduct[1][:, None], pad], axis=1
     )
-    applied = conduct * (6.0 * centre - beside) + centre
-    return centre + relax_rate * (source - applied) / (6.0 * conduct + 1.0)
-
-
-def pair_kernel(mask_ref, f_ref, pt_ref, q_ref, o_ref, total_ref, held_ref, order_ref):
+    step = relax_rate / (6.0 * conduct + 1.0)
+    layer = jnp.zeros((1, 8, 128), jnp.float32)
+
+    def relax(field, source):
+        above = jnp.concatenate([field[1:], layer], axis=0)
+        below = jnp.concatenate([layer, field[:-1]], axis=0)
+        flat = field.reshape(LAYERS * 8, 128)
+        right = jnp.where(lane < 127, pltpu.roll(flat, 127, axis=1).reshape(field.shape), 0.0)
+        left = jnp.where(lane > 0, pltpu.roll(flat, 1, axis=1).reshape(field.shape), 0.0)
+        ahead = pltpu.roll(field, 7, axis=1)
+        behind = pltpu.roll(field, 1, axis=1)
+        beside = (above + below) + (ahead + behind) + (right + left)
+        applied = conduct * (6.0 * field - beside) + field
+        return field + step * (source - applied)
+
+    def one_load(load, carry):
+        field = jnp.concatenate(
+            [halo_field[0, load], field_ref[load], halo_field[1, load]], axis=1
+        )
+        field = jnp.where(real, field, 0.0)
+        source = jnp.concatenate(
+            [
+                pad,
+                halo_source[0, load][:, None],
+                source_ref[load],
+                halo_source[1, load][:, None],
+                pad,
+            ],
+            axis=1,
+        )
+        field = jnp.where(real, relax(field, source), 0.0)
+        field = relax(field, source)
+        out_ref[load] = field[:, 2:6]
+        tops[load] = field[LAYERS - 1, 2:6]
+        return carry
+
+    lax.fori_loop(0, 32, one_load, 0, unroll=2)
+    for x in range(4):
+        top_ref[x] = tops[:, x, :].astype(jnp.bfloat16)
+
+
+def sweeps(*args):
+    vmem = pl.BlockSpec(memory_space=pltpu.VMEM)
+    return pl.pallas_call(
+        sweep_kernel,
+        out_shape=(
+            jax.ShapeDtypeStruct((32, LAYERS, 4, 128), jnp.float32),
+            jax.ShapeDtypeStruct((4, 32, 128), jnp.bfloat16),
+        ),
+        in_specs=[vmem] * len(args),
+        out_specs=(vmem, vmem),
+        scratch_shapes=[pltpu.VMEM((32, 4, 128), jnp.float32)],
+        compiler_params=pltpu.CompilerParams(vmem_limit_bytes=16 << 20),
+    )(*args)
+
+
+def pair_kernel(
+    mask_ref, f_far, pt_far, q_far, o_ref, f_ref, pt_ref, q_ref, total_ref, held_ref, order_ref, sems
+):
+    loads = [
+        pltpu.make_async_copy(far, near, sems.at[at])
+        for at, (far, near) in enumerate(((f_far, f_ref), (pt_far, pt_ref), (q_far, q_ref)))
+    ]
+    for load in loads:
+        load.start()
     order_ref[0] = 0
 
     def note(at, count):
@@ -54,6 +117,8 @@
         order_ref[count + 1 + u] = 0
     total_ref[...] = jnp.zeros(total_ref.shape, jnp.float32)
     held_ref[1] = jnp.zeros((256, TILE), jnp.bfloat16)
+    for load in loads:
+        load.wait()
 
     def step(b, carry):
         for u in range(UNROLL):
@@ -86,18 +151,22 @@
 
 
 def apply_pairs(mask, flux_rows, row_features, col_features):
-    vmem = pl.BlockSpec(memory_space=pltpu.VMEM)
+    hbm = pl.BlockSpec(memory_space=pltpu.HBM)
     return pl.pallas_call(
         pair_kernel,
         out_shape=jax.ShapeDtypeStruct((LINE, 32, 1024), jnp.bfloat16),
-        in_specs=[pl.BlockSpec(memory_space=pltpu.SMEM), vmem, vmem, vmem],
-        out_specs=vmem,
+        in_specs=[pl.BlockSpec(memory_space=pltpu.SMEM), hbm, hbm, hbm],
+        out_specs=pl.BlockSpec(memory_space=pltpu.VMEM),
         scratch_shapes=[
+            pltpu.VMEM(flux_rows.shape, jnp.bfloat16),
+            pltpu.VMEM(row_features.shape, jnp.bfloat16),
+            pltpu.VMEM(col_features.shape, jnp.bfloat16),
             pltpu.VMEM((4, 32, TILE), jnp.float32),
             pltpu.VMEM((2, 256, TILE), jnp.bfloat16),
             pltpu.SMEM((4 * TILES + UNROLL + 2,), jnp.int32),
+            pltpu.SemaphoreType.DMA((3,)),
         ],
-        compiler_params=pltpu.CompilerParams(vmem_limit_bytes=20 << 20),
+        compiler_params=pltpu.CompilerParams(vmem_limit_bytes=WIDE),
         cost_estimate=pl.CostEstimate(
             flops=100_000_000_000, bytes_accessed=8 << 20, transcendentals=0
         ),
@@ -243,11 +312,13 @@
 
 def plane_kernel(
     stage_ref,
-    pos_ref,
-    area_ref,
+    pos_far,
+    area_far,
     rows_ref,
     pt_ref,
     q_ref,
+    pos_ref,
+    area_ref,
     pt_held,
     q_held,
     plane_send,
@@ -256,17 +327,11 @@
 ):
     me = lax.axis_index("dev")
     m, r = me // LINE, lax.rem(me, LINE)
-    plane = [LINE * lax.rem(m + k, PLANE) + r for k in range(1, PLANE)]
-    greet(plane)
-    copies = []
-    for k in range(1, PLANE):
-        copies.append(
-            remote(stage_ref, rows_ref.at[m], plane_send, plane_recv, k - 1, plane[k - 1])
-        )
-    copies.append(pltpu.make_async_copy(stage_ref, rows_ref.at[m], local.at[0]))
-    for copy in copies:
-        copy.start()
-
+    y, x = m // 4, lax.rem(m, 4)
+    loads = [
+        pltpu.make_async_copy(pos_far, pos_ref, local.at[3]),
+        pltpu.make_async_copy(area_far, area_ref, local.at[4]),
+    ]
     def row_block(step, carry):
         for u in range(8):
             half = step * 8 + u
@@ -275,7 +340,40 @@
             pt_held[half] = part.T.astype(jnp.bfloat16)
         return carry
 
-    lax.fori_loop(0, TILES // 4, row_block, 0)
+    along_x = [LINE * (4 * y + lax.rem(x + k, 4)) + r for k in range(1, 4)]
+    along_y = [LINE * (4 * lax.rem(y + k, 4) + x) + r for k in range(1, 4)]
+    own = pltpu.make_async_copy(stage_ref, rows_ref.at[y, x], local.at[0])
+    for copy in loads + [own]:
+        copy.start()
+    greet(along_x + along_y)
+    one, two = slice(0, 128), slice(128, 272)
+    near, far = [], []
+    for k in range(3):
+        near.append(
+            remote(
+                stage_ref.at[one], rows_ref.at[y, x, one], plane_send, plane_recv, k, along_x[k]
+            )
+        )
+        near.append(
+            remote(
+                stage_ref.at[two], rows_ref.at[y, x, two], plane_send, plane_recv, 3 + k, along_y[k]
+            )
+        )
+        part = rows_ref.at[y, :, one]
+        far.append(remote(part, part, plane_send, plane_recv, 6 + k, along_y[k]))
+        part = rows_ref.at[:, x, two]
+        far.append(remote(part, part, plane_send, plane_recv, 9 + k, along_x[k]))
+    for copy in near:
+        copy.start()
+    for load in loads:
+        load.wait()
+    lax.fori_loop(0, 6, row_block, 0)
+    own.wait()
+    for copy in near:
+        copy.wait()
+    for copy in far:
+        copy.start()
+    lax.fori_loop(6, TILES // 4, row_block, 0)
     moves = [pltpu.make_async_copy(pt_held, pt_ref, local.at[1])]
     moves[0].start()
     for j in range(4):
@@ -285,7 +383,7 @@
             q_held[j, :, c * 512 : (c + 1) * 512] = part.astype(jnp.bfloat16)
     moves.append(pltpu.make_async_copy(q_held, q_ref, local.at[2]))
     moves[1].start()
-    for copy in copies + moves:
+    for copy in far + moves:
         copy.wait()
 
 
@@ -296,21 +394,23 @@
     return pl.pallas_call(
         plane_kernel,
         out_shape=(
-            jax.ShapeDtypeStruct((PLANE, 272, 128), jnp.bfloat16),
+            jax.ShapeDtypeStruct((4, 4, 272, 128), jnp.bfloat16),
             jax.ShapeDtypeStruct(row_shape, jnp.bfloat16),
             jax.ShapeDtypeStruct(col_shape, jnp.bfloat16),
         ),
-        in_specs=[vmem, vmem, vmem],
+        in_specs=[vmem, hbm, hbm],
         out_specs=(hbm, hbm, hbm),
         scratch_shapes=[
+            pltpu.VMEM(pos.shape, jnp.float32),
+            pltpu.VMEM(area.shape, jnp.float32),
             pltpu.VMEM(row_shape, jnp.bfloat16),
             pltpu.VMEM(col_shape, jnp.bfloat16),
-            pltpu.SemaphoreType.DMA((PLANE - 1,)),
-            pltpu.SemaphoreType.DMA((PLANE - 1,)),
-            pltpu.SemaphoreType.DMA((3,)),
+            pltpu.SemaphoreType.DMA((12,)),
+            pltpu.SemaphoreType.DMA((12,)),
+            pltpu.SemaphoreType.DMA((5,)),
         ],
         compiler_params=pltpu.CompilerParams(
-            collective_id=2, has_side_effects=True, vmem_limit_bytes=24 << 20
+            collective_id=2, has_side_effects=True, vmem_limit_bytes=WIDE
         ),
     )(stage, pos, area)
 
@@ -378,7 +478,7 @@
             pltpu.SemaphoreType.DMA((LINE - 1,)),
         ],
         compiler_params=pltpu.CompilerParams(
-            collective_id=1, has_side_effects=True, vmem_limit_bytes=16 << 20
+            collective_id=1, has_side_effects=True, vmem_limit_bytes=WIDE
         ),
     )(cells, partial, table, flux_in)
 
@@ -396,33 +496,18 @@
     pair_list,
 ):
     me = lax.axis_index("dev")
-    m, r = me // LINE, me % LINE
+    m = me // LINE
 
     lists = jnp.pad(pair_list.astype(jnp.float32), ((0, 0), (0, 126)))
-    stage, halo_field, halo_source, halo_factor = exchange_line(
-        flux_in, lists, field_in, source, cell_factor
-    )
-
-    inner = jnp.array([me > 0, me < LINE * PLANE - 1])
-    halo_field = jnp.where(inner.reshape(2, 1, 1, 1, 1), halo_field, 0.0)
-    halo_source = halo_source[:, :, :, None]
-    halo_factor = halo_factor[:, :, None]
-    wide_field = jnp.concatenate([halo_field[0], field_in, halo_field[1]], axis=2)
-    wide_source = jnp.concatenate([halo_source[0], source, halo_source[1]], axis=2)
-    wide_factor = jnp.concatenate([halo_factor[0], cell_factor, halo_factor[1]], axis=1)
-    conduct = coefficient(wide_factor, layer_material, material_scale)
-    once = relax_rows(wide_field, wide_source, conduct)
-    place = jnp.arange(6, dtype=jnp.int32)[:, None]
-    kept = ((place > 0) | inner[0]) & ((place < 5) | inner[1])
-    once = jnp.where(kept, once, 0.0)
-    field_now = relax_rows(once, source, conduct[:, 1:-1])
-    surface_top = field_now[:, -1].astype(jnp.bfloat16).transpose(1, 0, 2)
-
+    conduct = coefficient(cell_factor, layer_material, material_scale)
+    stage, *halos = exchange_line(flux_in, lists, field_in, source, conduct)
+    field_now, surface_top = sweeps(field_in, source, conduct, *halos)
     stage, surface_top = lax.optimization_barrier((stage, surface_top))
     table = lax.all_gather(surface_top, "dev", axis=0, tiled=True)
     rows, row_features, col_features = exchange_plane(
         stage, panel_pos, panel_area.reshape(1, -1)
     )
+    rows = rows.reshape(PLANE, 272, 128)
     pairs = rows[:, 256:272, 0:16].reshape(-1, 2)
     tile_ids = jnp.arange(TILES, dtype=jnp.bfloat16)
     upper = (pairs[:, 0:1] == tile_ids[None, :]).astype(jnp.bfloat16)

time: 141 us -> 143 us (1.014)
  the two profiles are of different devices: /device:TPU:23 before, /device:TPU:1 now
where the time goes in v5:
time: 143 us; the launch traced here: 140 us
  Pallas kernels  114 us (80%)
  between operations  14.1 us (10%)
  local copies, waits for them, and re-layouts  9.23 us (6%)
  other arithmetic  2.24 us (2%)
    pallas_call x1, Pallas kernels, apply_pairs(): pl.pallas_call(pair_kernel, out_shape=jax.ShapeDtypeStruct((LINE, 32, 102...  64.9 us
    pallas_call x1, Pallas kernels, exchange_plane(): pl.pallas_call(plane_kernel, out_shape=(jax.ShapeDtypeStruct((4, 4, 272,...  15.8 us
    pallas_call x1, Pallas kernels, finish(): pl.pallas_call(finish_kernel, out_shape=jax.ShapeDtypeStruct(flux_in.shap...  15.1 us
    pallas_call x1, Pallas kernels, exchange_line(): pl.pallas_call(line_kernel, out_shape=(jax.ShapeDtypeStruct((272, 128), j...  13.6 us
    unnamed x13, local copies, waits for them, and re-layouts  6.66 us
    pallas_call x1, Pallas kernels, sweeps(): pl.pallas_call(sweep_kernel, out_shape=(jax.ShapeDtypeStruct((32, LAYERS,...  4.09 us
  transfers between devices with their start and end apart: 1, of which 0 were waited for; matrix products, arithmetic and copies ran while one was open for 3% of the time, Pallas kernels for 58%

profile of v5, /device:TPU:1, one launch (start us, length us, event | category | flops | bytes accessed | tf_op | source)
XLA Modules:
  0.0 140.2 jit_solution(5652700705241063270)
XLA Ops:
  7.2 0.0 all-gather.2.cloned.1.call-start
  7.2 0.7 convert_element_type.10
  7.9 0.1 copy.20
  8.0 0.8 select_reduce_fusion
  8.7 0.8 broadcast_multiply_fusion.factor_ref.conduct_ref
  9.5 0.0 copy-start
  9.5 1.0 copy-done
  10.6 0.0 copy-start.2
  10.6 1.0 copy-done.2
  11.6 0.0 copy-start.4
  11.6 0.9 copy-done.4
  12.5 13.6 %shard_map.113 = (bf16[272,128]{1,0:T(8,128)(2,1)S(1)}, f32[2,32,8,2,128]{4,3,2,1,0:T(2,128)S(1)}, f32[2,32,8,128]{3,2,1,0:T(8,128)S(1)}, f32[2,8,128]{2,1,0:T(8,128)S(1)}) custom-call(f32[32,1024]{1,0:T(8,128)S(1)} %copy-done.4, f32[16,128]{1,0:T(8,128)S(1)} %pad.4.list_ref, f32[32,8,4,128]{3,2,1,0:T(4,128)S(1)} %copy-done, ...), custom_call_target="tpu_custom_call" | custom-call | tf_op jit(solution)/shard_map/pallas_call | solution.py:263
  26.1 0.0 copy-start.5
  26.1 0.0 copy-start.1
  26.2 1.1 copy-done.1
  27.2 0.0 copy-start.3
  27.2 1.0 copy-done.3
  28.3 4.1 %shard_map.114 = (f32[32,8,4,128]{3,2,1,0:T(4,128)}, bf16[4,32,128]{2,1,0:T(8,128)(2,1)}) custom-call(f32[32,8,4,128]{3,2,1,0:T(4,128)S(1)} %copy-done.1, f32[32,8,4,128]{3,2,1,0:T(4,128)S(1)} %copy-done.3, f32[8,4,128]{2,1,0:T(4,128)S(1)} %broadcast_multiply_fusion.factor_ref.conduct_ref, f32[2,32,8,2,128]{4,3,2,1,0:T(2,128)S(1)} %get-tuple-element.13.halo_field, ...), custom_call_target="tpu_custom_call" | custom-call | tf_op jit(solution)/shard_map/pallas_call | solution.py:87
  32.3 0.0 copy-done.5
  32.4 0.0 all-gather.2.cloned.1.call-update
  32.4 15.8 %shard_map.115 = (bf16[4,4,272,128]{3,2,1,0:T(8,128)(2,1)}, bf16[128,128,48]{2,1,0:T(8,128)(2,1)}, bf16[4,48,2048]{2,1,0:T(8,128)(2,1)}) custom-call(bf16[272,128]{1,0:T(8,128)(2,1)} %copy-done.5, f32[3,131072]{1,0:T(4,128)} %pos_far.1, f32[1,131072]{1,0:T(1,128)} %bitcast.4), custom_call_target="tpu_custom_call" | custom-call | tf_op jit(solution)/shard_map/pallas_call | solution.py:394
  48.2 0.9 slice.12
  49.1 0.4 reshape.24
  49.4 0.5 slice_reduce_fusion.1
  50.0 1.0 fusion
  51.0 0.1 copy.21
  51.1 0.6 reshape.25.mask_ref
  51.7 64.9 %shard_map.116.part_ref = bf16[8,32,1024]{2,1,0:T(8,128)(2,1)} custom-call(s32[256]{0:T(256)} %reshape.25.mask_ref, bf16[16,272,128]{2,1,0:T(8,128)(2,1)} %bitcast.7, bf16[64,256,48]{2,1,0:T(8,128)(2,1)} %bitcast.8, bf16[4,48,2048]{2,1,0:T(8,128)(2,1)} %get-tuple-element.22.q_far), custom_call_target="tpu_custom_call" | custom-call | flops 99999997952 | bytes 8388608 | tf_op jit(solution)/shard_map/pallas_call | solution.py:155
  116.6 0.0 all-gather.2.cloned.1.call-done.table_ref
  116.7 15.1 %shard_map.117 = f32[32,1024]{1,0:T(8,128)} custom-call(s32[1024]{0:T(1024)} %cell_ref.1, bf16[8,32,1024]{2,1,0:T(8,128)(2,1)} %shard_map.116.part_ref, bf16[512,32,128]{2,1,0:T(8,128)(2,1)} %all-gather.2.cloned.1.call-done.table_ref, f32[32,1024]{1,0:T(8,128)} %flux_ref.3), custom_call_target="tpu_custom_call" | custom-call | tf_op jit(solution)/shard_map/pallas_call | solution.py:462
  131.8 1.6 %copy.23 = f32[32,1024]{1,0:T(8,128)} copy(f32[32,1024]{1,0:T(8,128)} %shard_map.117) | data formatting | bytes 262144
  (2 shorter events, 0.0 us)
Async XLA Ops:
  7.2 109.5 %all-gather.2.cloned.1.call-start = ((), (), s32[]{:S(2)}) async-start(), calls=%async_computation | async-start | bytes 4227072 | tf_op jit(solution)/shard_map/all_gather | solution.py:506
  9.5 1.0 copy-start
  10.6 1.0 copy-start.2
  11.6 0.9 copy-start.4
  26.1 6.2 %copy-start.5 = (bf16[272,128]{1,0:T(8,128)(2,1)}, bf16[272,128]{1,0:T(8,128)(2,1)S(1)}, u32[]{:S(2)}) copy-start(bf16[272,128]{1,0:T(8,128)(2,1)S(1)} %get-tuple-element.19.stage_ref) | copy-start | bytes 208900
  26.1 1.1 copy-start.1
  27.2 1.0 copy-start.3
Sparse Core Ops, SparseCore 0:
  32.5 69.5 all-gather.1

commit v6 on v5

v6 whole, which is shorter than its diff:
```python
import math

import jax
import jax.numpy as jnp
from jax import lax
from jax.experimental import pallas as pl
from jax.experimental.pallas import tpu as pltpu
from jax.sharding import PartitionSpec as P

TILE = 2048
TILES = 64
LAYERS = 8
UNROLL = 4
WIDE = (63 << 20) + (1 << 19)
LINE = 8
PLANE = 16
COLS = 4 * TILE

softening = 0.0004
relax_rate = 0.8
update_rate = 0.5
kernel_gain = 0.25


def pair_kernel(
    mask_ref, f_far, pt_far, q_far, o_ref, f_ref, pt_ref, q_ref, total_ref, held_ref, order_ref, sems
):
    loads = [
        pltpu.make_async_copy(far, near, sems.at[at])
        for at, (far, near) in enumerate(((f_far, f_ref), (pt_far, pt_ref), (q_far, q_ref)))
    ]
    for load in loads:
        load.start()
    order_ref[0] = 0

    def note(at, count):
        order_ref[count + 1] = at
        return count + mask_ref[at]

    count = lax.fori_loop(0, 4 * TILES, note, jnp.int32(0))
    for u in range(UNROLL + 1):
        order_ref[count + 1 + u] = 0
    total_ref[...] = jnp.zeros(total_ref.shape, jnp.float32)
    held_ref[1] = jnp.zeros((256, TILE), jnp.bfloat16)
    for load in loads:
        load.wait()

    def step(b, carry):
        for u in range(UNROLL):
            t = b * UNROLL + u
            new, old = order_ref[t + 1], order_ref[t]
            valid = (t >= 1) & (t <= count)
            i = old % TILES
            at = pl.multiple_of((i % 4) * 64, 64)
            flux = jnp.concatenate(
                [f_ref[i // 4, pl.ds(at, 32), :], f_ref[i // 4, pl.ds(at + 32, 32), :]], axis=1
            )
            flux = jnp.where(valid, flux, jnp.zeros_like(flux))
            for c in range(4):
                columns = slice(c * 512, (c + 1) * 512)
                distance = jnp.dot(
                    pt_ref[new % TILES],
                    q_ref[new // TILES, :, columns],
                    preferred_element_type=jnp.float32,
                )
                held_ref[u % 2, :, columns] = lax.rsqrt(distance).astype(jnp.bfloat16)
                total_ref[old // TILES, :, columns] += jnp.dot(
                    flux, held_ref[1 - u % 2, :, columns], preferred_element_type=jnp.float32
                )
        return carry

    lax.fori_loop(0, (count + UNROLL) // UNROLL, step, 0)
    for j in range(4):
        for c in range(2):
            o_ref[2 * j + c] = total_ref[j, :, c * 1024 : (c + 1) * 1024].astype(jnp.bfloat16)


def apply_pairs(mask, flux_rows, row_features, col_features):
    hbm = pl.BlockSpec(memory_space=pltpu.HBM)
    return pl.pallas_call(
        pair_kernel,
        out_shape=jax.ShapeDtypeStruct((LINE, 32, 1024), jnp.bfloat16),
        in_specs=[pl.BlockSpec(memory_space=pltpu.SMEM), hbm, hbm, hbm],
        out_specs=pl.BlockSpec(memory_space=pltpu.VMEM),
        scratch_shapes=[
            pltpu.VMEM(flux_rows.shape, jnp.bfloat16),
            pltpu.VMEM(row_features.shape, jnp.bfloat16),
            pltpu.VMEM(col_features.shape, jnp.bfloat16),
            pltpu.VMEM((4, 32, TILE), jnp.float32),
            pltpu.VMEM((2, 256, TILE), jnp.bfloat16),
            pltpu.SMEM((4 * TILES + UNROLL + 2,), jnp.int32),
            pltpu.SemaphoreType.DMA((3,)),
        ],
        compiler_params=pltpu.CompilerParams(vmem_limit_bytes=WIDE),
        cost_estimate=pl.CostEstimate(
            flops=100_000_000_000, bytes_accessed=8 << 20, transcendentals=0
        ),
    )(mask, flux_rows, row_features, col_features)


def remote(src, dst, sends, recvs, at, device):
    return pltpu.make_async_remote_copy(
        src_ref=src,
        dst_ref=dst,
        send_sem=sends.at[at],
        recv_sem=recvs.at[at],
        device_id=(device,),
        device_id_type=pl.DeviceIdType.MESH,
    )


def greet(devices):
    barrier = pltpu.get_barrier_semaphore()
    for device in devices:
        pl.semaphore_signal(
            barrier, inc=1, device_id=(device,), device_id_type=pl.DeviceIdType.MESH
        )
    pl.semaphore_wait(barrier, len(devices))


def split3(value):
    high = value.astype(jnp.bfloat16).astype(jnp.float32)
    rest = value - high
    middle = rest.astype(jnp.bfloat16).astype(jnp.float32)
    return high, middle, rest - middle


def factors(pos, area, row_side):
    pos = pos - 0.5
    scale = (math.sqrt(TILE) / kernel_gain) / (area * area)
    norm = pos[0:1] * pos[0:1] + pos[1:2] * pos[1:2] + pos[2:3] * pos[2:3]
    one = jnp.ones_like(norm)
    rest = jnp.zeros((3, norm.shape[1]), jnp.float32)
    if row_side:
        parts = jnp.concatenate([norm + softening, one, -2.0 * pos, rest], axis=0) * scale
    else:
        parts = jnp.concatenate([one, norm, pos, rest], axis=0) * scale
    high, middle, low = split3(parts)
    if row_side:
        return jnp.concatenate([high, high, middle, middle, high, low], axis=0)
    return jnp.concatenate([high, middle, high, middle, low, high], axis=0)


def relax(field, source, conduct, step, lane):
    layer = jnp.zeros((1, 8, 128), jnp.float32)
    above = jnp.concatenate([field[1:], layer], axis=0)
    below = jnp.concatenate([layer, field[:-1]], axis=0)
    flat = field.reshape(LAYERS * 8, 128)
    right = jnp.where(lane < 127, pltpu.roll(flat, 127, axis=1).reshape(field.shape), 0.0)
    left = jnp.where(lane > 0, pltpu.roll(flat, 1, axis=1).reshape(field.shape), 0.0)
    ahead = pltpu.roll(field, 7, axis=1)
    behind = pltpu.roll(field, 1, axis=1)
    beside = (above + below) + (ahead + behind) + (right + left)
    applied = conduct * (6.0 * field - beside) + field
    return field + step * (source - applied)


def exchange_kernel(
    material_ref,
    scale_ref,
    list_ref,
    factor_ref,
    flux_far,
    field_far,
    source_far,
    pos_far,
    area_far,
    out_ref,
    top_ref,
    rows_ref,
    pt_ref,
    q_ref,
    flux_ref,
    field_ref,
    source_ref,
    pos_ref,
    area_ref,
    conduct_ref,
    slices,
    shared,
    stage,
    edge_field,
    edge_source,
    edge_conduct,
    halo_field,
    halo_source,
    halo_conduct,
    tops,
    pt_held,
    q_held,
    local,
    line_send,
    line_recv,
    edge_send,
    edge_recv,
    plane_send,
    plane_recv,
):
    me = lax.axis_index("dev")
    m, r = me // LINE, lax.rem(me, LINE)
    y, x = m // 4, lax.rem(m, 4)
    line = [LINE * m + lax.rem(r + k, LINE) for k in range(1, LINE)]
    after = lax.rem(me + 1, LINE * PLANE)
    before = lax.rem(me + LINE * PLANE - 1, LINE * PLANE)
    along_x = [LINE * (4 * y + lax.rem(x + k, 4)) + r for k in range(1, 4)]
    along_y = [LINE * (4 * lax.rem(y + k, 4) + x) + r for k in range(1, 4)]
    loads = [
        pltpu.make_async_copy(far, near, local.at[at])
        for at, (far, near) in enumerate(
            (
                (flux_far, flux_ref),
                (field_far, field_ref),
                (source_far, source_ref),
                (pos_far, pos_ref),
                (area_far, area_ref),
            )
        )
    ]
    for load in loads:
        load.start()
    partners = line + [after, before] + along_x + along_y
    barrier = pltpu.get_barrier_semaphore()
    for device in partners:
        pl.semaphore_signal(
            barrier, inc=1, device_id=(device,), device_id_type=pl.DeviceIdType.MESH
        )

    lane = lax.broadcasted_iota(jnp.int32, (16, 128), 1)
    pairs = list_ref[...].astype(jnp.float32)
    own_list = jnp.where(
        lane == 2 * r, pairs[:, 0:1], jnp.where(lane == 2 * r + 1, pairs[:, 1:2], 0.0)
    ).astype(jnp.bfloat16)
    loads[0].wait()
    for s in range(LINE):
        slices[s, 0:32, :] = flux_ref[:, s * 128 : (s + 1) * 128].astype(jnp.bfloat16)
        slices[s, 32:48, :] = own_list
    for layer in range(LAYERS):
        kind = material_ref[layer]
        scale = jnp.float32(0.0)
        for known in range(4):
            scale = scale + jnp.where(kind == known, scale_ref[known], 0.0)
        conduct_ref[layer] = factor_ref[layer] * scale
    loads[1].wait()
    loads[2].wait()
    for side, (at, one) in enumerate(((2, 3), (0, 0))):
        edge_field[side] = field_ref[:, :, at : at + 2, :]
        edge_source[side] = source_ref[:, :, one, :]
        edge_conduct[side] = conduct_ref[:, one, :]
    pl.semaphore_wait(barrier, len(partners))

    edges = []
    for side, device in enumerate((after, before)):
        for which, (src, dst) in enumerate(
            ((edge_field, halo_field), (edge_source, halo_source), (edge_conduct, halo_conduct))
        ):
            edges.append(
                remote(
                    src.at[side], dst.at[side], edge_send, edge_recv, 3 * side + which, device
                )
            )
    copies = []
    for k in range(1, LINE):
        there = lax.rem(r + k, LINE)
        copies.append(
            remote(slices.at[there], shared.at[r], line_send, line_recv, k - 1, line[k - 1])
        )
    for copy in copies + edges:
        copy.start()
    shared[r] = slices[r]

    def row_block(step, carry):
        for u in range(8):
            half = step * 8 + u
            at = pl.multiple_of(half * 1024 + r * 128, 128)
            part = factors(pos_ref[:, pl.ds(at, 128)], area_ref[:, pl.ds(at, 128)], True)
            pt_held[half] = part.T.astype(jnp.bfloat16)
        return carry

    loads[3].wait()
    loads[4].wait()
    lax.fori_loop(0, 3, row_block, 0)

    for copy in copies:
        copy.wait()
    lists = jnp.zeros((16, 128), jnp.float32)
    for s in range(LINE):
        stage[32 * s : 32 * s + 32, :] = shared[s, 0:32, :]
        lists = lists + shared[s, 32:48, :].astype(jnp.float32)
    stage[256:272, :] = lists.astype(jnp.bfloat16)
    own = pltpu.make_async_copy(stage, rows_ref.at[y, x], local.at[5])
    own.start()
    one, two = slice(0, 128), slice(128, 272)
    near, far = [], []
    for k in range(3):
        near.append(
            remote(stage.at[one], rows_ref.at[y, x, one], plane_send, plane_recv, k, along_x[k])
        )
        near.append(
            remote(
                stage.at[two], rows_ref.at[y, x, two], plane_send, plane_recv, 3 + k, along_y[k]
            )
        )
        part = rows_ref.at[y, :, one]
        far.append(remote(part, part, plane_send, plane_recv, 6 + k, along_y[k]))
        part = rows_ref.at[:, x, two]
        far.append(remote(part, part, plane_send, plane_recv, 9 + k, along_x[k]))
    for copy in near:
        copy.start()

    lax.fori_loop(3, 6, row_block, 0)
    own.wait()
    for copy in near:
        copy.wait()
    for copy in far:
        copy.start()

    for copy in edges:
        copy.wait()
    row = lax.broadcasted_iota(jnp.int32, (LAYERS, 8, 128), 1)
    lane = lax.broadcasted_iota(jnp.int32, (LAYERS, 8, 128), 2)
    real = ((row >= 2) | (me > 0)) & ((row < 6) | (me < LINE * PLANE - 1))
    pad = jnp.zeros((LAYERS, 1, 128), jnp.float32)
    conduct = jnp.concatenate(
        [pad, halo_conduct[0][:, None], conduct_ref[...], halo_conduct[1][:, None], pad], axis=1
    )
    step = relax_rate / (6.0 * conduct + 1.0)

    def one_load(load, carry):
        field = jnp.concatenate(
            [halo_field[0, load], field_ref[load], halo_field[1, load]], axis=1
        )
        field = jnp.where(real, field, 0.0)
        source = jnp.concatenate(
            [
                pad,
                halo_source[0, load][:, None],
                source_ref[load],
                halo_source[1, load][:, None],
                pad,
            ],
            axis=1,
        )
        field = jnp.where(real, relax(field, source, conduct, step, lane), 0.0)
        field = relax(field, source, conduct, step, lane)
        out_ref[load] = field[:, 2:6]
        tops[load] = field[LAYERS - 1, 2:6]
        return carry

    lax.fori_loop(0, 32, one_load, 0)
    for at in range(4):
        top_ref[at] = tops[:, at, :].astype(jnp.bfloat16)

    lax.fori_loop(6, TILES // 4, row_block, 0)
    moves = [pltpu.make_async_copy(pt_held, pt_ref, local.at[6])]
    moves[0].start()
    for j in range(4):
        for c in range(4):
            at = pl.multiple_of(m * COLS + j * TILE + c * 512, 512)
            part = factors(pos_ref[:, pl.ds(at, 512)], area_ref[:, pl.ds(at, 512)], False)
            q_held[j, :, c * 512 : (c + 1) * 512] = part.astype(jnp.bfloat16)
    moves.append(pltpu.make_async_copy(q_held, q_ref, local.at[7]))
    moves[1].start()
    for copy in far + moves:
        copy.wait()


def exchange(materials, scales, lists, factor, flux, field, source, pos, area):
    vmem = pl.BlockSpec(memory_space=pltpu.VMEM)
    hbm = pl.BlockSpec(memory_space=pltpu.HBM)
    smem = pl.BlockSpec(memory_space=pltpu.SMEM)
    row_shape, col_shape = (2 * TILES, 128, 48), (4, 48, TILE)
    f32, half = jnp.float32, jnp.bfloat16
    halo = [
        pltpu.VMEM((2, 32, LAYERS, 2, 128), f32),
        pltpu.VMEM((2, 32, LAYERS, 128), f32),
        pltpu.VMEM((2, LAYERS, 128), f32),
    ]
    return pl.pallas_call(
        exchange_kernel,
        out_shape=(
            jax.ShapeDtypeStruct(field.shape, f32),
            jax.ShapeDtypeStruct((4, 32, 128), half),
            jax.ShapeDtypeStruct((4, 4, 272, 128), half),
            jax.ShapeDtypeStruct(row_shape, half),
            jax.ShapeDtypeStruct(col_shape, half),
        ),
        in_specs=[smem, smem, vmem, vmem] + [hbm] * 5,
        out_specs=(vmem, vmem, hbm, hbm, hbm),
        scratch_shapes=[
            pltpu.VMEM(flux.shape, f32),
            pltpu.VMEM(field.shape, f32),
            pltpu.VMEM(source.shape, f32),
            pltpu.VMEM(pos.shape, f32),
            pltpu.VMEM(area.shape, f32),
            pltpu.VMEM(factor.shape, f32),
            pltpu.VMEM((LINE, 48, 128), half),
            pltpu.VMEM((LINE, 48, 128), half),
            pltpu.VMEM((272, 128), half),
        ]
        + halo
        + halo
        + [
            pltpu.VMEM((32, 4, 128), f32),
            pltpu.VMEM(row_shape, half),
            pltpu.VMEM(col_shape, half),
            pltpu.SemaphoreType.DMA((8,)),
            pltpu.SemaphoreType.DMA((LINE - 1,)),
            pltpu.SemaphoreType.DMA((LINE - 1,)),
            pltpu.SemaphoreType.DMA((6,)),
            pltpu.SemaphoreType.DMA((6,)),
            pltpu.SemaphoreType.DMA((12,)),
            pltpu.SemaphoreType.DMA((12,)),
        ],
        compiler_params=pltpu.CompilerParams(
            collective_id=0, has_side_effects=True, vmem_limit_bytes=WIDE
        ),
    )(materials, scales, lists, factor, flux, field, source, pos, area)


def reduce_kernel(part_ref, out_ref, landed, sends, recvs):
    me = lax.axis_index("dev")
    m, r = me // LINE, lax.rem(me, LINE)
    line = [LINE * m + lax.rem(r + k, LINE) for k in range(1, LINE)]
    greet(line)
    copies = []
    for k in range(1, LINE):
        there = lax.rem(r + k, LINE)
        copies.append(
            remote(part_ref.at[there], landed.at[k - 1], sends, recvs, k - 1, line[k - 1])
        )
    for copy in copies:
        copy.start()
    total = part_ref[r].astype(jnp.float32)
    for k, copy in enumerate(copies):
        copy.wait()
        total = total + landed[k].astype(jnp.float32)
    out_ref[...] = total


def reduce_line(partial):
    vmem = pl.BlockSpec(memory_space=pltpu.VMEM)
    return pl.pallas_call(
        reduce_kernel,
        out_shape=jax.ShapeDtypeStruct((32, 1024), jnp.float32),
        in_specs=[vmem],
        out_specs=vmem,
        scratch_shapes=[
            pltpu.VMEM((LINE - 1, 32, 1024), jnp.bfloat16),
            pltpu.SemaphoreType.DMA((LINE - 1,)),
            pltpu.SemaphoreType.DMA((LINE - 1,)),
        ],
        compiler_params=pltpu.CompilerParams(
            collective_id=1, has_side_effects=True, vmem_limit_bytes=8 << 20
        ),
    )(partial)


def finish_kernel(cell_ref, total_ref, flux_ref, table_ref, out_ref):
    lane = lax.broadcasted_iota(jnp.int32, (32, 128), 1)
    for g in range(8):

        def pick(step, held):
            for u in range(16):
                at = step * 16 + u
                cell = cell_ref[g * 128 + at]
                block = table_ref[lax.shift_right_logical(cell, 7)].astype(jnp.float32)
                moved = pltpu.roll(block, (at - cell) & 127, axis=1)
                held = jnp.where(lane == at, moved, held)
            return held

        traces = lax.fori_loop(0, 8, pick, jnp.zeros((32, 128), jnp.float32))
        at = slice(g * 128, (g + 1) * 128)
        out_ref[:, at] = flux_ref[:, at] + update_rate * (traces - total_ref[:, at])


def finish(cells, total, flux_in, table):
    vmem = pl.BlockSpec(memory_space=pltpu.VMEM)
    return pl.pallas_call(
        finish_kernel,
        out_shape=jax.ShapeDtypeStruct(flux_in.shape, jnp.float32),
        in_specs=[pl.BlockSpec(memory_space=pltpu.SMEM), vmem, vmem, vmem],
        out_specs=vmem,
        compiler_params=pltpu.CompilerParams(vmem_limit_bytes=8 << 20),
    )(cells, total, flux_in, table)


def body(
    field_in,
    source,
    cell_factor,
    layer_material,
    material_scale,
    panel_cell,
    panel_pos,
    panel_area,
    flux_in,
    pair_list,
):
    me = lax.axis_index("dev")
    m = me // LINE

    field_now, surface_top, rows, row_features, col_features = exchange(
        layer_material,
        material_scale,
        pair_list,
        cell_factor,
        flux_in,
        field_in,
        source,
        panel_pos,
        panel_area.reshape(1, -1),
    )
    table = lax.all_gather(surface_top, "dev", axis=0, tiled=True)
    rows = rows.reshape(PLANE, 272, 128)
    pairs = rows[:, 256:272, 0:16].reshape(-1, 2)
    tile_ids = jnp.arange(TILES, dtype=jnp.bfloat16)
    upper = (pairs[:, 0:1] == tile_ids[None, :]).astype(jnp.bfloat16)
    lower = (pairs[:, 1:2] == tile_ids[None, :]).astype(jnp.bfloat16)
    listed = lax.dot_general(
        upper, lower, (((0,), (0,)), ((), ())), preferred_element_type=jnp.float32
    )
    listed = (listed + listed.T > 0.0).astype(jnp.int32)
    mask = lax.dynamic_slice(listed, (4 * m, 0), (4, TILES)).reshape(-1)

    partial = apply_pairs(mask, rows, row_features.reshape(TILES, 256, 48), col_features)
    flux_out = finish(panel_cell, reduce_line(partial), flux_in, table)
    return (field_now, flux_out)


def solution(mesh):
    in_specs = (
        P(None, None, "dev", None),
        P(None, None, "dev", None),
        P(None, "dev", None),
        P(),
        P(),
        P("dev"),
        P(),
        P(),
        P(None, "dev"),
        P("dev", None),
    )
    out_specs = (P(None, None, "dev", None), P(None, "dev"))
    return jax.shard_map(body, mesh=mesh, in_specs=in_specs, out_specs=out_specs, check_vma=False)
```

time: 143 us -> 135 us (0.944)
  Pallas kernels: 114 us -> 111 us
  other arithmetic: 2.24 us -> 0.01 us
    pallas_call x3 -> x2, Pallas kernels: 33.5 us -> 41.6 us  [the longest x1 30.9 us: exchange(): pl.pallas_call(exchange_kernel, out_shape=(jax.ShapeDtypeStruct(field.sha...]
    pallas_call x1, Pallas kernels: 15.1 us -> 8.05 us  [finish(): pl.pallas_call(finish_kernel, out_shape=jax.ShapeDtypeStruct(flux_in.shap...]
    pallas_call x1, Pallas kernels: 64.9 us -> 60.9 us  [apply_pairs(): pl.pallas_call(pair_kernel, out_shape=jax.ShapeDtypeStruct((LINE, 32, 102...]
    unnamed x13 -> x12, local copies, waits for them, and re-layouts: 6.66 us -> 5.38 us
  transfers between devices with their start and end apart: 1 -> 1, of which waited for: 0 -> 0; matrix products, arithmetic and copies ran while one was open for 3% -> 3% of each run, Pallas kernels for 58% -> 54%
where the time goes in v6:
time: 135 us; the launch traced here: 134 us
  Pallas kernels  111 us (82%)
  between operations  14.1 us (10%)
  local copies, waits for them, and re-layouts  7.85 us (6%)
    pallas_call x1, Pallas kernels, apply_pairs(): pl.pallas_call(pair_kernel, out_shape=jax.ShapeDtypeStruct((LINE, 32, 102...  60.9 us
    pallas_call x1, Pallas kernels, exchange(): pl.pallas_call(exchange_kernel, out_shape=(jax.ShapeDtypeStruct(field.sha...  30.9 us
    pallas_call x1, Pallas kernels, reduce_line(): pl.pallas_call(reduce_kernel, out_shape=jax.ShapeDtypeStruct((32, 1024),...  10.6 us
    pallas_call x1, Pallas kernels, finish(): pl.pallas_call(finish_kernel, out_shape=jax.ShapeDtypeStruct(flux_in.shap...  8.05 us
    unnamed x12, local copies, waits for them, and re-layouts  5.38 us
  transfers between devices with their start and end apart: 1, of which 0 were waited for; matrix products, arithmetic and copies ran while one was open for 3% of the time, Pallas kernels for 54%

profile of v6, /device:TPU:1, one launch (start us, length us, event | category | flops | bytes accessed | tf_op | source)
XLA Modules:
  0.0 133.6 jit_solution(9158355281140150543)
XLA Ops:
  7.2 0.0 all-gather.2.cloned.1.call-start
  7.2 1.4 %copy.16.list_ref = s32[16,2]{1,0:T(8,128)} copy(s32[16,2]{0,1:T(2,128)} %param.19) | data formatting | bytes 256 | tf_op args[9]
  8.6 30.9 %shard_map.113 = (f32[32,8,4,128]{3,2,1,0:T(4,128)}, bf16[4,32,128]{2,1,0:T(8,128)(2,1)}, bf16[4,4,272,128]{3,2,1,0:T(8,128)(2,1)}, bf16[128,128,48]{2,1,0:T(8,128)(2,1)}, bf16[4,48,2048]{2,1,0:T(8,128)(2,1)}) custom-call(s32[8]{0:T(128)} %material_ref.1, f32[4]{0:T(128)} %scale_ref.1, s32[16,2]{1,0:T(8,128)} %copy.16.list_ref, f32[8,4,128]{2,1,0:T(4,128)} %factor_ref.1, ...), custom_call_target="tpu_custom_call" | custom-call | tf_op jit(solution)/shard_map/pallas_call | solution.py:378
  39.5 0.0 all-gather.2.cloned.1.call-update
  39.5 0.9 slice.12
  40.4 0.4 reshape.21
  40.8 0.5 slice_reduce_fusion.1
  41.3 1.0 fusion
  42.3 0.1 copy.17
  42.4 0.6 reshape.22.mask_ref
  43.1 0.0 copy-start.2
  43.1 0.0 copy-start.3
  43.1 60.9 %shard_map.114.part_ref = bf16[8,32,1024]{2,1,0:T(8,128)(2,1)} custom-call(s32[256]{0:T(256)} %reshape.22.mask_ref, bf16[16,272,128]{2,1,0:T(8,128)(2,1)} %bitcast.7, bf16[64,256,48]{2,1,0:T(8,128)(2,1)} %bitcast.8, bf16[4,48,2048]{2,1,0:T(8,128)(2,1)} %get-tuple-element.10.q_far), custom_call_target="tpu_custom_call" | custom-call | flops 99999997952 | bytes 8388608 | tf_op jit(solution)/shard_map/pallas_call | solution.py:80
  104.0 0.0 copy-start.1
  104.0 1.0 copy-done.1
  105.0 0.0 copy-start.4
  105.0 10.6 %shard_map.115.total_ref = f32[32,1024]{1,0:T(8,128)S(1)} custom-call(bf16[8,32,1024]{2,1,0:T(8,128)(2,1)S(1)} %copy-done.1), custom_call_target="tpu_custom_call" | custom-call | tf_op jit(solution)/shard_map/pallas_call | solution.py:442
  115.7 0.0 all-gather.2.cloned.1.call-done.table_ref
  115.7 0.0 copy-done.2
  115.7 0.0 copy-done.3
  115.7 0.0 copy-start
  115.7 2.2 %copy-done = bf16[512,32,128]{2,1,0:T(8,128)(2,1)S(1)} copy-done((bf16[512,32,128]{2,1,0:T(8,128)(2,1)S(1)}, bf16[512,32,128]{2,1,0:T(8,128)(2,1)}, u32[]{:S(2)}) %copy-start) | copy-done | bytes 4194328
  117.9 8.1 %shard_map.116 = f32[32,1024]{1,0:T(8,128)} custom-call(s32[1024]{0:T(1024)S(1)} %copy-done.3, f32[32,1024]{1,0:T(8,128)S(1)} %shard_map.115.total_ref, f32[32,1024]{1,0:T(8,128)S(1)} %copy-done.2, bf16[512,32,128]{2,1,0:T(8,128)(2,1)S(1)} %copy-done), custom_call_target="tpu_custom_call" | custom-call | tf_op jit(solution)/shard_map/pallas_call | solution.py:478
  126.0 0.0 copy-done.4
  126.0 0.8 copy.19
  (1 shorter events, 0.0 us)
Async XLA Ops:
  7.2 108.5 %all-gather.2.cloned.1.call-start = ((), (), s32[]{:S(2)}) async-start(), calls=%async_computation | async-start | bytes 4227072 | tf_op jit(solution)/shard_map/all_gather | solution.py:513
  43.1 72.6 %copy-start.2 = (f32[32,1024]{1,0:T(8,128)S(1)}, f32[32,1024]{1,0:T(8,128)}, u32[]{:S(2)}) copy-start(f32[32,1024]{1,0:T(8,128)} %flux_ref.1) | copy-start | bytes 393220
  43.1 72.6 %copy-start.3 = (s32[1024]{0:T(1024)S(1)}, s32[1024]{0:T(1024)}, u32[]{:S(2)}) copy-start(s32[1024]{0:T(1024)} %cell_ref.1) | copy-start | bytes 12292
  104.0 1.0 copy-start.1
  105.0 20.9 %copy-start.4 = (f32[32,8,4,128]{3,2,1,0:T(4,128)S(1)}, f32[32,8,4,128]{3,2,1,0:T(4,128)}, u32[]{:S(2)}) copy-start(f32[32,8,4,128]{3,2,1,0:T(4,128)} %get-tuple-element.16) | copy-start | bytes 1572868
  115.7 2.2 %copy-start = (bf16[512,32,128]{2,1,0:T(8,128)(2,1)S(1)}, bf16[512,32,128]{2,1,0:T(8,128)(2,1)}, u32[]{:S(2)}) copy-start(bf16[512,32,128]{2,1,0:T(8,128)(2,1)} %all-gather.2.cloned.1.call-done.table_ref) | copy-start | bytes 12582916
Sparse Core Ops, SparseCore 0:
  39.7 64.8 all-gather.1

commit v7 on v6

--- a/solution.py
+++ b/solution.py
@@ -417,71 +417,72 @@
     )(materials, scales, lists, factor, flux, field, source, pos, area)
 
 
-def reduce_kernel(part_ref, out_ref, landed, sends, recvs):
+def finish_kernel(
+    cell_ref, part_ref, table_ref, flux_ref, out_ref, table, landed, traces, load_sem, sends, recvs
+):
     me = lax.axis_index("dev")
     m, r = me // LINE, lax.rem(me, LINE)
+    load = pltpu.make_async_copy(table_ref, table, load_sem)
+    load.start()
     line = [LINE * m + lax.rem(r + k, LINE) for k in range(1, LINE)]
     greet(line)
     copies = []
     for k in range(1, LINE):
         there = lax.rem(r + k, LINE)
-        copies.append(
-            remote(part_ref.at[there], landed.at[k - 1], sends, recvs, k - 1, line[k - 1])
-        )
+        copy = remote(part_ref.at[there], landed.at[k - 1], sends, recvs, k - 1, line[k - 1])
+        copy.start()
+        copies.append(copy)
+    load.wait()
+    lane = lax.broadcasted_iota(jnp.int32, (32, 128), 1)
+
+    def group(g, carry):
+        def pick(step, held):
+            for u in range(16):
+                at = step * 16 + u
+                cell = cell_ref[g * 128 + at]
+                block = table[lax.shift_right_logical(cell, 7)].astype(jnp.float32)
+                moved = pltpu.roll(block, (at - cell) & 127, axis=1)
+                held = jnp.where(lane == at, moved, held)
+            return held
+
+        traces[g] = lax.fori_loop(0, 8, pick, jnp.zeros((32, 128), jnp.float32))
+        return carry
+
+    lax.fori_loop(0, 8, group, 0)
     for copy in copies:
-        copy.start()
+        copy.wait()
     total = part_ref[r].astype(jnp.float32)
-    for k, copy in enumerate(copies):
-        copy.wait()
+    for k in range(LINE - 1):
         total = total + landed[k].astype(jnp.float32)
-    out_ref[...] = total
-
-
-def reduce_line(partial):
+    for g in range(8):
+        at = slice(g * 128, (g + 1) * 128)
+        out_ref[:, at] = flux_ref[:, at] + update_rate * (traces[g] - total[:, at])
+
+
+def finish(cells, partial, table, flux_in):
     vmem = pl.BlockSpec(memory_space=pltpu.VMEM)
     return pl.pallas_call(
-        reduce_kernel,
-        out_shape=jax.ShapeDtypeStruct((32, 1024), jnp.float32),
-        in_specs=[vmem],
+        finish_kernel,
+        out_shape=jax.ShapeDtypeStruct(flux_in.shape, jnp.float32),
+        in_specs=[
+            pl.BlockSpec(memory_space=pltpu.SMEM),
+            vmem,
+            pl.BlockSpec(memory_space=pltpu.HBM),
+            vmem,
+        ],
         out_specs=vmem,
         scratch_shapes=[
+            pltpu.VMEM(table.shape, jnp.bfloat16),
             pltpu.VMEM((LINE - 1, 32, 1024), jnp.bfloat16),
+            pltpu.VMEM((8, 32, 128), jnp.float32),
+            pltpu.SemaphoreType.DMA,
             pltpu.SemaphoreType.DMA((LINE - 1,)),
             pltpu.SemaphoreType.DMA((LINE - 1,)),
         ],
         compiler_params=pltpu.CompilerParams(
-            collective_id=1, has_side_effects=True, vmem_limit_bytes=8 << 20
+            collective_id=1, has_side_effects=True, vmem_limit_bytes=WIDE
         ),
-    )(partial)
-
-
-def finish_kernel(cell_ref, total_ref, flux_ref, table_ref, out_ref):
-    lane = lax.broadcasted_iota(jnp.int32, (32, 128), 1)
-    for g in range(8):
-
-        def pick(step, held):
-            for u in range(16):
-                at = step * 16 + u
-                cell = cell_ref[g * 128 + at]
-                block = table_ref[lax.shift_right_logical(cell, 7)].astype(jnp.float32)
-                moved = pltpu.roll(block, (at - cell) & 127, axis=1)
-                held = jnp.where(lane == at, moved, held)
-            return held
-
-        traces = lax.fori_loop(0, 8, pick, jnp.zeros((32, 128), jnp.float32))
-        at = slice(g * 128, (g + 1) * 128)
-        out_ref[:, at] = flux_ref[:, at] + update_rate * (traces - total_ref[:, at])
-
-
-def finish(cells, total, flux_in, table):
-    vmem = pl.BlockSpec(memory_space=pltpu.VMEM)
-    return pl.pallas_call(
-        finish_kernel,
-        out_shape=jax.ShapeDtypeStruct(flux_in.shape, jnp.float32),
-        in_specs=[pl.BlockSpec(memory_space=pltpu.SMEM), vmem, vmem, vmem],
-        out_specs=vmem,
-        compiler_params=pltpu.CompilerParams(vmem_limit_bytes=8 << 20),
-    )(cells, total, flux_in, table)
+    )(cells, partial, table, flux_in)
 
 
 def body(
@@ -523,7 +524,7 @@
     mask = lax.dynamic_slice(listed, (4 * m, 0), (4, TILES)).reshape(-1)
 
     partial = apply_pairs(mask, rows, row_features.reshape(TILES, 256, 48), col_features)
-    flux_out = finish(panel_cell, reduce_line(partial), flux_in, table)
+    flux_out = finish(panel_cell, partial, table, flux_in)
     return (field_now, flux_out)
 
 

time: 135 us -> 127 us (0.941)
  Pallas kernels: 111 us -> 97.9 us
  waiting for transfers between devices: 0.04 us -> 6.23 us
    pallas_call x1 -> x0, Pallas kernels: 10.6 us -> none  [reduce_line(): pl.pallas_call(reduce_kernel, out_shape=jax.ShapeDtypeStruct((32, 1024),...]
    all_gather x1, waiting for transfers between devices: 0.02 us -> 6.22 us  [body(): table = lax.all_gather(surface_top, 'dev', axis=0, tiled=True)]
    pallas_call x1, Pallas kernels: 60.9 us -> 55.2 us  [apply_pairs(): pl.pallas_call(pair_kernel, out_shape=jax.ShapeDtypeStruct((LINE, 32, 102...]
    pallas_call x1, Pallas kernels: 8.05 us -> 11.7 us  [finish(): pl.pallas_call(finish_kernel, out_shape=jax.ShapeDtypeStruct(flux_in.shap...]
    unnamed x12 -> x3, local copies, waits for them, and re-layouts: 5.38 us -> 4.79 us
  transfers between devices with their start and end apart: 1 -> 1, of which waited for: 0 -> 1; matrix products, arithmetic and copies ran while one was open for 3% -> 3% of each run, Pallas kernels for 54% -> 44%
where the time goes in v7:
time: 127 us
  Pallas kernels  97.9 us (77%)
  between operations  14.1 us (11%)
  local copies, waits for them, and re-layouts  7.27 us (6%)
  waiting for transfers between devices  6.23 us (5%)
    pallas_call x1, Pallas kernels, apply_pairs(): pl.pallas_call(pair_kernel, out_shape=jax.ShapeDtypeStruct((LINE, 32, 102...  55.2 us
    pallas_call x1, Pallas kernels, exchange(): pl.pallas_call(exchange_kernel, out_shape=(jax.ShapeDtypeStruct(field.sha...  31 us
    pallas_call x1, Pallas kernels, finish(): pl.pallas_call(finish_kernel, out_shape=jax.ShapeDtypeStruct(flux_in.shap...  11.7 us
    all_gather x1, waiting for transfers between devices, body(): table = lax.all_gather(surface_top, 'dev', axis=0, tiled=True)  6.22 us
    unnamed x3, local copies, waits for them, and re-layouts  4.79 us
  transfers between devices with their start and end apart: 1, of which 1 were waited for; matrix products, arithmetic and copies ran while one was open for 3% of the time, Pallas kernels for 44%

profile of v7, /device:TPU:1, one launch (start us, length us, event | category | flops | bytes accessed | tf_op | source)
XLA Modules:
  0.0 126.6 jit_solution(10621558610615054644)
XLA Ops:
  7.2 0.0 all-gather.2.cloned.1.call-start
  7.2 1.4 %copy.16.list_ref = s32[16,2]{1,0:T(8,128)} copy(s32[16,2]{0,1:T(2,128)} %param.19) | data formatting | bytes 256 | tf_op args[9]
  8.6 31.0 %shard_map.113 = (f32[32,8,4,128]{3,2,1,0:T(4,128)}, bf16[4,32,128]{2,1,0:T(8,128)(2,1)}, bf16[4,4,272,128]{3,2,1,0:T(8,128)(2,1)}, bf16[128,128,48]{2,1,0:T(8,128)(2,1)}, bf16[4,48,2048]{2,1,0:T(8,128)(2,1)}) custom-call(s32[8]{0:T(128)} %material_ref.1, f32[4]{0:T(128)} %scale_ref.1, s32[16,2]{1,0:T(8,128)} %copy.16.list_ref, f32[8,4,128]{2,1,0:T(4,128)} %factor_ref.1, ...), custom_call_target="tpu_custom_call" | custom-call | tf_op jit(solution)/shard_map/pallas_call | solution.py:378
  39.5 0.0 all-gather.2.cloned.1.call-update
  39.6 0.9 slice.12
  40.4 0.4 reshape.21
  40.8 0.5 slice_reduce_fusion.1
  41.3 1.0 fusion
  42.3 0.1 copy.17
  42.4 0.6 reshape.22.mask_ref
  43.1 55.2 %shard_map.114.part_ref = bf16[8,32,1024]{2,1,0:T(8,128)(2,1)} custom-call(s32[256]{0:T(256)} %reshape.22.mask_ref, bf16[16,272,128]{2,1,0:T(8,128)(2,1)} %bitcast.7, bf16[64,256,48]{2,1,0:T(8,128)(2,1)} %bitcast.8, bf16[4,48,2048]{2,1,0:T(8,128)(2,1)} %get-tuple-element.10.q_far), custom_call_target="tpu_custom_call" | custom-call | flops 99999997952 | bytes 8388608 | tf_op jit(solution)/shard_map/pallas_call | solution.py:80
  98.3 6.2 %all-gather.2.cloned.1.call-done.table_ref = bf16[512,32,128]{2,1,0:T(8,128)(2,1)} async-done(((bf16[4,32,128]{2,1,0:T(8,128)(2,1)}), bf16[512,32,128]{2,1,0:T(8,128)(2,1)}) %all-gather.2.cloned.1.call-update) | async-done | bytes 4194320 | tf_op jit(solution)/shard_map/all_gather | solution.py:514
  104.6 11.7 %shard_map.115 = f32[32,1024]{1,0:T(8,128)} custom-call(s32[1024]{0:T(1024)} %cell_ref.1, bf16[8,32,1024]{2,1,0:T(8,128)(2,1)} %shard_map.114.part_ref, bf16[512,32,128]{2,1,0:T(8,128)(2,1)} %all-gather.2.cloned.1.call-done.table_ref, f32[32,1024]{1,0:T(8,128)} %flux_ref.1), custom_call_target="tpu_custom_call" | custom-call | tf_op jit(solution)/shard_map/pallas_call | solution.py:464
  116.3 1.9 %copy.20 = f32[32,8,4,128]{3,2,1,0:T(4,128)} copy(f32[32,8,4,128]{3,2,1,0:T(4,128)} %get-tuple-element.16) | data formatting | bytes 1048576
  118.1 1.6 %copy.21 = f32[32,1024]{1,0:T(8,128)} copy(f32[32,1024]{1,0:T(8,128)} %shard_map.115) | data formatting | bytes 262144
  (1 shorter events, 0.0 us)
Async XLA Ops:
  7.2 97.4 %all-gather.2.cloned.1.call-start = ((), (), s32[]{:S(2)}) async-start(), calls=%async_computation | async-start | bytes 4227072 | tf_op jit(solution)/shard_map/all_gather | solution.py:514
Sparse Core Ops, SparseCore 0:
  39.7 64.8 all-gather.1

commit v8 on v7

--- a/solution.py
+++ b/solution.py
@@ -225,11 +225,11 @@
             barrier, inc=1, device_id=(device,), device_id_type=pl.DeviceIdType.MESH
         )
 
-    lane = lax.broadcasted_iota(jnp.int32, (16, 128), 1)
-    pairs = list_ref[...].astype(jnp.float32)
-    own_list = jnp.where(
-        lane == 2 * r, pairs[:, 0:1], jnp.where(lane == 2 * r + 1, pairs[:, 1:2], 0.0)
-    ).astype(jnp.bfloat16)
+    pairs = jnp.concatenate(
+        [list_ref[...].astype(jnp.float32), jnp.zeros((2, 112), jnp.float32)], axis=1
+    )
+    pairs = jnp.concatenate([pairs, jnp.zeros((14, 128), jnp.float32)], axis=0)
+    own_list = pltpu.roll(pairs, 16 * r, axis=1).astype(jnp.bfloat16)
     loads[0].wait()
     for s in range(LINE):
         slices[s, 0:32, :] = flux_ref[:, s * 128 : (s + 1) * 128].astype(jnp.bfloat16)
@@ -278,7 +278,7 @@
 
     loads[3].wait()
     loads[4].wait()
-    lax.fori_loop(0, 3, row_block, 0)
+    lax.fori_loop(0, 8, row_block, 0)
 
     for copy in copies:
         copy.wait()
@@ -307,7 +307,9 @@
     for copy in near:
         copy.start()
 
-    lax.fori_loop(3, 6, row_block, 0)
+    lax.fori_loop(8, TILES // 4, row_block, 0)
+    moves = [pltpu.make_async_copy(pt_held, pt_ref, local.at[6])]
+    moves[0].start()
     own.wait()
     for copy in near:
         copy.wait()
@@ -346,13 +348,10 @@
         tops[load] = field[LAYERS - 1, 2:6]
         return carry
 
-    lax.fori_loop(0, 32, one_load, 0)
+    lax.fori_loop(0, 32, one_load, 0, unroll=4)
     for at in range(4):
         top_ref[at] = tops[:, at, :].astype(jnp.bfloat16)
 
-    lax.fori_loop(6, TILES // 4, row_block, 0)
-    moves = [pltpu.make_async_copy(pt_held, pt_ref, local.at[6])]
-    moves[0].start()
     for j in range(4):
         for c in range(4):
             at = pl.multiple_of(m * COLS + j * TILE + c * 512, 512)
@@ -503,7 +502,7 @@
     field_now, surface_top, rows, row_features, col_features = exchange(
         layer_material,
         material_scale,
-        pair_list,
+        pair_list.T,
         cell_factor,
         flux_in,
         field_in,
@@ -513,12 +512,11 @@
     )
     table = lax.all_gather(surface_top, "dev", axis=0, tiled=True)
     rows = rows.reshape(PLANE, 272, 128)
-    pairs = rows[:, 256:272, 0:16].reshape(-1, 2)
-    tile_ids = jnp.arange(TILES, dtype=jnp.bfloat16)
-    upper = (pairs[:, 0:1] == tile_ids[None, :]).astype(jnp.bfloat16)
-    lower = (pairs[:, 1:2] == tile_ids[None, :]).astype(jnp.bfloat16)
+    tile_ids = jnp.arange(TILES, dtype=jnp.bfloat16)[:, None]
+    upper = (rows[:, 256].reshape(1, -1) == tile_ids).astype(jnp.bfloat16)
+    lower = (rows[:, 257].reshape(1, -1) == tile_ids).astype(jnp.bfloat16)
     listed = lax.dot_general(
-        upper, lower, (((0,), (0,)), ((), ())), preferred_element_type=jnp.float32
+        upper, lower, (((1,), (1,)), ((), ())), preferred_element_type=jnp.float32
     )
     listed = (listed + listed.T > 0.0).astype(jnp.int32)
     mask = lax.dynamic_slice(listed, (4 * m, 0), (4, TILES)).reshape(-1)

time: 127 us -> 125 us (0.984)
  waiting for transfers between devices: 6.23 us -> 3.93 us
  local copies, waits for them, and re-layouts: 7.27 us -> 5.08 us
  Pallas kernels: 97.9 us -> 100 us
    pallas_call x1, Pallas kernels: 55.2 us -> 59.4 us  [apply_pairs(): pl.pallas_call(pair_kernel, out_shape=jax.ShapeDtypeStruct((LINE, 32, 102...]
    all_gather x1, waiting for transfers between devices: 6.22 us -> 3.91 us  [body(): table = lax.all_gather(surface_top, 'dev', axis=0, tiled=True)]
    pallas_call x1, Pallas kernels: 31 us -> 29.1 us  [exchange(): pl.pallas_call(exchange_kernel, out_shape=(jax.ShapeDtypeStruct(field.sha...]
    unnamed x3 -> x2, local copies, waits for them, and re-layouts: 4.79 us -> 3.44 us
  transfers between devices with their start and end apart: 1 -> 1, of which waited for: 1 -> 1; matrix products, arithmetic and copies ran while one was open for 3% -> 2% of each run, Pallas kernels for 44% -> 48%
where the time goes in v8:
time: 125 us; the launch traced here: 124 us
  Pallas kernels  100 us (80%)
  between operations  14.1 us (11%)
  local copies, waits for them, and re-layouts  5.08 us (4%)
  waiting for transfers between devices  3.93 us (3%)
    pallas_call x1, Pallas kernels, apply_pairs(): pl.pallas_call(pair_kernel, out_shape=jax.ShapeDtypeStruct((LINE, 32, 102...  59.4 us
    pallas_call x1, Pallas kernels, exchange(): pl.pallas_call(exchange_kernel, out_shape=(jax.ShapeDtypeStruct(field.sha...  29.1 us
    pallas_call x1, Pallas kernels, finish(): pl.pallas_call(finish_kernel, out_shape=jax.ShapeDtypeStruct(flux_in.shap...  11.7 us
    all_gather x1, waiting for transfers between devices, body(): table = lax.all_gather(surface_top, 'dev', axis=0, tiled=True)  3.91 us
    unnamed x2, local copies, waits for them, and re-layouts  3.44 us
  transfers between devices with their start and end apart: 1, of which 1 were waited for; matrix products, arithmetic and copies ran while one was open for 2% of the time, Pallas kernels for 48%

profile of v8, /device:TPU:1, one launch (start us, length us, event | category | flops | bytes accessed | tf_op | source)
XLA Modules:
  0.0 123.6 jit_solution(932855158331906590)
XLA Ops:
  7.2 0.0 all-gather.2.cloned.1.call-start
  7.2 29.1 %shard_map.113 = (f32[32,8,4,128]{3,2,1,0:T(4,128)}, bf16[4,32,128]{2,1,0:T(8,128)(2,1)}, bf16[4,4,272,128]{3,2,1,0:T(8,128)(2,1)}, bf16[128,128,48]{2,1,0:T(8,128)(2,1)}, bf16[4,48,2048]{2,1,0:T(8,128)(2,1)}) custom-call(s32[8]{0:T(128)} %material_ref.1, f32[4]{0:T(128)} %scale_ref.1, s32[2,16]{1,0:T(2,128)} %bitcast.11, f32[8,4,128]{2,1,0:T(4,128)} %factor_ref.1, ...), custom_call_target="tpu_custom_call" | custom-call | tf_op jit(solution)/shard_map/pallas_call | solution.py:377
  36.3 0.0 all-gather.2.cloned.1.call-update
  36.4 0.9 slice_reduce_fusion.1
  37.3 0.3 fusion
  37.6 0.1 copy.14
  37.7 0.6 reshape.20.mask_ref
  38.3 59.4 %shard_map.114.part_ref = bf16[8,32,1024]{2,1,0:T(8,128)(2,1)} custom-call(s32[256]{0:T(256)} %reshape.20.mask_ref, bf16[16,272,128]{2,1,0:T(8,128)(2,1)} %bitcast.13, bf16[64,256,48]{2,1,0:T(8,128)(2,1)} %bitcast.14, bf16[4,48,2048]{2,1,0:T(8,128)(2,1)} %get-tuple-element.10.q_far), custom_call_target="tpu_custom_call" | custom-call | flops 99999997952 | bytes 8388608 | tf_op jit(solution)/shard_map/pallas_call | solution.py:80
  97.7 3.9 %all-gather.2.cloned.1.call-done.table_ref = bf16[512,32,128]{2,1,0:T(8,128)(2,1)} async-done(((bf16[4,32,128]{2,1,0:T(8,128)(2,1)}), bf16[512,32,128]{2,1,0:T(8,128)(2,1)}) %all-gather.2.cloned.1.call-update) | async-done | bytes 4194320 | tf_op jit(solution)/shard_map/all_gather | solution.py:513
  101.6 11.7 %shard_map.115 = f32[32,1024]{1,0:T(8,128)} custom-call(s32[1024]{0:T(1024)} %cell_ref.1, bf16[8,32,1024]{2,1,0:T(8,128)(2,1)} %shard_map.114.part_ref, bf16[512,32,128]{2,1,0:T(8,128)(2,1)} %all-gather.2.cloned.1.call-done.table_ref, f32[32,1024]{1,0:T(8,128)} %flux_ref.1), custom_call_target="tpu_custom_call" | custom-call | tf_op jit(solution)/shard_map/pallas_call | solution.py:463
  113.3 1.9 %copy.17 = f32[32,8,4,128]{3,2,1,0:T(4,128)} copy(f32[32,8,4,128]{3,2,1,0:T(4,128)} %get-tuple-element.16) | data formatting | bytes 1048576
  115.2 1.6 %copy.18 = f32[32,1024]{1,0:T(8,128)} copy(f32[32,1024]{1,0:T(8,128)} %shard_map.115) | data formatting | bytes 262144
  (1 shorter events, 0.0 us)
Async XLA Ops:
  7.2 94.4 %all-gather.2.cloned.1.call-start = ((), (), s32[]{:S(2)}) async-start(), calls=%async_computation | async-start | bytes 4227072 | tf_op jit(solution)/shard_map/all_gather | solution.py:513
Sparse Core Ops, SparseCore 0:
  36.5 65.0 all-gather.1

commit v9 on v8

--- a/solution.py
+++ b/solution.py
@@ -11,6 +11,7 @@
 TILES = 64
 LAYERS = 8
 UNROLL = 4
+LONG = 16
 WIDE = (63 << 20) + (1 << 19)
 LINE = 8
 PLANE = 16
@@ -45,9 +46,9 @@
     for load in loads:
         load.wait()
 
-    def step(b, carry):
-        for u in range(UNROLL):
-            t = b * UNROLL + u
+    def run(start, steps):
+        for u in range(steps):
+            t = start + u
             new, old = order_ref[t + 1], order_ref[t]
             valid = (t >= 1) & (t <= count)
             i = old % TILES
@@ -67,9 +68,18 @@
                 total_ref[old // TILES, :, columns] += jnp.dot(
                     flux, held_ref[1 - u % 2, :, columns], preferred_element_type=jnp.float32
                 )
+
+    def long_block(b, carry):
+        run(b * LONG, LONG)
         return carry
 
-    lax.fori_loop(0, (count + UNROLL) // UNROLL, step, 0)
+    def short_block(b, carry):
+        run(full * LONG + b * UNROLL, UNROLL)
+        return carry
+
+    full = (count + 1) // LONG
+    lax.fori_loop(0, full, long_block, 0)
+    lax.fori_loop(0, (count + UNROLL - full * LONG) // UNROLL, short_block, 0)
     for j in range(4):
         for c in range(2):
             o_ref[2 * j + c] = total_ref[j, :, c * 1024 : (c + 1) * 1024].astype(jnp.bfloat16)
@@ -436,15 +446,17 @@
 
     def group(g, carry):
         def pick(step, held):
-            for u in range(16):
-                at = step * 16 + u
+            held = list(held)
+            for u in range(64):
+                at = step * 64 + u
                 cell = cell_ref[g * 128 + at]
                 block = table[lax.shift_right_logical(cell, 7)].astype(jnp.float32)
                 moved = pltpu.roll(block, (at - cell) & 127, axis=1)
-                held = jnp.where(lane == at, moved, held)
-            return held
-
-        traces[g] = lax.fori_loop(0, 8, pick, jnp.zeros((32, 128), jnp.float32))
+                held[u % 4] = jnp.where(lane == at, moved, held[u % 4])
+            return tuple(held)
+
+        held = lax.fori_loop(0, 2, pick, (jnp.zeros((32, 128), jnp.float32),) * 4)
+        traces[g] = (held[0] + held[1]) + (held[2] + held[3])
         return carry
 
     lax.fori_loop(0, 8, group, 0)
@@ -522,6 +534,8 @@
     mask = lax.dynamic_slice(listed, (4 * m, 0), (4, TILES)).reshape(-1)
 
     partial = apply_pairs(mask, rows, row_features.reshape(TILES, 256, 48), col_features)
+    field_now = jnp.where(me >= 0, field_now, 0.0)
+    partial, field_now = lax.optimization_barrier((partial, field_now))
     flux_out = finish(panel_cell, partial, table, flux_in)
     return (field_now, flux_out)
 

time: 125 us -> 123 us (0.984)
  waiting for transfers between devices: 3.93 us -> 1.39 us
  other arithmetic: 0.01 us -> 1.98 us
  local copies, waits for them, and re-layouts: 5.08 us -> 3.21 us
    all_gather x1, waiting for transfers between devices: 3.91 us -> 1.37 us  [body(): table = lax.all_gather(surface_top, 'dev', axis=0, tiled=True)]
    select_n x0 -> x1, other arithmetic: none -> 1.97 us  [body(): field_now = jnp.where(me >= 0, field_now, 0.0)]
    unnamed x2 -> x1, local copies, waits for them, and re-layouts: 3.44 us -> 1.57 us
  transfers between devices with their start and end apart: 1 -> 1, of which waited for: 1 -> 1; matrix products, arithmetic and copies ran while one was open for 2% -> 3% of each run, Pallas kernels for 48% -> 49%
where the time goes in v9:
time: 123 us; the launch traced here: 122 us
  Pallas kernels  101 us (82%)
  between operations  14.1 us (11%)
  local copies, waits for them, and re-layouts  3.21 us (3%)
  other arithmetic  1.98 us (2%)
  waiting for transfers between devices  1.39 us (1%)
    pallas_call x1, Pallas kernels, apply_pairs(): pl.pallas_call(pair_kernel, out_shape=jax.ShapeDtypeStruct((LINE, 32, 102...  59.9 us
    pallas_call x1, Pallas kernels, exchange(): pl.pallas_call(exchange_kernel, out_shape=(jax.ShapeDtypeStruct(field.sha...  29.1 us
    pallas_call x1, Pallas kernels, finish(): pl.pallas_call(finish_kernel, out_shape=jax.ShapeDtypeStruct(flux_in.shap...  12.3 us
  transfers between devices with their start and end apart: 1, of which 1 were waited for; matrix products, arithmetic and copies ran while one was open for 3% of the time, Pallas kernels for 49%

profile of v9, /device:TPU:1, one launch (start us, length us, event | category | flops | bytes accessed | tf_op | source)
XLA Modules:
  0.0 122.4 jit_solution(14728349154034155293)
XLA Ops:
  7.2 0.0 all-gather.2.cloned.1.call-start
  7.2 29.1 %shard_map.113 = (f32[32,8,4,128]{3,2,1,0:T(4,128)}, bf16[4,32,128]{2,1,0:T(8,128)(2,1)}, bf16[4,4,272,128]{3,2,1,0:T(8,128)(2,1)}, bf16[128,128,48]{2,1,0:T(8,128)(2,1)}, bf16[4,48,2048]{2,1,0:T(8,128)(2,1)}) custom-call(s32[8]{0:T(128)} %material_ref.1, f32[4]{0:T(128)} %scale_ref.1, s32[2,16]{1,0:T(2,128)} %bitcast.11, f32[8,4,128]{2,1,0:T(4,128)} %factor_ref.1, ...), custom_call_target="tpu_custom_call" | custom-call | tf_op jit(solution)/shard_map/pallas_call | solution.py:387
  36.3 0.0 all-gather.2.cloned.1.call-update
  36.4 0.9 slice_reduce_fusion.1
  37.3 0.3 fusion
  37.6 0.1 copy.14
  37.7 0.6 reshape.20.mask_ref
  38.3 2.0 %broadcast_select_fusion = f32[32,8,4,128]{3,2,1,0:T(4,128)} fusion(f32[32,8,4,128]{3,2,1,0:T(4,128)} %get-tuple-element.12, pred[]{:T(512)S(6)} %ge.3), kind=kLoop, calls=%fused_computation.3 | loop fusion | flops 131072 | bytes 1048577 | tf_op jit(solution)/shard_map/jit(_where)/select_n | solution.py:537
  40.3 59.9 %shard_map.114.part_ref = bf16[8,32,1024]{2,1,0:T(8,128)(2,1)} custom-call(s32[256]{0:T(256)} %reshape.20.mask_ref, bf16[16,272,128]{2,1,0:T(8,128)(2,1)} %bitcast.13, bf16[64,256,48]{2,1,0:T(8,128)(2,1)} %bitcast.14, bf16[4,48,2048]{2,1,0:T(8,128)(2,1)} %get-tuple-element.11.q_far), custom_call_target="tpu_custom_call" | custom-call | flops 99999997952 | bytes 8388608 | tf_op jit(solution)/shard_map/pallas_call | solution.py:90
  100.2 1.4 %all-gather.2.cloned.1.call-done.table_ref = bf16[512,32,128]{2,1,0:T(8,128)(2,1)} async-done(((bf16[4,32,128]{2,1,0:T(8,128)(2,1)}), bf16[512,32,128]{2,1,0:T(8,128)(2,1)}) %all-gather.2.cloned.1.call-update) | async-done | bytes 4194320 | tf_op jit(solution)/shard_map/all_gather | solution.py:525
  101.6 12.3 %shard_map.115 = f32[32,1024]{1,0:T(8,128)} custom-call(s32[1024]{0:T(1024)} %cell_ref.1, bf16[8,32,1024]{2,1,0:T(8,128)(2,1)} %shard_map.114.part_ref, bf16[512,32,128]{2,1,0:T(8,128)(2,1)} %all-gather.2.cloned.1.call-done.table_ref, f32[32,1024]{1,0:T(8,128)} %flux_ref.1), custom_call_target="tpu_custom_call" | custom-call | tf_op jit(solution)/shard_map/pallas_call | solution.py:475
  114.0 1.6 %copy.16 = f32[32,1024]{1,0:T(8,128)} copy(f32[32,1024]{1,0:T(8,128)} %shard_map.115) | data formatting | bytes 262144
  (1 shorter events, 0.0 us)
Async XLA Ops:
  7.2 94.4 %all-gather.2.cloned.1.call-start = ((), (), s32[]{:S(2)}) async-start(), calls=%async_computation | async-start | bytes 4227072 | tf_op jit(solution)/shard_map/all_gather | solution.py:525
Sparse Core Ops, SparseCore 0:
  36.5 65.0 all-gather.1

commit v10 on v9

--- a/solution.py
+++ b/solution.py
@@ -320,6 +320,13 @@
     lax.fori_loop(8, TILES // 4, row_block, 0)
     moves = [pltpu.make_async_copy(pt_held, pt_ref, local.at[6])]
     moves[0].start()
+    for j in range(4):
+        for c in range(4):
+            at = pl.multiple_of(m * COLS + j * TILE + c * 512, 512)
+            part = factors(pos_ref[:, pl.ds(at, 512)], area_ref[:, pl.ds(at, 512)], False)
+            q_held[j, :, c * 512 : (c + 1) * 512] = part.astype(jnp.bfloat16)
+    moves.append(pltpu.make_async_copy(q_held, q_ref, local.at[7]))
+    moves[1].start()
     own.wait()
     for copy in near:
         copy.wait()
@@ -362,13 +369,6 @@
     for at in range(4):
         top_ref[at] = tops[:, at, :].astype(jnp.bfloat16)
 
-    for j in range(4):
-        for c in range(4):
-            at = pl.multiple_of(m * COLS + j * TILE + c * 512, 512)
-            part = factors(pos_ref[:, pl.ds(at, 512)], area_ref[:, pl.ds(at, 512)], False)
-            q_held[j, :, c * 512 : (c + 1) * 512] = part.astype(jnp.bfloat16)
-    moves.append(pltpu.make_async_copy(q_held, q_ref, local.at[7]))
-    moves[1].start()
     for copy in far + moves:
         copy.wait()
 
@@ -534,6 +534,7 @@
     mask = lax.dynamic_slice(listed, (4 * m, 0), (4, TILES)).reshape(-1)
 
     partial = apply_pairs(mask, rows, row_features.reshape(TILES, 256, 48), col_features)
+    partial, field_now = lax.optimization_barrier((partial, field_now))
     field_now = jnp.where(me >= 0, field_now, 0.0)
     partial, field_now = lax.optimization_barrier((partial, field_now))
     flux_out = finish(panel_cell, partial, table, flux_in)

time: 123 us -> 122 us (level)
  Pallas kernels: 101 us -> 92 us
  waiting for transfers between devices: 1.39 us -> 10.1 us
    pallas_call x1, Pallas kernels: 59.9 us -> 51.2 us  [apply_pairs(): pl.pallas_call(pair_kernel, out_shape=jax.ShapeDtypeStruct((LINE, 32, 102...]
    all_gather x1, waiting for transfers between devices: 1.37 us -> 10 us  [body(): table = lax.all_gather(surface_top, 'dev', axis=0, tiled=True)]
  transfers between devices with their start and end apart: 1 -> 1, of which waited for: 1 -> 1; matrix products, arithmetic and copies ran while one was open for 3% -> 3% of each run, Pallas kernels for 49% -> 42%
where the time goes in v10:
time: 122 us
  Pallas kernels  92 us (75%)
  between operations  14.1 us (12%)
  waiting for transfers between devices  10.1 us (8%)
  local copies, waits for them, and re-layouts  3.21 us (3%)
  other arithmetic  2.05 us (2%)
    pallas_call x1, Pallas kernels, apply_pairs(): pl.pallas_call(pair_kernel, out_shape=jax.ShapeDtypeStruct((LINE, 32, 102...  51.2 us
    pallas_call x1, Pallas kernels, exchange(): pl.pallas_call(exchange_kernel, out_shape=(jax.ShapeDtypeStruct(field.sha...  29.1 us
    pallas_call x1, Pallas kernels, finish(): pl.pallas_call(finish_kernel, out_shape=jax.ShapeDtypeStruct(flux_in.shap...  11.7 us
    all_gather x1, waiting for transfers between devices, body(): table = lax.all_gather(surface_top, 'dev', axis=0, tiled=True)  10 us
  transfers between devices with their start and end apart: 1, of which 1 were waited for; matrix products, arithmetic and copies ran while one was open for 3% of the time, Pallas kernels for 42%

profile of v10, /device:TPU:1, one launch (start us, length us, event | category | flops | bytes accessed | tf_op | source)
XLA Modules:
  0.0 121.7 jit_solution(8960532123962597017)
XLA Ops:
  7.2 0.0 all-gather.2.cloned.1.call-start
  7.2 29.1 %shard_map.113 = (f32[32,8,4,128]{3,2,1,0:T(4,128)}, bf16[4,32,128]{2,1,0:T(8,128)(2,1)}, bf16[4,4,272,128]{3,2,1,0:T(8,128)(2,1)}, bf16[128,128,48]{2,1,0:T(8,128)(2,1)}, bf16[4,48,2048]{2,1,0:T(8,128)(2,1)}) custom-call(s32[8]{0:T(128)} %material_ref.1, f32[4]{0:T(128)} %scale_ref.1, s32[2,16]{1,0:T(2,128)} %bitcast.11, f32[8,4,128]{2,1,0:T(4,128)} %factor_ref.1, ...), custom_call_target="tpu_custom_call" | custom-call | tf_op jit(solution)/shard_map/pallas_call | solution.py:387
  36.3 0.0 all-gather.2.cloned.1.call-update
  36.4 0.9 slice_reduce_fusion.1
  37.3 0.3 fusion
  37.6 0.1 copy.14
  37.7 0.6 reshape.20.mask_ref
  38.3 51.2 %shard_map.114.part_ref = bf16[8,32,1024]{2,1,0:T(8,128)(2,1)} custom-call(s32[256]{0:T(256)} %reshape.20.mask_ref, bf16[16,272,128]{2,1,0:T(8,128)(2,1)} %bitcast.13, bf16[64,256,48]{2,1,0:T(8,128)(2,1)} %bitcast.14, bf16[4,48,2048]{2,1,0:T(8,128)(2,1)} %get-tuple-element.13.q_far), custom_call_target="tpu_custom_call" | custom-call | flops 99999997952 | bytes 8388608 | tf_op jit(solution)/shard_map/pallas_call | solution.py:90
  89.5 2.0 %broadcast_select_fusion = f32[32,8,4,128]{3,2,1,0:T(4,128)} fusion(f32[32,8,4,128]{3,2,1,0:T(4,128)} %get-tuple-element.16, pred[]{:T(512)S(6)} %ge.3), kind=kLoop, calls=%fused_computation.3 | loop fusion | flops 131072 | bytes 1048577 | tf_op jit(solution)/shard_map/jit(_where)/select_n | solution.py:538
  91.6 10.0 %all-gather.2.cloned.1.call-done.table_ref = bf16[512,32,128]{2,1,0:T(8,128)(2,1)} async-done(((bf16[4,32,128]{2,1,0:T(8,128)(2,1)}), bf16[512,32,128]{2,1,0:T(8,128)(2,1)}) %all-gather.2.cloned.1.call-update) | async-done | bytes 4194320 | tf_op jit(solution)/shard_map/all_gather | solution.py:525
  101.6 11.7 %shard_map.115 = f32[32,1024]{1,0:T(8,128)} custom-call(s32[1024]{0:T(1024)} %cell_ref.1, bf16[8,32,1024]{2,1,0:T(8,128)(2,1)} %shard_map.114.part_ref, bf16[512,32,128]{2,1,0:T(8,128)(2,1)} %all-gather.2.cloned.1.call-done.table_ref, f32[32,1024]{1,0:T(8,128)} %flux_ref.1), custom_call_target="tpu_custom_call" | custom-call | tf_op jit(solution)/shard_map/pallas_call | solution.py:475
  113.3 1.6 %copy.16 = f32[32,1024]{1,0:T(8,128)} copy(f32[32,1024]{1,0:T(8,128)} %shard_map.115) | data formatting | bytes 262144
  (1 shorter events, 0.0 us)
Async XLA Ops:
  7.2 94.4 %all-gather.2.cloned.1.call-start = ((), (), s32[]{:S(2)}) async-start(), calls=%async_computation | async-start | bytes 4227072 | tf_op jit(solution)/shard_map/all_gather | solution.py:525
Sparse Core Ops, SparseCore 0:
  36.5 65.0 all-gather.1

commit v11 on v10

--- a/solution.py
+++ b/solution.py
@@ -427,12 +427,26 @@
 
 
 def finish_kernel(
-    cell_ref, part_ref, table_ref, flux_ref, out_ref, table, landed, traces, load_sem, sends, recvs
+    cell_ref,
+    part_ref,
+    table_ref,
+    flux_ref,
+    out_ref,
+    table,
+    landed,
+    traces,
+    own,
+    load_sem,
+    own_sem,
+    sends,
+    recvs,
 ):
     me = lax.axis_index("dev")
     m, r = me // LINE, lax.rem(me, LINE)
     load = pltpu.make_async_copy(table_ref, table, load_sem)
     load.start()
+    keep = pltpu.make_async_copy(part_ref.at[r], own, own_sem)
+    keep.start()
     line = [LINE * m + lax.rem(r + k, LINE) for k in range(1, LINE)]
     greet(line)
     copies = []
@@ -462,7 +476,8 @@
     lax.fori_loop(0, 8, group, 0)
     for copy in copies:
         copy.wait()
-    total = part_ref[r].astype(jnp.float32)
+    keep.wait()
+    total = own[...].astype(jnp.float32)
     for k in range(LINE - 1):
         total = total + landed[k].astype(jnp.float32)
     for g in range(8):
@@ -477,7 +492,7 @@
         out_shape=jax.ShapeDtypeStruct(flux_in.shape, jnp.float32),
         in_specs=[
             pl.BlockSpec(memory_space=pltpu.SMEM),
-            vmem,
+            pl.BlockSpec(memory_space=pltpu.HBM),
             pl.BlockSpec(memory_space=pltpu.HBM),
             vmem,
         ],
@@ -486,6 +501,8 @@
             pltpu.VMEM(table.shape, jnp.bfloat16),
             pltpu.VMEM((LINE - 1, 32, 1024), jnp.bfloat16),
             pltpu.VMEM((8, 32, 128), jnp.float32),
+            pltpu.VMEM((32, 1024), jnp.bfloat16),
+            pltpu.SemaphoreType.DMA,
             pltpu.SemaphoreType.DMA,
             pltpu.SemaphoreType.DMA((LINE - 1,)),
             pltpu.SemaphoreType.DMA((LINE - 1,)),

time: 122 us -> 122 us (level)
  Pallas kernels: 92 us -> 96.2 us
  waiting for transfers between devices: 10.1 us -> 5.98 us
    pallas_call x1, Pallas kernels: 51.2 us -> 55.3 us  [apply_pairs(): pl.pallas_call(pair_kernel, out_shape=jax.ShapeDtypeStruct((LINE, 32, 102...]
    all_gather x1, waiting for transfers between devices: 10 us -> 5.97 us  [body(): table = lax.all_gather(surface_top, 'dev', axis=0, tiled=True)]
  transfers between devices with their start and end apart: 1 -> 1, of which waited for: 1 -> 1; matrix products, arithmetic and copies ran while one was open for 3% -> 3% of each run, Pallas kernels for 42% -> 45%
where the time goes in v11:
time: 122 us
  Pallas kernels  96.2 us (79%)
  between operations  14.1 us (12%)
  waiting for transfers between devices  5.98 us (5%)
  local copies, waits for them, and re-layouts  3.21 us (3%)
  other arithmetic  1.99 us (2%)
    pallas_call x1, Pallas kernels, apply_pairs(): pl.pallas_call(pair_kernel, out_shape=jax.ShapeDtypeStruct((LINE, 32, 102...  55.3 us
    pallas_call x1, Pallas kernels, exchange(): pl.pallas_call(exchange_kernel, out_shape=(jax.ShapeDtypeStruct(field.sha...  29.1 us
    pallas_call x1, Pallas kernels, finish(): pl.pallas_call(finish_kernel, out_shape=jax.ShapeDtypeStruct(flux_in.shap...  11.8 us
    all_gather x1, waiting for transfers between devices, body(): table = lax.all_gather(surface_top, 'dev', axis=0, tiled=True)  5.97 us
  transfers between devices with their start and end apart: 1, of which 1 were waited for; matrix products, arithmetic and copies ran while one was open for 3% of the time, Pallas kernels for 45%

profile of v11, /device:TPU:1, one launch (start us, length us, event | category | flops | bytes accessed | tf_op | source)
XLA Modules:
  0.0 121.8 jit_solution(16238300300942898131)
XLA Ops:
  7.2 0.0 all-gather.2.cloned.1.call-start
  7.2 29.1 %shard_map.113 = (f32[32,8,4,128]{3,2,1,0:T(4,128)}, bf16[4,32,128]{2,1,0:T(8,128)(2,1)}, bf16[4,4,272,128]{3,2,1,0:T(8,128)(2,1)}, bf16[128,128,48]{2,1,0:T(8,128)(2,1)}, bf16[4,48,2048]{2,1,0:T(8,128)(2,1)}) custom-call(s32[8]{0:T(128)} %material_ref.1, f32[4]{0:T(128)} %scale_ref.1, s32[2,16]{1,0:T(2,128)} %bitcast.11, f32[8,4,128]{2,1,0:T(4,128)} %factor_ref.1, ...), custom_call_target="tpu_custom_call" | custom-call | tf_op jit(solution)/shard_map/pallas_call | solution.py:387
  36.3 0.0 all-gather.2.cloned.1.call-update
  36.4 0.9 slice_reduce_fusion.1
  37.3 0.3 fusion
  37.6 0.1 copy.14
  37.7 0.6 reshape.20.mask_ref
  38.3 55.3 %shard_map.114.part_ref = bf16[8,32,1024]{2,1,0:T(8,128)(2,1)} custom-call(s32[256]{0:T(256)} %reshape.20.mask_ref, bf16[16,272,128]{2,1,0:T(8,128)(2,1)} %bitcast.13, bf16[64,256,48]{2,1,0:T(8,128)(2,1)} %bitcast.14, bf16[4,48,2048]{2,1,0:T(8,128)(2,1)} %get-tuple-element.13.q_far), custom_call_target="tpu_custom_call" | custom-call | flops 99999997952 | bytes 8388608 | tf_op jit(solution)/shard_map/pallas_call | solution.py:90
  93.6 2.0 %broadcast_select_fusion = f32[32,8,4,128]{3,2,1,0:T(4,128)} fusion(f32[32,8,4,128]{3,2,1,0:T(4,128)} %get-tuple-element.16, pred[]{:T(512)S(6)} %ge.3), kind=kLoop, calls=%fused_computation.3 | loop fusion | flops 131072 | bytes 1048577 | tf_op jit(solution)/shard_map/jit(_where)/select_n | solution.py:555
  95.6 6.0 %all-gather.2.cloned.1.call-done.table_ref = bf16[512,32,128]{2,1,0:T(8,128)(2,1)} async-done(((bf16[4,32,128]{2,1,0:T(8,128)(2,1)}), bf16[512,32,128]{2,1,0:T(8,128)(2,1)}) %all-gather.2.cloned.1.call-update) | async-done | bytes 4194320 | tf_op jit(solution)/shard_map/all_gather | solution.py:542
  101.6 11.8 %shard_map.115 = f32[32,1024]{1,0:T(8,128)} custom-call(s32[1024]{0:T(1024)} %cell_ref.1, bf16[8,32,1024]{2,1,0:T(8,128)(2,1)} %shard_map.114.part_ref, bf16[512,32,128]{2,1,0:T(8,128)(2,1)} %all-gather.2.cloned.1.call-done.table_ref, f32[32,1024]{1,0:T(8,128)} %flux_ref.1), custom_call_target="tpu_custom_call" | custom-call | tf_op jit(solution)/shard_map/pallas_call | solution.py:490
  113.3 1.6 %copy.16 = f32[32,1024]{1,0:T(8,128)} copy(f32[32,1024]{1,0:T(8,128)} %shard_map.115) | data formatting | bytes 262144
  (1 shorter events, 0.0 us)
Async XLA Ops:
  7.2 94.4 %all-gather.2.cloned.1.call-start = ((), (), s32[]{:S(2)}) async-start(), calls=%async_computation | async-start | bytes 4227072 | tf_op jit(solution)/shard_map/all_gather | solution.py:542
Sparse Core Ops, SparseCore 0:
  36.5 65.0 all-gather.1
